TPU v7x, 128 devices: a whole 4x4x4 slice. The times are simulated.
128 devices in a mesh: row: 8 (over y, core), col: 16 (over x, z).
Axes of the slice: x: 4, y: 4, z: 4, core: 2. Of those that a mesh axis runs over, the one named last changes fastest.
Arguments:
- tokens: bfloat16 [104, 320, 384], P('row', 'col')
- row_sizes: int32 [8], replicated, may hold values from 1 to 13, 88 in all
- col_sizes: int32 [16], replicated, may hold values from 1 to 20, 256 in all
- norm_gain: float32 [384], replicated, may hold values from 0.25 to 1.75
- query_weight: bfloat16 [384, 384], replicated
- key_weight: bfloat16 [384, 384], replicated
- value_weight: bfloat16 [384, 384], replicated, may hold values from -0.3125 to 0.3125
- out_weight: bfloat16 [384, 384], replicated, may hold values from -0.625 to 0.625
- cache_one: bfloat16 [2, 104, 320, 384], P(None, 'row', 'col'), may hold values from -6 to 6
- gain_one: float32 [384], replicated, may hold values from 0.25 to 1.75
- conv_one: bfloat16 [3, 3, 3, 384, 384], replicated, may hold values from -0.0625 to 0.0625
- cache_two: bfloat16 [2, 208, 640, 384], P(None, 'row', 'col'), may hold values from -6 to 6
- gain_two: float32 [384], replicated, may hold values from 0.25 to 1.75
- conv_two: bfloat16 [3, 3, 3, 384, 192], replicated, may hold values from -0.0625 to 0.0625
Outputs:
- decoded: bfloat16 [208, 640, 192], P('row', 'col')
Inputs may be any that keep to these rules, and one draw needn't show every extreme that they name: `row_sizes`: positive tile heights that sum to 88; the tallest has exactly 13 rows. `col_sizes`: positive tile widths that sum to 256; the widest has exactly 20 columns.
All inputs are finite; a program needn't handle non-finite values.
Results may differ from a plain program's by a relative error of at most 0.0095.
Values may be sent and summed in bfloat16 or wider, within the bound.
No kernel may reach another device: no remote copies, remote signals or barrier semaphores. Data moves between devices by JAX's collectives and lax.ppermute only.
A program may use at most 320 MiB of HBM per device.

v0:
```python
import math

import jax
import jax.numpy as jnp
from jax import lax
from jax.sharding import PartitionSpec as P

epsilon = 1e-06
masked_score = -1e30


def with_halo(block, sides, width):
    for axis, dim in sides:
        count = lax.axis_size(axis)
        forward = [(i, i + 1) for i in range(count - 1)]
        backward = [(target, source) for source, target in forward]
        low = lax.ppermute(
            lax.slice_in_dim(block, block.shape[dim] - width, None, axis=dim), axis, forward
        )
        high = lax.ppermute(lax.slice_in_dim(block, 0, width, axis=dim), axis, backward)
        block = jnp.concatenate([low, block, high], axis=dim)
    return block


def select_size(size_table, position):
    marks = jnp.arange(size_table.shape[0], dtype=jnp.int32) == position
    return jnp.sum(jnp.where(marks, size_table, 0))


def lookup(size_table, positions):
    marks = positions[:, None] == jnp.arange(size_table.shape[0], dtype=jnp.int32)[None, :]
    return jnp.sum(jnp.where(marks, size_table[None, :], 0), axis=1)


def rms_scale(values_in, gain_vec):
    wide = values_in.astype(jnp.float32)
    return wide * lax.rsqrt(jnp.mean(wide * wide, axis=-1, keepdims=True) + epsilon) * gain_vec


def edge_rows(frames, row_count, col_count):
    height = frames.shape[1]
    breadth = frames.shape[2]
    last_row = lax.dynamic_slice_in_dim(frames, row_count - 1, 1, 1)
    frames = lax.dynamic_update_slice_in_dim(frames, last_row, height - 1, 1)
    last_col = lax.dynamic_slice_in_dim(frames, col_count - 1, 1, 2)
    return lax.dynamic_update_slice_in_dim(frames, last_col, breadth - 1, 2)


def settle(padded, row_count, col_count):
    bottom = padded[:, -1:]
    padded = lax.dynamic_update_slice_in_dim(padded, bottom, row_count + 1, 1)
    right_col = padded[:, :, -1:]
    return lax.dynamic_update_slice_in_dim(padded, right_col, col_count + 1, 2)


def convolve(extended, kernel):
    channels = extended.shape[3]
    height = extended.shape[1] - 2
    breadth = extended.shape[2] - 2
    columns = [
        extended[t_step, a_step : a_step + height, b_step : b_step + breadth]
        for t_step in range(3)
        for a_step in range(3)
        for b_step in range(3)
    ]
    stacked = jnp.concatenate(columns, axis=-1).reshape(height * breadth, 27 * channels)
    product = jnp.dot(
        stacked, kernel.reshape(27 * channels, kernel.shape[-1]), preferred_element_type=jnp.float32
    )
    return product.reshape(height, breadth, kernel.shape[-1])


def upsample(frames):
    return jnp.repeat(jnp.repeat(frames, 2, axis=1), 2, axis=2)


def local(
    tokens,
    row_sizes,
    col_sizes,
    norm_gain,
    query_weight,
    key_weight,
    value_weight,
    out_weight,
    cache_one,
    gain_one,
    conv_one,
    cache_two,
    gain_two,
    conv_two,
):
    tile_rows, tile_cols, channels = tokens.shape
    col_devices = lax.axis_size("col")
    row_count = select_size(row_sizes, lax.axis_index("row"))
    col_count = select_size(col_sizes, lax.axis_index("col"))
    per_device = tile_rows * tile_cols
    scale = 1.0 / math.sqrt(channels)
    flat_normed = rms_scale(tokens, norm_gain).astype(jnp.bfloat16).reshape(per_device, channels)
    queries = jnp.dot(flat_normed, query_weight, preferred_element_type=jnp.float32).astype(
        jnp.bfloat16
    )
    own_keys = jnp.dot(flat_normed, key_weight, preferred_element_type=jnp.float32).astype(
        jnp.bfloat16
    )
    own_values = jnp.dot(flat_normed, value_weight, preferred_element_type=jnp.float32).astype(
        jnp.bfloat16
    )
    key_rows = lax.all_gather(own_keys, ("row", "col"), axis=0, tiled=True)
    running_max = jnp.full((per_device,), masked_score, jnp.float32)
    slot_index = jnp.arange(key_rows.shape[0], dtype=jnp.int32)
    device = slot_index // per_device
    local_slot = slot_index - device * per_device
    tile_row = device // col_devices
    tile_col = device - tile_row * col_devices
    local_row = local_slot // tile_cols
    local_col = local_slot - local_row * tile_cols
    usable = (local_row < lookup(row_sizes, tile_row)) & (local_col < lookup(col_sizes, tile_col))
    scores = jnp.einsum("qc,kc->qk", queries, key_rows, preferred_element_type=jnp.float32) * scale
    scores = jnp.where(usable[None, :], scores, masked_score)
    new_max = jnp.maximum(running_max, jnp.max(scores, axis=1))
    expos = jnp.exp(scores - new_max[:, None]) * usable[None, :].astype(jnp.float32)
    denominator = jnp.sum(expos, axis=1)
    accumulated = jnp.dot(
        expos.astype(jnp.bfloat16),
        lax.all_gather(own_values, ("row", "col"), axis=0, tiled=True),
        preferred_element_type=jnp.float32,
    )
    attention = (accumulated / denominator[:, None]).astype(jnp.bfloat16)
    projected = jnp.dot(attention, out_weight, preferred_element_type=jnp.float32).reshape(
        tile_rows, tile_cols, channels
    )
    mixed = (tokens.astype(jnp.float32) + projected).astype(jnp.bfloat16)
    act_one = jax.nn.silu(rms_scale(mixed, gain_one)).astype(jnp.bfloat16)
    frames_one = jnp.concatenate([cache_one, act_one[None]], axis=0)
    prepared = edge_rows(frames_one, row_count, col_count)
    padded = with_halo(prepared, (("row", 1), ("col", 2)), 1)
    extended = settle(padded, row_count, col_count)
    y_one = convolve(extended, conv_one).astype(jnp.bfloat16)
    act_small = jax.nn.silu(rms_scale(y_one, gain_two)).astype(jnp.bfloat16)[None]
    fine_rows = 2 * row_count
    fine_cols = 2 * col_count
    frames_two = jnp.concatenate([cache_two, upsample(act_small)], axis=0)
    prepared_two = edge_rows(frames_two, fine_rows, fine_cols)
    padded_two = with_halo(prepared_two, (("row", 1), ("col", 2)), 1)
    extended_two = settle(padded_two, fine_rows, fine_cols)
    y_two = convolve(extended_two, conv_two)
    row_usable = jnp.arange(2 * tile_rows, dtype=jnp.int32) < fine_rows
    col_usable = jnp.arange(2 * tile_cols, dtype=jnp.int32) < fine_cols
    usable = (row_usable[:, None] & col_usable[None, :])[:, :, None]
    return jnp.where(usable, y_two, 0.0).astype(jnp.bfloat16)


def solution(mesh):
    placed = (
        P("row", "col", None),
        P(),
        P(),
        P(),
        P(),
        P(),
        P(),
        P(),
        P(None, "row", "col", None),
        P(),
        P(),
        P(None, "row", "col", None),
        P(),
        P(),
    )
    return jax.shard_map(
        local, mesh=mesh, in_specs=placed, out_specs=P("row", "col", None), check_vma=False
    )
```

profile of v0, /device:TPU:1, one launch (start us, length us, event | category | flops | bytes accessed | tf_op | source)
XLA Modules:
  0.0 388.0 jit_solution(13467160023956242634)
XLA Ops:
  8.8 1.9 fusion.15
  10.8 1.9 fusion.16
  21.8 87.1 %all-gather.5.cloned.1.call-done = bf16[128,260,384]{2,1,0:T(8,128)(2,1)} async-done(((bf16[1,260,384]{2,1,0:T(8,128)(2,1)}), bf16[128,260,384]{2,1,0:T(8,128)(2,1)}) %all-gather.5.cloned.1.call-update) | async-done | bytes 25559056 | tf_op jit(solution)/shard_map/all_gather | solution.py:109
  108.9 31.3 %reshape.388 = bf16[33280,384]{1,0:T(8,128)(2,1)} reshape(bf16[128,260,384]{2,1,0:T(8,128)(2,1)} %all-gather.5.cloned.1.call-done) | data formatting | bytes 51118080
  140.2 25.4 %fusion.99 = (f32[260]{0:T(512)S(1)}, f32[260,33280]{1,0:T(8,128)}) fusion(bf16[33280,384]{1,0:T(8,128)(2,1)} %reshape.388, bf16[260,384]{1,0:T(8,128)(2,1)S(1)} %reshape.383, bf16[384,384]{1,0:T(8,128)(2,1)S(1)} %copy-done, pred[33280]{0:T(1024)(128)(4,1)S(1)} %get-tuple-element.6), kind=kOutput, calls=%fused_computation.208 | convolution fusion | flops 6748085248 | bytes 60699152 | tf_op jit(solution)/shard_map/qc,kc->qk/dot_general | solution.py:119
  165.6 17.3 %fusion.1 = f32[260]{0:T(512)S(1)} fusion(f32[260,33280]{1,0:T(8,128)} %get-tuple-element.16, f32[33280]{0:T(1024)S(1)} %get-tuple-element.5, f32[260]{0:T(512)S(1)} %broadcast_maximum_fusion), kind=kLoop, calls=%fused_computation.3 | loop fusion | flops 25958140 | bytes 34746400 | tf_op jit(solution)/shard_map/reduce_sum | solution.py:123
  182.9 22.8 %all-gather.7.cloned.1.call-done = bf16[128,260,384]{2,1,0:T(8,128)(2,1)} async-done(((bf16[1,260,384]{2,1,0:T(8,128)(2,1)}), bf16[128,260,384]{2,1,0:T(8,128)(2,1)}) %all-gather.7.cloned.1.call-update) | async-done | bytes 25559056 | tf_op jit(solution)/shard_map/all_gather | solution.py:126
  205.6 31.2 %reshape.390 = bf16[33280,384]{1,0:T(8,128)(2,1)} reshape(bf16[128,260,384]{2,1,0:T(8,128)(2,1)} %all-gather.7.cloned.1.call-done) | data formatting | bytes 51118080
  236.9 22.0 %fusion.12 = bf16[260,384]{1,0:T(8,128)(2,1)S(1)} fusion(bf16[33280,384]{1,0:T(8,128)(2,1)} %reshape.390, f32[260,33280]{1,0:T(8,128)} %get-tuple-element.16, f32[33280]{0:T(1024)S(1)} %get-tuple-element.5, f32[260]{0:T(512)S(1)} %broadcast_maximum_fusion, f32[260]{0:T(512)S(1)} %fusion.1), kind=kOutput, calls=%fused_computation.19 | convolution fusion | flops 6671508480 | bytes 60505120 | tf_op jit(solution)/shard_map/dot_general | solution.py:124
  261.5 3.3 collective-permute-start
  264.7 1.9 collective-permute-start.1
  270.3 2.6 collective-permute-start.2
  279.9 1.8 dynamic_update_slice.27
  283.5 6.2 %multiply_reduce_fusion = (f32[13,20]{1,0:T(8,128)S(1)}, f32[13,20,384]{2,1,0:T(8,128)S(1)}) fusion(bf16[13,20,10368]{2,1,0:T(8,128)(2,1)S(1)} %fusion.57, bf16[10368,384,1]{1,0,2:T(8,128)(2,1)} %bitcast.243), kind=kOutput, calls=%fused_computation.100 | convolution fusion | flops 2070681344 | bytes 13754384 | tf_op jit(solution)/shard_map/dot_general | solution.py:67
  293.1 3.4 dynamic_update_slice.29
  296.5 4.4 %collective-permute-start.4 = (bf16[3,1,40,384]{3,2,1,0:T(8,128)(2,1)S(1)}, bf16[3,1,40,384]{3,2,1,0:T(8,128)(2,1)S(1)}, u32[]{:S(2)}, u32[]{:S(2)}) collective-permute-start(bf16[3,1,40,384]{3,2,1,0:T(8,128)(2,1)S(1)} %get-tuple-element.9), channel_id=1, source_target_pairs={{0,16},{16,32},{32,48},{48,64},{64,80},{80,96},{96,112},{1,17},{17... | collective-permute-start | bytes 276488 | tf_op jit(solution)/shard_map/ppermute | solution.py:17
  301.0 1.9 collective-permute-start.5
  302.9 3.9 %collective-permute-done.5 = bf16[3,1,40,384]{3,2,1,0:T(8,128)(2,1)S(1)} collective-permute-done((bf16[3,1,40,384]{3,2,1,0:T(8,128)(2,1)S(1)}, bf16[3,1,40,384]{3,2,1,0:T(8,128)(2,1)S(1)}, u32[]{:S(2)}, u32[]{:S(2)}) %collective-permute-start.5) | collective-permute-done | bytes 92192 | tf_op jit(solution)/shard_map/ppermute | solution.py:20
  307.0 3.2 collective-permute-start.6
  311.6 7.9 %copy.21 = bf16[3,3,3,384,192]{3,2,1,0,4:T(4,128)(2,1)} copy(bf16[3,3,3,384,192]{3,4,2,1,0:T(8,128)(2,1)} %param.27) | data formatting | bytes 7962624 | tf_op args[13]
  319.5 10.1 %reshape.392 = bf16[10368,192,1]{0,1,2:T(8,128)(2,1)} reshape(bf16[3,3,3,384,192]{3,2,1,0,4:T(4,128)(2,1)} %copy.21) | data formatting | bytes 7962624 | tf_op jit(solution)/shard_map/reshape | solution.py:68
  330.2 4.4 %pad_maximum_fusion = bf16[3,28,42,384]{3,2,1,0:T(8,128)(2,1)S(1)} fusion(bf16[3,28,1,384]{3,2,1,0:T(2,128)(2,1)} %collective-permute-done.7, bf16[3,1,40,384]{3,2,1,0:T(8,128)(2,1)S(1)} %collective-permute-done.5, bf16[3,26,40,384]{3,2,1,0:T(8,128)(2,1)} %copy-done.2, bf16[3,1,40,384]{3,2,1,0:T(8,128)(2,1)S(1)} %collective-permute-done.4, ...), kind=kLoop, calls=%fused_computation.8 | loop fusion | flops 13547520 | bytes 5419008 | tf_op jit(solution)/shard_map/concatenate | solution.py:21
  334.9 3.6 dynamic_update_slice.31
  370.0 11.2 %fusion.7 = bf16[26,40,192]{2,1,0:T(8,128)(2,1)} fusion(bf16[26,40,10368]{2,1,0:T(8,128)(2,1)} %fusion.17, bf16[10368,192,1]{0,1,2:T(8,128)(2,1)S(1)} %copy-done.4, pred[26,40]{1,0:T(8,128)(4,1)S(1)} %broadcast_and_fusion), kind=kOutput, calls=%fused_computation.12 | convolution fusion | flops 4140963840 | bytes 25947152 | tf_op jit(solution)/shard_map/dot_general | solution.py:67
  (133 shorter events, 56.9 us)
Async XLA Ops:
  6.5 133.6 %copy-start = (bf16[384,384]{1,0:T(8,128)(2,1)S(1)}, bf16[384,384]{1,0:T(8,128)(2,1)}, u32[]{:S(2)}) copy-start(bf16[384,384]{1,0:T(8,128)(2,1)} %param.18) | copy-start | bytes 884740
  6.5 102.3 %all-gather.5.cloned.1.call-start = ((), (), s32[]{:S(2)}) async-start(), calls=%async_computation | async-start | bytes 26155008 | tf_op jit(solution)/shard_map/all_gather | solution.py:109
  10.8 194.9 %all-gather.7.cloned.1.call-start = ((), (), s32[]{:S(2)}) async-start(), calls=%async_computation.1 | async-start | bytes 26155008 | tf_op jit(solution)/shard_map/all_gather | solution.py:126
  236.9 22.0 %copy-start.6 = (bf16[384,384]{1,0:T(8,128)(2,1)S(1)}, bf16[384,384]{1,0:T(8,128)(2,1)}, u32[]{:S(2)}) copy-start(bf16[384,384]{1,0:T(8,128)(2,1)} %param.21) | copy-start | bytes 884740
  236.9 22.4 %copy-start.5 = (bf16[13,20,384]{2,1,0:T(8,128)(2,1)S(1)}, bf16[13,20,384]{2,1,0:T(8,128)(2,1)}, u32[]{:S(2)}) copy-start(bf16[13,20,384]{2,1,0:T(8,128)(2,1)} %param.14) | copy-start | bytes 599044
  236.9 22.5 %copy-start.8 = (f32[384]{0:T(512)S(1)}, f32[384]{0:T(512)}, u32[]{:S(2)}) copy-start(f32[384]{0:T(512)} %param.23) | copy-start | bytes 4612
  261.4 16.1 %copy-start.3 = (bf16[3,13,20,384]{3,2,1,0:T(8,128)(2,1)}, bf16[3,13,20,384]{3,2,1,0:T(8,128)(2,1)S(1)}, u32[]{:S(2)}) copy-start(bf16[3,13,20,384]{3,2,1,0:T(8,128)(2,1)S(1)} %dynamic_update_slice.25) | copy-start | bytes 1797124
  261.5 7.5 %collective-permute-start = (bf16[3,1,20,384]{3,2,1,0:T(8,128)(2,1)S(1)}, bf16[3,1,20,384]{3,2,1,0:T(8,128)(2,1)S(1)}, u32[]{:S(2)}, u32[]{:S(2)}) collective-permute-start(bf16[3,1,20,384]{3,2,1,0:T(8,128)(2,1)S(1)} %get-tuple-element.13), channel_id=1, source_target_pairs={{0,16},{16,32},{32,48},{48,64},{64,80},{80,96},{96,112},{1,17},{17... | collective-permute-start | bytes 138248 | tf_op jit(solution)/shard_map/ppermute | solution.py:17
  264.7 5.5 %collective-permute-start.1 = (bf16[3,1,20,384]{3,2,1,0:T(8,128)(2,1)S(1)}, bf16[3,1,20,384]{3,2,1,0:T(8,128)(2,1)S(1)}, u32[]{:S(2)}, u32[]{:S(2)}) collective-permute-start(bf16[3,1,20,384]{3,2,1,0:T(8,128)(2,1)S(1)} %get-tuple-element.14), channel_id=1, source_target_pairs={{16,0},{32,16},{48,32},{64,48},{80,64},{96,80},{112,96},{17,1},{33... | collective-permute-start | bytes 138248 | tf_op jit(solution)/shard_map/ppermute | solution.py:20
  270.3 7.2 %collective-permute-start.2 = (bf16[3,15,1,384]{3,2,1,0:T(2,128)(2,1)S(1)}, bf16[3,15,1,384]{3,2,1,0:T(2,128)(2,1)S(1)}, u32[]{:S(2)}, u32[]{:S(2)}) collective-permute-start(bf16[3,15,1,384]{3,2,1,0:T(2,128)(2,1)S(1)} %get-tuple-element.11), channel_id=1, source_target_pairs={{0,1},{1,2},{2,3},{3,4},{4,5},{5,6},{6,7},{7,8},{8,9},{9,10},{10,1... | collective-permute-start | bytes 103688 | tf_op jit(solution)/shard_map/ppermute | solution.py:17
  272.9 5.2 %collective-permute-start.3 = (bf16[3,15,1,384]{3,2,1,0:T(2,128)(2,1)S(1)}, bf16[3,15,1,384]{3,2,1,0:T(2,128)(2,1)}, u32[]{:S(2)}, u32[]{:S(2)}) collective-permute-start(bf16[3,15,1,384]{3,2,1,0:T(2,128)(2,1)S(1)} %get-tuple-element.12), channel_id=1, source_target_pairs={{1,0},{2,1},{3,2},{4,3},{5,4},{6,5},{7,6},{8,7},{9,8},{10,9},{11,1... | collective-permute-start | bytes 103688 | tf_op jit(solution)/shard_map/ppermute | solution.py:20
  283.5 6.2 %copy-start.9 = (f32[384]{0:T(512)S(1)}, f32[384]{0:T(512)}, u32[]{:S(2)}) copy-start(f32[384]{0:T(512)} %param.26) | copy-start | bytes 4612
  296.5 33.1 %copy-start.2 = (bf16[3,26,40,384]{3,2,1,0:T(8,128)(2,1)}, bf16[3,26,40,384]{3,2,1,0:T(8,128)(2,1)S(1)}, u32[]{:S(2)}) copy-start(bf16[3,26,40,384]{3,2,1,0:T(8,128)(2,1)S(1)} %dynamic_update_slice.29) | copy-start | bytes 7188484
  296.5 6.4 %collective-permute-start.4 = (bf16[3,1,40,384]{3,2,1,0:T(8,128)(2,1)S(1)}, bf16[3,1,40,384]{3,2,1,0:T(8,128)(2,1)S(1)}, u32[]{:S(2)}, u32[]{:S(2)}) collective-permute-start(bf16[3,1,40,384]{3,2,1,0:T(8,128)(2,1)S(1)} %get-tuple-element.9), channel_id=1, source_target_pairs={{0,16},{16,32},{32,48},{48,64},{64,80},{80,96},{96,112},{1,17},{17... | collective-permute-start | bytes 276488 | tf_op jit(solution)/shard_map/ppermute | solution.py:17
  301.0 5.9 %collective-permute-start.5 = (bf16[3,1,40,384]{3,2,1,0:T(8,128)(2,1)S(1)}, bf16[3,1,40,384]{3,2,1,0:T(8,128)(2,1)S(1)}, u32[]{:S(2)}, u32[]{:S(2)}) collective-permute-start(bf16[3,1,40,384]{3,2,1,0:T(8,128)(2,1)S(1)} %get-tuple-element.10), channel_id=1, source_target_pairs={{16,0},{32,16},{48,32},{64,48},{80,64},{96,80},{112,96},{17,1},{33... | collective-permute-start | bytes 276488 | tf_op jit(solution)/shard_map/ppermute | solution.py:20
  307.0 22.6 %collective-permute-start.6 = (bf16[3,28,1,384]{3,2,1,0:T(2,128)(2,1)S(1)}, bf16[3,28,1,384]{3,2,1,0:T(2,128)(2,1)S(1)}, u32[]{:S(2)}, u32[]{:S(2)}) collective-permute-start(bf16[3,28,1,384]{3,2,1,0:T(2,128)(2,1)S(1)} %get-tuple-element.7), channel_id=1, source_target_pairs={{0,1},{1,2},{2,3},{3,4},{4,5},{5,6},{6,7},{7,8},{8,9},{9,10},{10,1... | collective-permute-start | bytes 193544 | tf_op jit(solution)/shard_map/ppermute | solution.py:17
  310.2 20.0 %collective-permute-start.7 = (bf16[3,28,1,384]{3,2,1,0:T(2,128)(2,1)S(1)}, bf16[3,28,1,384]{3,2,1,0:T(2,128)(2,1)}, u32[]{:S(2)}, u32[]{:S(2)}) collective-permute-start(bf16[3,28,1,384]{3,2,1,0:T(2,128)(2,1)S(1)} %get-tuple-element.8), channel_id=1, source_target_pairs={{1,0},{2,1},{3,2},{4,3},{5,4},{6,5},{7,6},{8,7},{9,8},{10,9},{11,1... | collective-permute-start | bytes 193544 | tf_op jit(solution)/shard_map/ppermute | solution.py:20
  329.6 0.7 copy-start.7
  360.4 9.6 %copy-start.4 = (bf16[10368,192,1]{0,1,2:T(8,128)(2,1)S(1)}, bf16[10368,192,1]{0,1,2:T(8,128)(2,1)}, u32[]{:S(2)}) copy-start(bf16[10368,192,1]{0,1,2:T(8,128)(2,1)} %reshape.392) | copy-start | bytes 11943940
  370.0 11.2 %copy-start.1 = (bf16[384,384]{1,0:T(8,128)(2,1)S(1)}, bf16[384,384]{1,0:T(8,128)(2,1)}, u32[]{:S(2)}) copy-start(bf16[384,384]{1,0:T(8,128)(2,1)} %param.18) | copy-start | bytes 884740
Sparse Core Ops, SparseCore 0:
  10.9 97.9 all-gather.4
  111.9 93.7 all-gather.6
where the time goes:
time: 394 us; the launch traced here: 388 us
  local copies, waits for them, and re-layouts  131 us (33%)
  waiting for transfers between devices  116 us (29%)
  matrix products  68.9 us (17%)
  other arithmetic  32.1 us (8%)
  between operations  20.4 us (5%)
  starting transfers between devices  20.1 us (5%)
    unnamed x77, local copies, waits for them, and re-layouts  106 us
    all_gather x1, waiting for transfers between devices, local(): key_rows = lax.all_gather(own_keys, ('row', 'col'), axis=0, tiled=True)  87.1 us
    dot_general x1, matrix products, local(): jnp.einsum('qc,kc->qk', queries, key_rows, preferred_element_type=jnp.flo...  25.4 us
    all_gather x1, waiting for transfers between devices, local(): lax.all_gather(own_values, ('row', 'col'), axis=0, tiled=True)  22.8 us
    dot_general x1, matrix products, local(): jnp.dot(expos.astype(jnp.bfloat16), lax.all_gather(own_values, ('row', 'c...  22 us
    dot_general x2, matrix products, convolve(): jnp.dot(stacked, kernel.reshape(27 * channels, kernel.shape[-1]), preferr...  17.3 us
    reduce_sum x1, other arithmetic, local(): denominator = jnp.sum(expos, axis=1)  17.3 us
    ppermute x4, starting transfers between devices, with_halo(): lax.ppermute(lax.slice_in_dim(block, block.shape[dim] - width, None, axis...  13.4 us
  transfers between devices with their start and end apart: 10, of which 5 were waited for; matrix products, arithmetic and copies ran while one was open for 26% of the time, Pallas kernels for 0%

commit v1 on v0

v1 whole, which is shorter than its diff:
```python
import math

import jax
import jax.numpy as jnp
from jax import lax
from jax.experimental import pallas as pl
from jax.experimental.pallas import tpu as pltpu
from jax.sharding import Mesh
from jax.sharding import PartitionSpec as P

epsilon = 1e-06
masked_score = -1e30
ROWS = ("y", "core")
COLS = ("x", "z")
HALO = 2
KEY_TILE = 272
KEY_CHUNK = 512
MAX_CHUNKS = 14
KEY_ROWS = MAX_CHUNKS * KEY_CHUNK + KEY_CHUNK
QUERY_BLOCK = 352
BLOCK_ROWS = 384
VMEM_BYTES = 60 * 1024 * 1024


def rms_scale(values_in, gain_vec):
    wide = values_in.astype(jnp.float32)
    return wide * lax.rsqrt(jnp.mean(wide * wide, axis=-1, keepdims=True) + epsilon) * gain_vec


def silu(v):
    return v / (1.0 + jnp.exp(-v))


def hop(value, axes, count, step):
    pairs = [(i, i + step) for i in range(count) if 0 <= i + step < count]
    return lax.ppermute(value, axes, pairs)


def pick(values, index, axis):
    return lax.dynamic_index_in_dim(values, jnp.maximum(index, 0), axis, keepdims=False)


def place(values, part, index, axis):
    return lax.dynamic_update_slice_in_dim(values, part, index, axis)


def put_rows(ref, start, value):
    for g in range(ref.shape[0]):
        ref[g, pl.ds(start, value.shape[0]), :] = value[:, g * 128 : (g + 1) * 128]


def get_rows(ref, start, count):
    return jnp.concatenate([ref[g, pl.ds(start, count), :] for g in range(ref.shape[0])], axis=1)


def query_kernel(starts_ref, strip_ref, gain_ref, qw_ref, kw_ref, query_ref, frame_ref, wide_ref, *, half, lat_rows, scale):
    front = HALO * half
    wide_ref[...] = jnp.zeros_like(wide_ref)
    tiles, tall, _ = strip_ref.shape
    for t in range(tiles):
        put_rows(wide_ref, front + starts_ref[t] * half, strip_ref[t].astype(jnp.float32))
    count = lat_rows * half
    frame_ref[...] = get_rows(wide_ref, starts_ref[tiles] * half, BLOCK_ROWS).astype(jnp.bfloat16)
    for i in range(count // QUERY_BLOCK):
        raw = get_rows(wide_ref, front + i * QUERY_BLOCK, QUERY_BLOCK)
        normed = rms_scale(raw, gain_ref[...]).astype(jnp.bfloat16)
        query = jnp.dot(normed, qw_ref[...], preferred_element_type=jnp.float32).astype(jnp.bfloat16)
        turned = lax.dot_general(query, kw_ref[...], (((1,), (1,)), ((), ())), preferred_element_type=jnp.float32)
        query_ref[i * QUERY_BLOCK : (i + 1) * QUERY_BLOCK, :] = (turned * scale).astype(jnp.bfloat16)


def attention_kernel(
    offsets_ref, chunks_ref, starts_ref, query_ref, tile_ref, bias_ref, out_ref,
    key_ref, score_ref, top_ref, sum_ref, acc_ref, wide_ref, stat_ref, *, half
):
    tiles = tile_ref.shape[0]

    def gather(t, carry):
        offset = pl.multiple_of(offsets_ref[t], 16)
        key_ref[pl.ds(offset, KEY_TILE), :] = tile_ref[t]
        return carry

    lax.fori_loop(0, tiles, gather, 0)
    tail = pl.multiple_of(offsets_ref[tiles], 16)
    key_ref[pl.ds(tail, KEY_CHUNK), :] = jnp.zeros((KEY_CHUNK, key_ref.shape[1]), jnp.bfloat16)
    front = HALO * half
    total = wide_ref.shape[1]
    count = query_ref.shape[0]
    wide_ref[:, 0:front, :] = jnp.zeros((3, front, 128), jnp.float32)
    wide_ref[:, front + count : total, :] = jnp.zeros((3, total - front - count, 128), jnp.float32)
    stat_ref[0:front, :] = jnp.zeros((front, 128), jnp.float32)
    stat_ref[front + count : total, :] = jnp.zeros((total - front - count, 128), jnp.float32)
    chunk_count = chunks_ref[0]
    blocks = count // QUERY_BLOCK
    lane_groups = KEY_CHUNK // 128

    def keys_at(j):
        return key_ref[pl.ds(pl.multiple_of(j * KEY_CHUNK, KEY_CHUNK), KEY_CHUNK), :]

    def score_step(i, j):
        slot = i % 2
        query = query_ref[i * QUERY_BLOCK : (i + 1) * QUERY_BLOCK, :]
        s = lax.dot_general(query, keys_at(j), (((1,), (1,)), ((), ())), preferred_element_type=jnp.float32)
        s = s + bias_ref[j]
        score_ref[slot, j] = s
        best = s[:, 0:128]
        for g in range(1, lane_groups):
            best = jnp.maximum(best, s[:, g * 128 : (g + 1) * 128])
        top_ref[slot] = jnp.maximum(top_ref[slot], best)

    def value_step(i, j):
        slot = i % 2
        p = jnp.exp2(score_ref[slot, j] - jnp.max(top_ref[slot], axis=1, keepdims=True))
        part = p[:, 0:128]
        for g in range(1, lane_groups):
            part = part + p[:, g * 128 : (g + 1) * 128]
        sum_ref[...] = sum_ref[...] + part
        acc_ref[...] = acc_ref[...] + jnp.dot(p.astype(jnp.bfloat16), keys_at(j), preferred_element_type=jnp.float32)

    for i in range(blocks + 1):
        if i < blocks:
            top_ref[i % 2] = jnp.full((QUERY_BLOCK, 128), masked_score, jnp.float32)
        if i > 0:
            last = (i - 1) % 2
            best = jnp.max(top_ref[last], axis=1, keepdims=True)
            top_ref[last] = jnp.broadcast_to(best, (QUERY_BLOCK, 128))
            sum_ref[...] = jnp.zeros_like(sum_ref)
            acc_ref[...] = jnp.zeros_like(acc_ref)

        def step(j, carry):
            if i < blocks:
                score_step(i, j)
            if i > 0:
                value_step(i - 1, j)
            return carry

        lax.fori_loop(0, chunk_count, step, 0)
        if i > 0:
            denominator = jnp.sum(sum_ref[...], axis=1, keepdims=True)
            lo = front + (i - 1) * QUERY_BLOCK
            put_rows(wide_ref, lo, acc_ref[...] / denominator)
            level = top_ref[(i - 1) % 2] + jnp.log2(jnp.broadcast_to(denominator, (QUERY_BLOCK, 128)))
            high = level.astype(jnp.bfloat16).astype(jnp.float32)
            mid = (level - high).astype(jnp.bfloat16).astype(jnp.float32)
            low = level - high - mid
            lane = lax.broadcasted_iota(jnp.int32, (QUERY_BLOCK, 128), 1)
            packed = jnp.where(lane == 0, high, jnp.where(lane == 1, mid, jnp.where(lane == 2, low, 0.0)))
            stat_ref[lo : lo + QUERY_BLOCK, :] = packed
    select = (
        lax.broadcasted_iota(jnp.int32, (16, 128), 0) == lax.broadcasted_iota(jnp.int32, (16, 128), 1)
    ).astype(jnp.bfloat16)
    for b in range(out_ref.shape[0]):
        offset = starts_ref[b] * half
        out_ref[b, 0 : BLOCK_ROWS - 16, :] = get_rows(wide_ref, offset, BLOCK_ROWS - 16).astype(jnp.bfloat16)
        levels = stat_ref[pl.ds(offset, BLOCK_ROWS), :].astype(jnp.bfloat16)
        out_ref[b, BLOCK_ROWS - 16 : BLOCK_ROWS, :] = lax.dot_general(
            select, levels, (((1,), (1,)), ((), ())), preferred_element_type=jnp.float32
        ).astype(jnp.bfloat16)


def merge_kernel(part_ref, frame_ref, mask_ref, vw_ref, ow_ref, gain_ref, act_ref):
    groups = part_ref.shape[0]
    ones = (lax.broadcasted_iota(jnp.int32, (16, 128), 0) < 3).astype(jnp.bfloat16)
    levels = [
        lax.dot_general(
            part_ref[g, BLOCK_ROWS - 16 : BLOCK_ROWS, :], ones, (((0,), (0,)), ((), ())), preferred_element_type=jnp.float32
        )
        for g in range(groups)
    ]
    best = levels[0]
    for g in range(1, groups):
        best = jnp.maximum(best, levels[g])
    weights = [jnp.exp2(level - best) for level in levels]
    total = weights[0]
    for g in range(1, groups):
        total = total + weights[g]
    merged = None
    for g in range(groups):
        share = weights[g] / total
        term = part_ref[g].astype(jnp.float32) * jnp.concatenate([share] * 3, axis=1)
        merged = term if merged is None else merged + term
    merged = merged.astype(jnp.bfloat16)
    attention = jnp.dot(merged, vw_ref[...], preferred_element_type=jnp.float32).astype(jnp.bfloat16)
    projected = jnp.dot(attention, ow_ref[...], preferred_element_type=jnp.float32)
    mixed = (frame_ref[...].astype(jnp.float32) + projected).astype(jnp.bfloat16)
    act = silu(rms_scale(mixed, gain_ref[...]))
    usable = jnp.concatenate([mask_ref[...]] * 3, axis=1) > 0.0
    act_ref[...] = jnp.where(usable, act, 0.0).astype(jnp.bfloat16)


def conv(frames, kernel):
    depth = frames.shape[0]
    total = None
    for t in range(depth):
        part = lax.conv_general_dilated(
            frames[t][None], kernel[t], (1, 1), "VALID",
            dimension_numbers=("NHWC", "HWIO", "NHWC"), preferred_element_type=jnp.float32,
        )[0]
        total = part if total is None else total + part
    return total


def local(
    tokens, row_sizes, col_sizes, norm_gain, query_weight, key_weight, value_weight, out_weight,
    cache_one, gain_one, conv_one, cache_two, gain_two, conv_two,
):
    tile_rows, tile_cols, channels = tokens.shape
    n_row = row_sizes.shape[0]
    n_col = col_sizes.shape[0]
    n_y = lax.axis_size("y")
    lat_rows = 88
    ext_cols = tile_cols + 2 * HALO
    half = ext_cols // 2
    core = lax.axis_index("core")
    y_at = lax.axis_index("y")
    row_at = y_at * lax.axis_size("core") + core
    col_at = lax.axis_index("x") * lax.axis_size("z") + lax.axis_index("z")
    row_starts = jnp.cumsum(row_sizes) - row_sizes
    col_starts = jnp.cumsum(col_sizes) - col_sizes
    row_padded = jnp.pad(row_sizes, (1, 1))
    col_padded = jnp.pad(col_sizes, (1, 1))
    tall = row_padded[row_at + 1]
    wide = col_padded[col_at + 1]

    normed = rms_scale(tokens, norm_gain).astype(jnp.bfloat16).reshape(tile_rows * tile_cols, channels)
    slot = jnp.arange(tile_rows * tile_cols, dtype=jnp.int32)
    slot_row = slot // tile_cols
    slot_col = slot - slot_row * tile_cols
    target = jnp.where((slot_row < tall) & (slot_col < wide), slot_row * wide + slot_col, -1)
    chosen = (jnp.arange(KEY_TILE, dtype=jnp.int32)[:, None] == target[None, :]).astype(jnp.bfloat16)
    own_keys = jnp.dot(chosen, normed, preferred_element_type=jnp.float32).astype(jnp.bfloat16)
    tiles = lax.all_gather(own_keys, ("core", "x", "z"), axis=0, tiled=False)
    pair_sizes = lax.dynamic_slice_in_dim(row_sizes, 2 * y_at, 2)
    counts = (pair_sizes[:, None] * col_sizes[None, :]).reshape(-1)
    padded = (counts + 15) // 16 * 16
    ends = jnp.cumsum(padded)
    offsets = jnp.concatenate([jnp.zeros((1,), jnp.int32), ends]).astype(jnp.int32)
    chunk_count = ((ends[-1:] + KEY_CHUNK - 1) // KEY_CHUNK).astype(jnp.int32)
    key_slot = jnp.arange(MAX_CHUNKS * KEY_CHUNK, dtype=jnp.int32)
    key_ok = jnp.any((key_slot[:, None] >= offsets[None, :-1]) & (key_slot[:, None] < (offsets[:-1] + counts)[None, :]), axis=1)
    bias = jnp.where(key_ok, 0.0, masked_score).astype(jnp.float32).reshape(MAX_CHUNKS, 1, KEY_CHUNK)

    coarse = jnp.concatenate([cache_one, tokens[None]], axis=0)
    last_two = pick(coarse, wide - 2, 2)
    last_one = pick(coarse, wide - 1, 2)
    first_one = coarse[:, :, 0]
    first_two = coarse[:, :, 1]
    fine_last = pick(cache_two, 2 * wide - 1, 2)
    fine_first = cache_two[:, :, 0]
    flat = lambda *parts: jnp.concatenate([p.reshape(-1, channels) for p in parts], axis=0)
    near = 3 * tile_rows
    from_left = hop(flat(last_two, last_one, fine_last), COLS, n_col, 1)
    from_right = hop(flat(first_one, first_two, fine_first), COLS, n_col, -1)
    from_left_far = hop(flat(last_one), COLS, n_col, 2)
    from_right_far = hop(flat(first_one), COLS, n_col, -2)
    left_two = jnp.where(col_padded[col_at] >= 2, from_left[:near], from_left_far)
    right_two = jnp.where(col_padded[jnp.minimum(col_at + 2, n_col + 1)] >= 2, from_right[near : 2 * near], from_right_far)
    line = lambda v: v.reshape(3, tile_rows, 1, channels)
    coarse_ext = jnp.concatenate(
        [line(left_two), line(from_left[near : 2 * near]), coarse, jnp.zeros((3, tile_rows, 2, channels), coarse.dtype)], axis=2
    )
    coarse_ext = place(coarse_ext, jnp.concatenate([line(from_right[:near]), line(right_two)], axis=2), wide + HALO, 2)
    fine_line = lambda v: v.reshape(2, 2 * tile_rows, 1, channels)
    fine_ext = jnp.concatenate([fine_line(from_left[2 * near :]), cache_two, fine_line(jnp.zeros_like(from_left[2 * near :]))], axis=2)
    fine_ext = place(fine_ext, fine_line(from_right[2 * near :]), 2 * wide + 1, 2)

    strip = coarse_ext[2]
    own_half = jnp.where(core == 0, strip[:, :half], strip[:, half:])
    other_half = jnp.where(core == 0, strip[:, half:], strip[:, :half])
    swap = [(0, 1), (1, 0)]
    sibling_half = lax.ppermute(other_half, "core", swap)
    two = jnp.where(core == 0, jnp.stack([own_half, sibling_half]), jnp.stack([sibling_half, own_half]))
    two = two.reshape(2, tile_rows * half, channels)
    tall_tile = (tile_rows * half + 15) // 16 * 16
    two = jnp.pad(two, ((0, 0), (0, tall_tile - tile_rows * half), (0, 0)))
    column = lax.all_gather(two.reshape(2 * tall_tile, channels), "y", axis=0, tiled=True).reshape(n_row, tall_tile, channels)
    chip_starts = row_starts[::2]
    tables = jnp.concatenate([row_starts, pick(row_starts, 2 * y_at, 0)[None]]).astype(jnp.int32)
    smem = pl.BlockSpec(memory_space=pltpu.SMEM)
    wide_rows = lat_rows * half + BLOCK_ROWS
    params = pltpu.CompilerParams(vmem_limit_bytes=VMEM_BYTES)
    vmem = lambda: pl.BlockSpec(memory_space=pltpu.VMEM)
    scale = math.log2(math.e) / math.sqrt(channels)

    def query_body(*refs):
        query_kernel(*refs, half=half, lat_rows=lat_rows, scale=scale)

    queries, frame = pl.pallas_call(
        query_body,
        in_specs=[smem, vmem(), vmem(), vmem(), vmem()],
        out_specs=[vmem(), vmem()],
        out_shape=[
            jax.ShapeDtypeStruct((lat_rows * half, channels), jnp.bfloat16),
            jax.ShapeDtypeStruct((BLOCK_ROWS, channels), jnp.bfloat16),
        ],
        scratch_shapes=[pltpu.VMEM((3, wide_rows, 128), jnp.float32)],
        compiler_params=params,
    )(tables, column, norm_gain[None], query_weight, key_weight)

    prior = coarse_ext[:2]
    row_last_two = pick(prior, tall - 2, 1)
    row_last_one = pick(prior, tall - 1, 1)
    near = 2 * ext_cols
    from_up = hop(flat(row_last_two, row_last_one, pick(fine_ext, 2 * tall - 1, 1)), ROWS, n_row, 1)
    from_down = hop(flat(prior[:, 0], prior[:, 1], fine_ext[:, 0]), ROWS, n_row, -1)
    from_up_far = hop(flat(row_last_one), ROWS, n_row, 2)
    from_down_far = hop(flat(prior[:, 0]), ROWS, n_row, -2)
    up_two = jnp.where(row_padded[row_at] >= 2, from_up[:near], from_up_far)
    down_two = jnp.where(row_padded[jnp.minimum(row_at + 2, n_row + 1)] >= 2, from_down[near : 2 * near], from_down_far)
    line = lambda v: v.reshape(2, 1, ext_cols, channels)
    prior_ext = jnp.concatenate(
        [line(up_two), line(from_up[near : 2 * near]), prior, jnp.zeros((2, 2, ext_cols, channels), prior.dtype)], axis=1
    )
    prior_ext = place(prior_ext, jnp.concatenate([line(from_down[:near]), line(down_two)], axis=1), tall + HALO, 1)
    fine_line = lambda v: v.reshape(2, 1, 2 * tile_cols + 2, channels)
    fine_full = jnp.concatenate([fine_line(from_up[2 * near :]), fine_ext, fine_line(jnp.zeros_like(from_up[2 * near :]))], axis=1)
    fine_full = place(fine_full, fine_line(from_down[2 * near :]), 2 * tall + 1, 1)
    prior_sum_one = conv(prior_ext, conv_one)
    prior_sum_two = conv(fine_full, conv_two)

    def attention_body(*refs):
        attention_kernel(*refs, half=half)

    parts = pl.pallas_call(
        attention_body,
        in_specs=[smem, smem, smem, vmem(), vmem(), vmem()],
        out_specs=vmem(),
        out_shape=jax.ShapeDtypeStruct((n_y, BLOCK_ROWS, channels), jnp.bfloat16),
        scratch_shapes=[
            pltpu.VMEM((KEY_ROWS, channels), jnp.bfloat16),
            pltpu.VMEM((2, MAX_CHUNKS, QUERY_BLOCK, KEY_CHUNK), jnp.float32),
            pltpu.VMEM((2, QUERY_BLOCK, 128), jnp.float32),
            pltpu.VMEM((QUERY_BLOCK, 128), jnp.float32),
            pltpu.VMEM((QUERY_BLOCK, channels), jnp.float32),
            pltpu.VMEM((3, wide_rows, 128), jnp.float32),
            pltpu.VMEM((wide_rows, 128), jnp.float32),
        ],
        compiler_params=params,
    )(offsets, chunk_count, chip_starts.astype(jnp.int32), queries, tiles.reshape(2 * n_col, KEY_TILE, channels), bias)
    parts = lax.all_to_all(parts, "y", 0, 0)

    spot = jnp.arange(BLOCK_ROWS, dtype=jnp.int32)
    spot_row = pick(row_starts, 2 * y_at, 0) - HALO + spot // half
    spot_col = pick(col_starts, col_at, 0) - HALO + spot % half + half * core
    inside = (spot_row >= 0) & (spot_row < lat_rows) & (spot_col >= 0) & (spot_col < jnp.sum(col_sizes))
    mask = jnp.broadcast_to(inside.astype(jnp.float32)[:, None], (BLOCK_ROWS, 128))
    act = pl.pallas_call(
        merge_kernel,
        in_specs=[vmem()] * 6 + [],
        out_specs=vmem(),
        out_shape=jax.ShapeDtypeStruct((BLOCK_ROWS, channels), jnp.bfloat16),
        compiler_params=params,
    )(parts, frame, mask, value_weight, out_weight, gain_one[None])
    act = act.reshape(BLOCK_ROWS // half, half, channels)
    ext_rows = tile_rows + 2 * HALO
    upper = act[:ext_rows]
    lower = lax.dynamic_slice_in_dim(act, row_sizes[2 * y_at], ext_rows, 0)
    mine = jnp.where(core == 0, upper, lower)
    theirs = lax.ppermute(jnp.where(core == 0, lower, upper), "core", swap)
    act_one = jnp.where(
        core == 0, jnp.concatenate([mine, theirs], axis=1), jnp.concatenate([theirs, mine], axis=1)
    )

    y_one = (conv(act_one[None], conv_one[2:]) + prior_sum_one).astype(jnp.bfloat16)
    act_small = silu(rms_scale(y_one, gain_two)).astype(jnp.bfloat16)
    near_row = jnp.arange(tile_rows + 2, dtype=jnp.int32) + pick(row_starts, row_at, 0) - 1
    near_col = jnp.arange(tile_cols + 2, dtype=jnp.int32) + pick(col_starts, col_at, 0) - 1
    inside = ((near_row >= 0) & (near_row < lat_rows))[:, None] & ((near_col >= 0) & (near_col < jnp.sum(col_sizes)))[None, :]
    act_small = jnp.where(inside[:, :, None], act_small, jnp.zeros_like(act_small))
    act_two = jnp.repeat(jnp.repeat(act_small, 2, axis=0), 2, axis=1)[1:-1, 1:-1]
    y_two = conv(act_two[None], conv_two[2:]) + prior_sum_two
    row_usable = jnp.arange(2 * tile_rows, dtype=jnp.int32) < 2 * tall
    col_usable = jnp.arange(2 * tile_cols, dtype=jnp.int32) < 2 * wide
    usable = (row_usable[:, None] & col_usable[None, :])[:, :, None]
    return jnp.where(usable, y_two, 0.0).astype(jnp.bfloat16)


def solution(mesh):
    grid = Mesh(mesh.devices.reshape(4, 2, 4, 4), ("y", "core", "x", "z"))
    placed = (
        P(ROWS, COLS, None), P(), P(), P(), P(), P(), P(), P(),
        P(None, ROWS, COLS, None), P(), P(), P(None, ROWS, COLS, None), P(), P(),
    )
    return jax.shard_map(local, mesh=grid, in_specs=placed, out_specs=P(ROWS, COLS, None), check_vma=False)
```

time: 394 us -> 190 us (0.48)
  waiting for transfers between devices: 116 us -> 3.04 us
  local copies, waits for them, and re-layouts: 131 us -> 29.6 us
  matrix products: 68.9 us -> 23.8 us
  Pallas kernels: 0 us -> 37.2 us
  starting transfers between devices: 20.1 us -> 37.1 us
  other arithmetic: 32.1 us -> 17 us
  blocking collectives: 0 us -> 12.3 us
  between operations: 20.4 us -> 26.4 us
    all_gather x2 -> x1, waiting for transfers between devices: 110 us -> 0.02 us  [local(): tiles = lax.all_gather(own_keys, ('core', 'x', 'z'), axis=0, tiled=False)]
    unnamed x77 -> x37, local copies, waits for them, and re-layouts: 106 us -> 2.99 us
    dot_general x7 -> x1, matrix products: 68.9 us -> 0.97 us  [local(): jnp.dot(chosen, normed, preferred_element_type=jnp.float32)]
    pallas_call x0 -> x3, Pallas kernels: none -> 37.2 us  [the longest x1 29.6 us: local(): pl.pallas_call(attention_body, in_specs=[smem, smem, smem, vmem(), vmem()...]
    conv_general_dilated x0 -> x6, matrix products: none -> 22.9 us  [conv(): lax.conv_general_dilated(frames[t][None], kernel[t], (1, 1), 'VALID', dim...]
    reduce_sum x5 -> x0, other arithmetic: 22.3 us -> none  [the longest x1 17.3 us: local(): denominator = jnp.sum(expos, axis=1)]
    all_gather x0 -> x1, blocking collectives: none -> 12.3 us  [local(): lax.all_gather(two.reshape(2 * tall_tile, channels), 'y', axis=0, tiled=T...]
    ppermute x8 -> x10, starting transfers between devices: 20 us -> 31.5 us  [the longest x8 23.8 us: hop(): return lax.ppermute(value, axes, pairs)]
  transfers between devices with their start and end apart: 10 -> 12, of which waited for: 5 -> 1; matrix products, arithmetic and copies ran while one was open for 26% -> 23% of each run, Pallas kernels for 0% -> 2%
where the time goes in v1:
time: 190 us; the launch traced here: 186 us
  Pallas kernels  37.2 us (20%)
  starting transfers between devices  37.1 us (20%)
  local copies, waits for them, and re-layouts  29.6 us (16%)
  between operations  26.4 us (14%)
  matrix products  23.8 us (13%)
  other arithmetic  17 us (9%)
  blocking collectives  12.3 us (6%)
  waiting for transfers between devices  3.04 us (2%)
    pallas_call x1, Pallas kernels, local(): pl.pallas_call(attention_body, in_specs=[smem, smem, smem, vmem(), vmem()...  29.6 us
    ppermute x8, starting transfers between devices, hop(): return lax.ppermute(value, axes, pairs)  23.8 us
    conv_general_dilated x6, matrix products, conv(): lax.conv_general_dilated(frames[t][None], kernel[t], (1, 1), 'VALID', dim...  22.9 us
    all_gather x1, blocking collectives, local(): lax.all_gather(two.reshape(2 * tall_tile, channels), 'y', axis=0, tiled=T...  12.3 us
    ppermute x1, starting transfers between devices, local(): theirs = lax.ppermute(jnp.where(core == 0, lower, upper), 'core', swap)  5.61 us
    all_to_all x1, starting transfers between devices, local(): parts = lax.all_to_all(parts, 'y', 0, 0)  5.54 us
    conv_general_dilated x15, local copies, waits for them, and re-layouts, conv(): lax.conv_general_dilated(frames[t][None], kernel[t], (1, 1), 'VALID', dim...  4.71 us
    dynamic_update_slice x3, local copies, waits for them, and re-layouts, place(): return lax.dynamic_update_slice_in_dim(values, part, index, axis)  4.68 us
  transfers between devices with their start and end apart: 12, of which 1 were waited for; matrix products, arithmetic and copies ran while one was open for 23% of the time, Pallas kernels for 2%

profile of v1, /device:TPU:1, one launch (start us, length us, event | category | flops | bytes accessed | tf_op | source)
XLA Modules:
  0.0 186.4 jit_solution(10482790382843937708)
XLA Ops:
  10.2 1.4 pad_dynamic-slice_fusion.7
  16.0 6.3 %collective-permute-start.1 = (bf16[39,384]{1,0:T(8,128)(2,1)S(1)}, bf16[39,384]{1,0:T(8,128)(2,1)S(1)}, u32[]{:S(2)}, u32[]{:S(2)}) collective-permute-start(bf16[39,384]{1,0:T(8,128)(2,1)S(1)} %reshape.476), channel_id=1, source_target_pairs={{0,2},{1,3},{2,4},{3,5},{4,6},{5,7},{6,8},{7,9},{8,10},{9,11},{10,... | collective-permute-start | bytes 89864 | tf_op jit(solution)/shard_map/ppermute | solution.py:36
  24.2 1.5 slice_reduce_fusion
  27.2 4.0 %collective-permute-start = (bf16[130,384]{1,0:T(8,128)(2,1)S(1)}, bf16[130,384]{1,0:T(8,128)(2,1)S(1)}, u32[]{:S(2)}, u32[]{:S(2)}) collective-permute-start(bf16[130,384]{1,0:T(8,128)(2,1)S(1)} %pad_maximum_fusion.2), channel_id=1, source_target_pairs={{0,1},{1,2},{2,3},{3,4},{4,5},{5,6},{6,7},{7,8},{8,9},{9,10},{10,1... | collective-permute-start | bytes 299528 | tf_op jit(solution)/shard_map/ppermute | solution.py:36
  53.4 2.4 %dynamic_update_slice.12 = bf16[3,13,24,384]{3,2,1,0:T(8,128)(2,1)S(1)} dynamic-update-slice(bf16[3,13,24,384]{3,2,1,0:T(8,128)(2,1)S(1)} %maximum_maximum_fusion.2, bf16[3,13,2,384]{3,2,1,0:T(2,128)(2,1)S(1)} %copy.82, s32[]{:T(128)} %constant.182.clone.1, s32[]{:T(128)} %constant.182.clone.1, s32[]{:T(128)S(6)} %select_n.227, s32[]{:T(128)} %constant.182.clone.1) | dynamic-update-slice | bytes 119812 | tf_op jit(solution)/shard_map/dynamic_update_slice | solution.py:44
  57.2 4.6 %collective-permute-start.7 = (bf16[48,384]{1,0:T(8,128)(2,1)S(1)}, bf16[48,384]{1,0:T(8,128)(2,1)}, u32[]{:S(2)}, u32[]{:S(2)}) collective-permute-start(bf16[48,384]{1,0:T(8,128)(2,1)S(1)} %bitcast.152), channel_id=1, source_target_pairs={{0,32},{16,48},{32,64},{48,80},{64,96},{80,112},{1,33},{17,49},{33... | collective-permute-start | bytes 110600 | tf_op jit(solution)/shard_map/ppermute | solution.py:36
  61.9 2.2 %collective-permute-start.4 = (bf16[13,12,384]{2,1,0:T(8,128)(2,1)S(1)}, bf16[13,12,384]{2,1,0:T(8,128)(2,1)S(1)}, u32[]{:S(2)}, u32[]{:S(2)}) collective-permute-start(bf16[13,12,384]{2,1,0:T(8,128)(2,1)S(1)} %get-tuple-element.28), channel_id=1, source_target_pairs={{0,16},{16,0},{1,17},{17,1},{2,18},{18,2},{3,19},{19,3},{4,20},{20... | collective-permute-start | bytes 359432 | tf_op jit(solution)/shard_map/ppermute | solution.py:271
  64.1 2.3 %maximum_maximum_fusion.1 = bf16[2,26,42,384]{3,2,1,0:T(8,128)(2,1)S(1)} fusion(bf16[2,26,40,384]{3,2,1,0:T(8,128)(2,1)} %param.25, bf16[2,26,1,384]{3,2,1,0:T(2,128)(2,1)S(1)} %reshape.568, bf16[42]{0:T(256)(128)(2,1)S(1)} %pad.51.clone), kind=kLoop, calls=%fused_computation.14 | loop fusion | flops 5031936 | bytes 3314772 | tf_op jit(solution)/shard_map/concatenate | solution.py:264
  66.4 2.3 %dynamic_update_slice.13 = bf16[2,26,42,384]{3,2,1,0:T(8,128)(2,1)S(1)} dynamic-update-slice(bf16[2,26,42,384]{3,2,1,0:T(8,128)(2,1)S(1)} %maximum_maximum_fusion.1, bf16[2,26,1,384]{3,2,1,0:T(2,128)(2,1)S(1)} %reshape.569, s32[]{:T(128)} %constant.182.clone.1, s32[]{:T(128)} %constant.182.clone.1, s32[]{:T(128)S(6)} %select_n.243, s32[]{:T(128)} %constant.182.clone.1) | dynamic-update-slice | bytes 79876 | tf_op jit(solution)/shard_map/dynamic_update_slice | solution.py:44
  69.5 2.6 %collective-permute-start.6 = (bf16[180,384]{1,0:T(8,128)(2,1)}, bf16[180,384]{1,0:T(8,128)(2,1)}, u32[]{:S(2)}, u32[]{:S(2)}) collective-permute-start(bf16[180,384]{1,0:T(8,128)(2,1)} %pad_maximum_fusion), channel_id=1, source_target_pairs={{0,16},{16,32},{32,48},{48,64},{64,80},{80,96},{96,112},{1,17},{17... | collective-permute-start | bytes 414728 | tf_op jit(solution)/shard_map/ppermute | solution.py:36
  72.1 2.4 %collective-permute-start.8 = (bf16[180,384]{1,0:T(8,128)(2,1)S(1)}, bf16[180,384]{1,0:T(8,128)(2,1)S(1)}, u32[]{:S(2)}, u32[]{:S(2)}) collective-permute-start(bf16[180,384]{1,0:T(8,128)(2,1)S(1)} %pad_maximum_fusion.1), channel_id=1, source_target_pairs={{16,0},{32,16},{48,32},{64,48},{80,64},{96,80},{112,96},{17,1},{33... | collective-permute-start | bytes 414728 | tf_op jit(solution)/shard_map/ppermute | solution.py:36
  74.7 12.3 %all_gather.9 = bf16[1280,384]{1,0:T(8,128)(2,1)} all-gather(bf16[320,384]{1,0:T(8,128)(2,1)S(1)} %bitcast.147), channel_id=1, replica_groups=mesh['y'=4,'core'=2,'x'=4,'z'=4] {'y'}, dimensions={0}, use_global_device_ids=true | all-gather | bytes 1228800 | tf_op jit(solution)/shard_map/all_gather | solution.py:276
  86.9 4.1 %shard_map.136 = (bf16[1056,384]{1,0:T(8,128)(2,1)}, bf16[384,384]{1,0:T(8,128)(2,1)}) custom-call(s32[9]{0:T(128)} %pad_add_fusion.1.refs_0_, bf16[8,160,384]{2,1,0:T(8,128)(2,1)} %bitcast.142, f32[1,384]{1,0:T(1,128)} %broadcast_in_dim.87.refs_2_, bf16[384,384]{1,0:T(8,128)(2,1)} %refs_3_.1, bf16[384,384]{1,0:T(8,128)(2,1)} %refs_4_.1), custom_call_target="tpu_custom_call" | custom-call | tf_op jit(solution)/shard_map/pallas_call | solution.py:288
  100.4 29.6 %shard_map.137 = bf16[4,384,384]{2,1,0:T(8,128)(2,1)} custom-call(s32[33]{0:T(128)} %copy-done.10, s32[1]{0:T(128)S(6)} %select_n.218.refs_1_, s32[4]{0:T(128)} %slice.122.refs_2_, bf16[1056,384]{1,0:T(8,128)(2,1)} %get-tuple-element.7.refs_3_, bf16[32,272,384]{2,1,0:T(8,128)(2,1)} %bitcast.137, f32[14,1,512]{2,1,0:T(1,128)} %bitcast.160), custom_call_target="tpu_custom_call" | custom-call | tf_op jit(solution)/shard_map/pallas_call | solution.py:324
  130.0 5.5 %all-to-all-start = ((bf16[4,384,384]{2,1,0:T(8,128)(2,1)}), bf16[4,384,384]{2,1,0:T(8,128)(2,1)S(1)}, u32[]{:S(2)}, u32[]{:S(2)}) async-start(bf16[4,384,384]{2,1,0:T(8,128)(2,1)} %shard_map.137), calls=%async_computation | async-start | bytes 2359296 | tf_op jit(solution)/shard_map/all_to_all | solution.py:340
  135.5 4.3 %fusion.33 = f32[26,8,6,192]{3,1,2,0:T(8,128)S(1)} fusion(bf16[28,1,7,2,384]{4,2,3,0,1:T(8,128)(2,1)S(1)} %slice.201, bf16[28,1,8,6,384]{4,2,3,0,1:T(8,128)(2,1)} %copy-done.2, bf16[3,3,3,384,192]{3,4,2,1,0:T(8,128)(2,1)} %param.27, pred[8,6]{0,1:T(8,128)(4,1)S(1)} %copy-done.14), kind=kOutput, calls=%fused_computation.33 | convolution fusion | flops 1660594176 | bytes 3618864 | tf_op jit(solution)/shard_map/conv_general_dilated | solution.py:195
  139.8 4.9 %fusion.45 = f32[26,8,6,192]{3,1,2,0:T(8,128)} fusion(f32[26,8,6,192]{3,1,2,0:T(8,128)S(1)} %fusion.33, bf16[28,1,7,2,384]{4,2,3,0,1:T(8,128)(2,1)S(1)} %copy-done.6, bf16[28,1,8,6,384]{4,2,3,0,1:T(8,128)(2,1)S(1)} %copy.102, bf16[3,3,3,384,192]{3,4,2,1,0:T(8,128)(2,1)} %param.27, pred[8,6]{0,1:T(8,128)(4,1)S(1)} %copy-done.14), kind=kOutput, calls=%fused_computation.37 | convolution fusion | flops 1660833792 | bytes 4577328 | tf_op jit(solution)/shard_map/conv_general_dilated | solution.py:195
  144.7 3.0 %all-to-all-done.part_ref = bf16[4,384,384]{2,1,0:T(8,128)(2,1)S(1)} async-done(((bf16[4,384,384]{2,1,0:T(8,128)(2,1)}), bf16[4,384,384]{2,1,0:T(8,128)(2,1)S(1)}, u32[]{:S(2)}, u32[]{:S(2)}) %all-to-all-start) | async-done | bytes 1179680 | tf_op jit(solution)/shard_map/all_to_all | solution.py:340
  148.8 3.6 %shard_map.138 = bf16[384,384]{1,0:T(8,128)(2,1)} custom-call(bf16[4,384,384]{2,1,0:T(8,128)(2,1)} %copy-done, bf16[384,384]{1,0:T(8,128)(2,1)} %get-tuple-element.8.frame_ref, f32[384,128]{1,0:T(8,128)} %broadcast_in_dim.90.mask_ref, bf16[384,384]{1,0:T(8,128)(2,1)} %vw_ref.1, bf16[384,384]{1,0:T(8,128)(2,1)} %ow_ref.1, f32[1,384]{1,0:T(1,128)} %broadcast_in_dim.91.gain_ref), custom_call_target="tpu_custom_call" | custom-call | tf_op jit(solution)/shard_map/pallas_call | solution.py:347
  154.4 5.6 %collective-permute-start.5 = (bf16[17,12,384]{2,1,0:T(8,128)(2,1)S(1)}, bf16[17,12,384]{2,1,0:T(8,128)(2,1)S(1)}, u32[]{:S(2)}, u32[]{:S(2)}) collective-permute-start(bf16[17,12,384]{2,1,0:T(8,128)(2,1)S(1)} %get-tuple-element.24), channel_id=1, source_target_pairs={{0,16},{16,0},{1,17},{17,1},{2,18},{18,2},{3,19},{19,3},{4,20},{20... | collective-permute-start | bytes 470024 | tf_op jit(solution)/shard_map/ppermute | solution.py:359
  160.0 3.3 %fusion.57 = f32[15,8,3,384]{3,1,2,0:T(8,128)S(1)} fusion(bf16[3,3,3,384,384]{4,3,2,1,0:T(8,128)(2,1)} %param.24, bf16[17,1,7,2,384]{4,2,3,0,1:T(8,128)(2,1)S(1)} %slice.190, bf16[17,1,8,3,384]{4,2,3,0,1:T(8,128)(2,1)S(1)} %copy-done.4, pred[8,3]{0,1:T(4,128)(4,1)S(1)} %copy-done.15), kind=kOutput, calls=%fused_computation.45 | convolution fusion | flops 957219840 | bytes 3703320 | tf_op jit(solution)/shard_map/conv_general_dilated | solution.py:195
  164.0 3.3 %fusion.54 = f32[15,8,3,384]{3,1,2,0:T(8,128)S(1)} fusion(bf16[3,3,3,384,384]{4,3,2,1,0:T(8,128)(2,1)} %param.24, bf16[17,1,7,2,384]{4,2,3,0,1:T(8,128)(2,1)S(1)} %slice.178, bf16[17,1,8,3,384]{4,2,3,0,1:T(8,128)(2,1)S(1)} %copy.84, pred[8,3]{0,1:T(4,128)(4,1)S(1)} %copy-done.15), kind=kOutput, calls=%fused_computation.44 | convolution fusion | flops 957219840 | bytes 3703320 | tf_op jit(solution)/shard_map/conv_general_dilated | solution.py:195
  167.3 3.3 %fusion.69 = bf16[15,8,3,384]{3,1,2,0:T(8,128)(2,1)S(1)} fusion(f32[15,8,3,384]{3,1,2,0:T(8,128)S(1)} %fusion.54, f32[15,8,3,384]{3,1,2,0:T(8,128)S(1)} %fusion.57, bf16[3,3,3,384,384]{4,3,2,1,0:T(8,128)(2,1)} %param.24, bf16[17,1,7,2,384]{4,2,3,0,1:T(8,128)(2,1)S(1)} %slice.192, bf16[17,1,8,3,384]{4,2,3,0,1:T(8,128)(2,1)S(1)} %copy.94, ...), kind=kOutput, calls=%fused_computation.49 | convolution fusion | flops 957634560 | bytes 4532760 | tf_op jit(solution)/shard_map/conv_general_dilated | solution.py:195
  174.1 3.9 %fusion.42 = bf16[26,8,6,192]{3,1,2,0:T(8,128)(2,1)S(1)} fusion(f32[26,8,6,192]{3,1,2,0:T(8,128)S(1)} %copy-done.16, bf16[28,1,7,2,384]{4,2,3,0,1:T(8,128)(2,1)S(1)} %slice.195, bf16[28,1,8,6,384]{4,2,3,0,1:T(8,128)(2,1)S(1)} %copy.97, bf16[3,3,3,384,192]{3,4,2,1,0:T(8,128)(2,1)} %param.27, pred[8,6]{0,1:T(8,128)(4,1)S(1)} %copy-done.14), kind=kOutput, calls=%fused_computation.36 | convolution fusion | flops 1661073408 | bytes 4098096 | tf_op jit(solution)/shard_map/conv_general_dilated | solution.py:195
  (180 shorter events, 41.6 us)
Async XLA Ops:
  6.5 8.7 %copy-start.1 = (bf16[13,20,384]{2,1,0:T(8,128)(2,1)S(1)}, bf16[13,20,384]{2,1,0:T(8,128)(2,1)}, u32[]{:S(2)}) copy-start(bf16[13,20,384]{2,1,0:T(8,128)(2,1)} %param.14) | copy-start | bytes 599044
  6.5 8.6 %copy-start.5 = (bf16[2,13,20,384]{3,0,2,1:T(2,128)(2,1)S(1)}, bf16[2,13,20,384]{3,0,2,1:T(2,128)(2,1)}, u32[]{:S(2)}) copy-start(bf16[2,13,20,384]{3,0,2,1:T(2,128)(2,1)} %param.22) | copy-start | bytes 1198084
  6.5 93.9 %all-gather.3.cloned.1.call-start = ((), (), s32[]{:S(2)}) async-start(), calls=%async_computation.1 | async-start | bytes 6893568 | tf_op jit(solution)/shard_map/all_gather | solution.py:232
  8.8 22.5 %copy-start.11 = (s32[8]{0:T(128)S(1)}, s32[8]{0:T(128)}, u32[]{:S(2)}) copy-start(s32[8]{0:T(128)} %param.15) | copy-start | bytes 100
  8.8 23.3 %copy-start.8 = (s32[16]{0:T(128)S(1)}, s32[16]{0:T(128)}, u32[]{:S(2)}) copy-start(s32[16]{0:T(128)} %param.16) | copy-start | bytes 196
  11.7 33.7 %copy-start.7 = (f32[384]{0:T(512)S(1)}, f32[384]{0:T(512)}, u32[]{:S(2)}) copy-start(f32[384]{0:T(512)} %param.17) | copy-start | bytes 4612
  12.9 38.5 %copy-start.12 = (f32[384]{0:T(512)S(1)}, f32[384]{0:T(512)}, u32[]{:S(2)}) copy-start(f32[384]{0:T(512)} %param.23) | copy-start | bytes 4612
  16.0 36.8 %collective-permute-start.1 = (bf16[39,384]{1,0:T(8,128)(2,1)S(1)}, bf16[39,384]{1,0:T(8,128)(2,1)S(1)}, u32[]{:S(2)}, u32[]{:S(2)}) collective-permute-start(bf16[39,384]{1,0:T(8,128)(2,1)S(1)} %reshape.476), channel_id=1, source_target_pairs={{0,2},{1,3},{2,4},{3,5},{4,6},{5,7},{6,8},{7,9},{8,10},{9,11},{10,... | collective-permute-start | bytes 89864 | tf_op jit(solution)/shard_map/ppermute | solution.py:36
  22.3 30.2 %collective-permute-start.3 = (bf16[39,384]{1,0:T(8,128)(2,1)S(1)}, bf16[39,384]{1,0:T(8,128)(2,1)S(1)}, u32[]{:S(2)}, u32[]{:S(2)}) collective-permute-start(bf16[39,384]{1,0:T(8,128)(2,1)S(1)} %reshape_squeeze.20), channel_id=1, source_target_pairs={{2,0},{3,1},{4,2},{5,3},{6,4},{7,5},{8,6},{9,7},{10,8},{11,9},{12,... | collective-permute-start | bytes 89864 | tf_op jit(solution)/shard_map/ppermute | solution.py:36
  25.8 26.7 %collective-permute-start.2 = (bf16[130,384]{1,0:T(8,128)(2,1)S(1)}, bf16[130,384]{1,0:T(8,128)(2,1)S(1)}, u32[]{:S(2)}, u32[]{:S(2)}) collective-permute-start(bf16[130,384]{1,0:T(8,128)(2,1)S(1)} %pad_maximum_fusion.3), channel_id=1, source_target_pairs={{1,0},{2,1},{3,2},{4,3},{5,4},{6,5},{7,6},{8,7},{9,8},{10,9},{11,1... | collective-permute-start | bytes 299528 | tf_op jit(solution)/shard_map/ppermute | solution.py:36
  27.2 25.5 %collective-permute-start = (bf16[130,384]{1,0:T(8,128)(2,1)S(1)}, bf16[130,384]{1,0:T(8,128)(2,1)S(1)}, u32[]{:S(2)}, u32[]{:S(2)}) collective-permute-start(bf16[130,384]{1,0:T(8,128)(2,1)S(1)} %pad_maximum_fusion.2), channel_id=1, source_target_pairs={{0,1},{1,2},{2,3},{3,4},{4,5},{5,6},{6,7},{7,8},{8,9},{9,10},{10,1... | collective-permute-start | bytes 299528 | tf_op jit(solution)/shard_map/ppermute | solution.py:36
  37.9 18.0 %copy-start.10 = (s32[33]{0:T(128)}, s32[33]{0:T(128)S(1)}, u32[]{:S(2)}) copy-start(s32[33]{0:T(128)S(1)} %pad_add_fusion.refs_0_) | copy-start | bytes 400
  55.9 39.3 %collective-permute-start.9 = (bf16[48,384]{1,0:T(8,128)(2,1)S(1)}, bf16[48,384]{1,0:T(8,128)(2,1)S(1)}, u32[]{:S(2)}, u32[]{:S(2)}) collective-permute-start(bf16[48,384]{1,0:T(8,128)(2,1)S(1)} %bitcast.150), channel_id=1, source_target_pairs={{32,0},{48,16},{64,32},{80,48},{96,64},{112,80},{33,1},{49,17},{65... | collective-permute-start | bytes 110600 | tf_op jit(solution)/shard_map/ppermute | solution.py:36
  57.2 35.3 %collective-permute-start.7 = (bf16[48,384]{1,0:T(8,128)(2,1)S(1)}, bf16[48,384]{1,0:T(8,128)(2,1)}, u32[]{:S(2)}, u32[]{:S(2)}) collective-permute-start(bf16[48,384]{1,0:T(8,128)(2,1)S(1)} %bitcast.152), channel_id=1, source_target_pairs={{0,32},{16,48},{32,64},{48,80},{64,96},{80,112},{1,33},{17,49},{33... | collective-permute-start | bytes 110600 | tf_op jit(solution)/shard_map/ppermute | solution.py:36
  61.9 12.6 %collective-permute-start.4 = (bf16[13,12,384]{2,1,0:T(8,128)(2,1)S(1)}, bf16[13,12,384]{2,1,0:T(8,128)(2,1)S(1)}, u32[]{:S(2)}, u32[]{:S(2)}) collective-permute-start(bf16[13,12,384]{2,1,0:T(8,128)(2,1)S(1)} %get-tuple-element.28), channel_id=1, source_target_pairs={{0,16},{16,0},{1,17},{17,1},{2,18},{18,2},{3,19},{19,3},{4,20},{20... | collective-permute-start | bytes 359432 | tf_op jit(solution)/shard_map/ppermute | solution.py:271
  69.5 21.5 %collective-permute-start.6 = (bf16[180,384]{1,0:T(8,128)(2,1)}, bf16[180,384]{1,0:T(8,128)(2,1)}, u32[]{:S(2)}, u32[]{:S(2)}) collective-permute-start(bf16[180,384]{1,0:T(8,128)(2,1)} %pad_maximum_fusion), channel_id=1, source_target_pairs={{0,16},{16,32},{32,48},{48,64},{64,80},{80,96},{96,112},{1,17},{17... | collective-permute-start | bytes 414728 | tf_op jit(solution)/shard_map/ppermute | solution.py:36
  72.1 19.8 %collective-permute-start.8 = (bf16[180,384]{1,0:T(8,128)(2,1)S(1)}, bf16[180,384]{1,0:T(8,128)(2,1)S(1)}, u32[]{:S(2)}, u32[]{:S(2)}) collective-permute-start(bf16[180,384]{1,0:T(8,128)(2,1)S(1)} %pad_maximum_fusion.1), channel_id=1, source_target_pairs={{16,0},{32,16},{48,32},{64,48},{80,64},{96,80},{112,96},{17,1},{33... | collective-permute-start | bytes 414728 | tf_op jit(solution)/shard_map/ppermute | solution.py:36
  74.6 17.3 %copy-start.13 = (bf16[28]{0:T(256)(128)(2,1)S(1)}, bf16[28]{0:T(256)(128)(2,1)}, u32[]{:S(2)}) copy-start(bf16[28]{0:T(256)(128)(2,1)} %pad.30.clone) | copy-start | bytes 172
  130.0 5.5 %copy-start.14 = (pred[8,6]{0,1:T(8,128)(4,1)S(1)}, pred[8,6]{0,1:T(8,128)(4,1)}, u32[]{:S(2)}) copy-start(pred[8,6]{0,1:T(8,128)(4,1)} %constant.254) | copy-start | bytes 148
  130.0 17.7 %all-to-all-start = ((bf16[4,384,384]{2,1,0:T(8,128)(2,1)}), bf16[4,384,384]{2,1,0:T(8,128)(2,1)S(1)}, u32[]{:S(2)}, u32[]{:S(2)}) async-start(bf16[4,384,384]{2,1,0:T(8,128)(2,1)} %shard_map.137), calls=%async_computation | async-start | bytes 2359296 | tf_op jit(solution)/shard_map/all_to_all | solution.py:340
  135.5 4.3 %copy-start.6 = (bf16[28,1,7,2,384]{4,2,3,0,1:T(8,128)(2,1)S(1)}, bf16[28,1,7,2,384]{4,2,3,0,1:T(8,128)(2,1)}, u32[]{:S(2)}) copy-start(bf16[28,1,7,2,384]{4,2,3,0,1:T(8,128)(2,1)} %slice.199) | copy-start | bytes 903172
  148.8 11.2 %copy-start.4 = (bf16[17,1,8,3,384]{4,2,3,0,1:T(8,128)(2,1)S(1)}, bf16[17,1,8,3,384]{4,2,3,0,1:T(8,128)(2,1)}, u32[]{:S(2)}) copy-start(bf16[17,1,8,3,384]{4,2,3,0,1:T(8,128)(2,1)} %copy-done.3) | copy-start | bytes 940036
  148.8 11.2 %copy-start.15 = (pred[8,3]{0,1:T(4,128)(4,1)S(1)}, pred[8,3]{0,1:T(4,128)(4,1)}, u32[]{:S(2)}) copy-start(pred[8,3]{0,1:T(4,128)(4,1)} %constant.255) | copy-start | bytes 76
  154.4 9.1 %collective-permute-start.5 = (bf16[17,12,384]{2,1,0:T(8,128)(2,1)S(1)}, bf16[17,12,384]{2,1,0:T(8,128)(2,1)S(1)}, u32[]{:S(2)}, u32[]{:S(2)}) collective-permute-start(bf16[17,12,384]{2,1,0:T(8,128)(2,1)S(1)} %get-tuple-element.24), channel_id=1, source_target_pairs={{0,16},{16,0},{1,17},{17,1},{2,18},{18,2},{3,19},{19,3},{4,20},{20... | collective-permute-start | bytes 470024 | tf_op jit(solution)/shard_map/ppermute | solution.py:359
  (5 other events, 7.7 us)
Sparse Core Ops, SparseCore 0:
  14.0 54.7 all-gather.2

commit v2 on v1

v2 whole, which is shorter than its diff:
```python
import math

import jax
import jax.numpy as jnp
from jax import lax
from jax.experimental import pallas as pl
from jax.experimental.pallas import tpu as pltpu
from jax.sharding import Mesh
from jax.sharding import PartitionSpec as P

epsilon = 1e-06
masked_score = -1e30
ROWS = ("y", "core")
COLS = ("x", "z")
LAT_ROWS = 88
LAT_COLS = 256
TILE_ROWS = 13
TILE_COLS = 20
HALO = 2
EXT_ROWS = TILE_ROWS + 2 * HALO
EXT_COLS = TILE_COLS + 2 * HALO
HALF = EXT_COLS // 2
FRONT = HALO * HALF
FINE_ROWS = 2 * TILE_ROWS
FINE_COLS = 2 * TILE_COLS
FINE_PITCH = 48
KEY_TILE = 272
KEY_CHUNK = 512
MAX_CHUNKS = 14
KEY_ROWS = MAX_CHUNKS * KEY_CHUNK + KEY_CHUNK
QUERY_BLOCK = 352
BLOCK_ROWS = 384
HALF_ROWS = 208
WIDE_ROWS = LAT_ROWS * HALF + BLOCK_ROWS
TALL_TILE = 160
VMEM_BYTES = 60 * 1024 * 1024
NEAR = 48


def rms_scale(values_in, gain_vec):
    wide = values_in.astype(jnp.float32)
    return wide * lax.rsqrt(jnp.mean(wide * wide, axis=-1, keepdims=True) + epsilon) * gain_vec


def silu(v):
    return v / (1.0 + jnp.exp(-v))


def hop(value, axes, count, step):
    pairs = [(i, i + step) for i in range(count) if 0 <= i + step < count]
    return lax.ppermute(value, axes, pairs)


def put_rows(ref, start, value):
    for g in range(ref.shape[0]):
        ref[g, pl.ds(start, value.shape[0]), :] = value[:, g * 128 : (g + 1) * 128].astype(ref.dtype)


def get_rows(ref, start, count, stride=None):
    return jnp.concatenate([ref[g, pl.ds(start, count, stride), :] for g in range(ref.shape[0])], axis=1)


def put_strided(ref, start, stride, value):
    for g in range(ref.shape[0]):
        ref[g, pl.ds(start, value.shape[0], stride), :] = value[:, g * 128 : (g + 1) * 128].astype(ref.dtype)


def before(size_ref, index):
    total = 0
    for t in range(size_ref.shape[0]):
        total = total + jnp.where(t < index, size_ref[t], 0)
    return total


def size_at(size_ref, index):
    count = size_ref.shape[0]
    inside = (index >= 0) & (index < count)
    return jnp.where(inside, size_ref[jnp.clip(index, 0, count - 1)], 0)


def prepare_kernel(
    place_ref, row_ref, col_ref, token_ref, one_ref, two_ref, gain_ref,
    key_ref, right_ref, left_ref, right_far_ref, left_far_ref, pack_ref, coarse_ref, fine_ref,
):
    wide = col_ref[place_ref[1]]
    pack_ref[...] = jnp.zeros_like(pack_ref)
    for i in range(TILE_ROWS):
        raw = token_ref[i].astype(jnp.float32)
        put_rows(coarse_ref, (2 * TILE_ROWS + i) * 24, raw)
        put_rows(pack_ref, i * wide, rms_scale(raw, gain_ref[...]))
    key_ref[...] = get_rows(pack_ref, 0, KEY_TILE).astype(jnp.bfloat16)
    for f in range(2):
        for i in range(TILE_ROWS):
            put_rows(coarse_ref, (f * TILE_ROWS + i) * 24, one_ref[f, i].astype(jnp.float32))

        def copy_fine(i, carry):
            put_rows(fine_ref, pl.multiple_of((f * FINE_ROWS + i) * FINE_COLS, 8), two_ref[f, i].astype(jnp.float32))
            return carry

        lax.fori_loop(0, FINE_ROWS, copy_fine, 0)
    near = 3 * TILE_ROWS
    fine = 2 * FINE_ROWS
    for ref in (right_ref, left_ref, right_far_ref, left_far_ref):
        ref[...] = jnp.zeros_like(ref)
    last = get_rows(coarse_ref, wide - 1, near, 24).astype(jnp.bfloat16)
    first = get_rows(coarse_ref, 0, near, 24).astype(jnp.bfloat16)
    right_ref[0:near, :] = last
    right_ref[NEAR : NEAR + near, :] = get_rows(coarse_ref, jnp.maximum(wide - 2, 0), near, 24).astype(jnp.bfloat16)
    right_ref[2 * NEAR : 2 * NEAR + fine, :] = get_rows(fine_ref, 2 * wide - 1, fine, FINE_COLS).astype(jnp.bfloat16)
    left_ref[0:near, :] = first
    left_ref[NEAR : NEAR + near, :] = get_rows(coarse_ref, 1, near, 24).astype(jnp.bfloat16)
    left_ref[2 * NEAR : 2 * NEAR + fine, :] = get_rows(fine_ref, 0, fine, FINE_COLS).astype(jnp.bfloat16)
    right_far_ref[0:near, :] = last
    left_far_ref[0:near, :] = first


def columns_kernel(
    place_ref, row_ref, col_ref, token_ref, one_ref, two_ref, from_left_ref, from_right_ref, from_left_far_ref, from_right_far_ref,
    mine_ref, other_ref, prior_ref, fine_out_ref, down_ref, up_ref, down_far_ref, up_far_ref, coarse_ref, fine_ref, half_ref,
):
    core = place_ref[2]
    tall = row_ref[place_ref[0]]
    wide = col_ref[place_ref[1]]
    left_wide = size_at(col_ref, place_ref[1] - 1)
    right_wide = size_at(col_ref, place_ref[1] + 1)
    near = 3 * TILE_ROWS
    fine = 2 * FINE_ROWS
    blank = jnp.zeros((near, 384), jnp.float32)
    put_strided(coarse_ref, EXT_COLS - 2, EXT_COLS, blank)
    put_strided(coarse_ref, EXT_COLS - 1, EXT_COLS, blank)
    for f in range(3):
        for i in range(TILE_ROWS):
            row = one_ref[f, i] if f < 2 else token_ref[i]
            put_rows(coarse_ref, (f * TILE_ROWS + i) * EXT_COLS + HALO, row.astype(jnp.float32))
    left_two = jnp.where(left_wide >= 2, from_left_ref[NEAR : NEAR + near, :], from_left_far_ref[0:near, :])
    right_two = jnp.where(right_wide >= 2, from_right_ref[NEAR : NEAR + near, :], from_right_far_ref[0:near, :])
    put_strided(coarse_ref, 0, EXT_COLS, left_two.astype(jnp.float32))
    put_strided(coarse_ref, 1, EXT_COLS, from_left_ref[0:near, :].astype(jnp.float32))
    put_strided(coarse_ref, wide + 2, EXT_COLS, from_right_ref[0:near, :].astype(jnp.float32))
    put_strided(coarse_ref, wide + 3, EXT_COLS, right_two.astype(jnp.float32))
    for side, ref in ((core, mine_ref), (1 - core, other_ref)):
        for i in range(TILE_ROWS):
            put_rows(half_ref, i * HALF, get_rows(coarse_ref, (2 * TILE_ROWS + i) * EXT_COLS + side * HALF, HALF))
        half_ref[:, TILE_ROWS * HALF : TALL_TILE, :] = jnp.zeros((3, TALL_TILE - TILE_ROWS * HALF, 128), jnp.float32)
        ref[...] = get_rows(half_ref, 0, TALL_TILE).astype(jnp.bfloat16)
    for i in range(2 * TILE_ROWS):
        prior_ref[i] = get_rows(coarse_ref, i * EXT_COLS, EXT_COLS).astype(jnp.bfloat16)
    for c in range(FINE_COLS + 1, FINE_PITCH):
        put_strided(fine_ref, c, FINE_PITCH, jnp.zeros((fine, 384), jnp.float32))
    for f in range(2):

        def copy_fine(i, carry):
            put_rows(fine_ref, (f * FINE_ROWS + i) * FINE_PITCH + 1, two_ref[f, i].astype(jnp.float32))
            return carry

        lax.fori_loop(0, FINE_ROWS, copy_fine, 0)
    put_strided(fine_ref, 0, FINE_PITCH, from_left_ref[2 * NEAR : 2 * NEAR + fine, :].astype(jnp.float32))
    put_strided(fine_ref, 2 * wide + 1, FINE_PITCH, from_right_ref[2 * NEAR : 2 * NEAR + fine, :].astype(jnp.float32))

    def write_fine(i, carry):
        fine_out_ref[i] = get_rows(fine_ref, pl.multiple_of(i * FINE_PITCH, 8), FINE_PITCH).astype(jnp.bfloat16)
        return carry

    lax.fori_loop(0, fine, write_fine, 0)
    for f in range(2):
        base = f * TILE_ROWS
        last = prior_ref[base + tall - 1]
        down_ref[f] = last
        down_ref[2 + f] = prior_ref[base + jnp.maximum(tall - 2, 0)]
        down_far_ref[f] = last
        up_ref[f] = prior_ref[base]
        up_ref[2 + f] = prior_ref[base + 1]
        up_far_ref[f] = prior_ref[base]
        bottom = fine_out_ref[f * FINE_ROWS + 2 * tall - 1]
        top = fine_out_ref[f * FINE_ROWS]
        for h in range(2):
            down_ref[4 + 2 * f + h] = bottom[h * 24 : (h + 1) * 24]
            up_ref[4 + 2 * f + h] = top[h * 24 : (h + 1) * 24]


def prior_kernel(
    place_ref, row_ref, prior_ref, fine_ref, from_up_ref, from_down_ref, from_up_far_ref, from_down_far_ref, one_ref, two_ref,
    sum_one_ref, sum_two_ref, coarse_ref, wide_ref, part_ref,
):
    tall = row_ref[place_ref[0]]
    up_tall = size_at(row_ref, place_ref[0] - 1)
    down_tall = size_at(row_ref, place_ref[0] + 1)
    for f in range(2):
        coarse_ref[f, 0] = jnp.where(up_tall >= 2, from_up_ref[2 + f], from_up_far_ref[f])
        coarse_ref[f, 1] = from_up_ref[f]
        for i in range(TILE_ROWS):
            coarse_ref[f, HALO + i] = prior_ref[f * TILE_ROWS + i]
        for i in (TILE_ROWS + 2, TILE_ROWS + 3):
            coarse_ref[f, i] = jnp.zeros((EXT_COLS, 384), jnp.bfloat16)
        coarse_ref[f, tall + 2] = from_down_ref[f]
        coarse_ref[f, tall + 3] = jnp.where(down_tall >= 2, from_down_ref[2 + f], from_down_far_ref[f])
        wide_ref[f, 0] = jnp.concatenate([from_up_ref[4 + 2 * f], from_up_ref[5 + 2 * f]], axis=0)

        def copy_fine(i, carry):
            wide_ref[f, 1 + i] = fine_ref[f * FINE_ROWS + i]
            return carry

        lax.fori_loop(0, FINE_ROWS, copy_fine, 0)
        wide_ref[f, FINE_ROWS + 1] = jnp.zeros((FINE_PITCH, 384), jnp.bfloat16)
        wide_ref[f, 2 * tall + 1] = jnp.concatenate([from_down_ref[4 + 2 * f], from_down_ref[5 + 2 * f]], axis=0)
    rows = TILE_ROWS + 2
    left = jnp.concatenate(
        [coarse_ref[f, a : a + rows].reshape(rows * EXT_COLS, 384) for f in range(2) for a in range(3)], axis=1
    )
    sum_one_ref[...] = shifted_sum(left, lambda b: jnp.concatenate([one_ref[f, a, b] for f in range(2) for a in range(3)], axis=0), part_ref, 3)
    step = 13
    for r in range(0, FINE_ROWS, step):
        left = jnp.concatenate(
            [wide_ref[f, r + a : r + a + step].reshape(step * FINE_PITCH, 384) for f in range(2) for a in range(3)], axis=1
        )
        sum_two_ref[r * FINE_PITCH : (r + step) * FINE_PITCH, :] = shifted_sum(
            left, lambda b: jnp.concatenate([two_ref[f, a, b] for f in range(2) for a in range(3)], axis=0), part_ref, 2
        )[:, 0:192]


def shifted_sum(left, weight_of, part_ref, groups):
    count = left.shape[0]
    total = jnp.dot(left, weight_of(0), preferred_element_type=jnp.float32)
    for b in (1, 2):
        product = jnp.dot(left, weight_of(b), preferred_element_type=jnp.float32)
        width = product.shape[1]
        for g in range(groups):
            hi = min((g + 1) * 128, width)
            part_ref[g, 0:count, 0 : hi - g * 128] = product[:, g * 128 : hi]
        moved = jnp.concatenate([part_ref[g, b : b + count, :] for g in range(groups)], axis=1)
        total = total + moved[:, 0:width]
    return total


def query_kernel(
    place_ref, row_ref, own_ref, one_ref, two_ref, three_ref, gain_ref, qw_ref, kw_ref, query_ref, frame_ref, wide_ref, *, scale
):
    y_at = place_ref[0] // 2
    wide_ref[...] = jnp.zeros_like(wide_ref)
    slot = lax.broadcasted_iota(jnp.int32, (TALL_TILE, 128), 0)
    for k, ref in enumerate((own_ref, one_ref, two_ref, three_ref)):
        source = jnp.bitwise_and(y_at - k, 3)
        for t in range(2):
            start = FRONT + before(row_ref, 2 * source + t) * HALF
            usable = slot < row_ref[2 * source + t] * HALF
            part = ref[t].astype(jnp.float32)
            for g in range(3):
                held = wide_ref[g, pl.ds(start, TALL_TILE), :]
                wide_ref[g, pl.ds(start, TALL_TILE), :] = jnp.where(usable, part[:, g * 128 : (g + 1) * 128], held)
    count = LAT_ROWS * HALF
    frame_ref[...] = get_rows(wide_ref, before(row_ref, 2 * y_at) * HALF, BLOCK_ROWS).astype(jnp.bfloat16)
    for i in range(count // QUERY_BLOCK):
        raw = get_rows(wide_ref, FRONT + i * QUERY_BLOCK, QUERY_BLOCK)
        normed = rms_scale(raw, gain_ref[...]).astype(jnp.bfloat16)
        query = jnp.dot(normed, qw_ref[...], preferred_element_type=jnp.float32).astype(jnp.bfloat16)
        turned = lax.dot_general(query, kw_ref[...], (((1,), (1,)), ((), ())), preferred_element_type=jnp.float32)
        query_ref[i * QUERY_BLOCK : (i + 1) * QUERY_BLOCK, :] = (turned * scale).astype(jnp.bfloat16)


def attention_kernel(
    place_ref, row_ref, col_ref, query_ref, tile_ref, out_ref,
    key_ref, bias_ref, score_ref, top_ref, sum_ref, acc_ref, wide_ref, stat_ref,
):
    tiles = tile_ref.shape[0]
    cols = col_ref.shape[0]
    y_at = place_ref[0] // 2
    spot = lax.broadcasted_iota(jnp.int32, (16, KEY_CHUNK), 0) * KEY_CHUNK + lax.broadcasted_iota(jnp.int32, (16, KEY_CHUNK), 1)

    def gather(t, carry):
        offset, bias = carry
        offset = pl.multiple_of(offset, 16)
        key_ref[pl.ds(offset, KEY_TILE), :] = tile_ref[t]
        count = row_ref[2 * y_at + t // cols] * col_ref[t % cols]
        bias = jnp.where((spot >= offset) & (spot < offset + count), 0.0, bias)
        return offset + (count + 15) // 16 * 16, bias

    tail, bias = lax.fori_loop(0, tiles, gather, (jnp.int32(0), jnp.full((16, KEY_CHUNK), masked_score, jnp.float32)))
    tail = pl.multiple_of(tail, 16)
    key_ref[pl.ds(tail, KEY_CHUNK), :] = jnp.zeros((KEY_CHUNK, key_ref.shape[1]), jnp.bfloat16)
    for j in range(MAX_CHUNKS):
        bias_ref[j] = bias[j : j + 1, :]
    chunk_count = (tail + KEY_CHUNK - 1) // KEY_CHUNK
    total = wide_ref.shape[1]
    count = query_ref.shape[0]
    wide_ref[:, 0:FRONT, :] = jnp.zeros((3, FRONT, 128), jnp.float32)
    wide_ref[:, FRONT + count : total, :] = jnp.zeros((3, total - FRONT - count, 128), jnp.float32)
    stat_ref[0:FRONT, :] = jnp.zeros((FRONT, 128), jnp.float32)
    stat_ref[FRONT + count : total, :] = jnp.zeros((total - FRONT - count, 128), jnp.float32)
    blocks = count // QUERY_BLOCK
    lane_groups = KEY_CHUNK // 128

    def keys_at(j):
        return key_ref[pl.ds(pl.multiple_of(j * KEY_CHUNK, KEY_CHUNK), KEY_CHUNK), :]

    def score_step(i, j):
        slot = i % 2
        query = query_ref[i * QUERY_BLOCK : (i + 1) * QUERY_BLOCK, :]
        s = lax.dot_general(query, keys_at(j), (((1,), (1,)), ((), ())), preferred_element_type=jnp.float32)
        s = s + bias_ref[j]
        score_ref[slot, j] = s
        best = s[:, 0:128]
        for g in range(1, lane_groups):
            best = jnp.maximum(best, s[:, g * 128 : (g + 1) * 128])
        top_ref[slot] = jnp.maximum(top_ref[slot], best)

    def value_step(i, j):
        slot = i % 2
        top = top_ref[slot]
        p = jnp.exp2(score_ref[slot, j] - jnp.concatenate([top] * lane_groups, axis=1))
        part = p[:, 0:128]
        for g in range(1, lane_groups):
            part = part + p[:, g * 128 : (g + 1) * 128]
        sum_ref[...] = sum_ref[...] + part
        acc_ref[...] = acc_ref[...] + jnp.dot(p.astype(jnp.bfloat16), keys_at(j), preferred_element_type=jnp.float32)

    for i in range(blocks + 1):
        if i < blocks:
            top_ref[i % 2] = jnp.full((QUERY_BLOCK, 128), masked_score, jnp.float32)
        if i > 0:
            last = (i - 1) % 2
            best = jnp.max(top_ref[last], axis=1, keepdims=True)
            top_ref[last] = jnp.broadcast_to(best, (QUERY_BLOCK, 128))
            sum_ref[...] = jnp.zeros_like(sum_ref)
            acc_ref[...] = jnp.zeros_like(acc_ref)

        def step(j, carry):
            if i < blocks:
                score_step(i, j)
            if i > 0:
                value_step(i - 1, j)
            return carry

        lax.fori_loop(0, chunk_count, step, 0)
        if i > 0:
            denominator = jnp.sum(sum_ref[...], axis=1, keepdims=True)
            lo = FRONT + (i - 1) * QUERY_BLOCK
            put_rows(wide_ref, lo, acc_ref[...] / denominator)
            level = top_ref[(i - 1) % 2] + jnp.log2(jnp.broadcast_to(denominator, (QUERY_BLOCK, 128)))
            high = level.astype(jnp.bfloat16).astype(jnp.float32)
            mid = (level - high).astype(jnp.bfloat16).astype(jnp.float32)
            low = level - high - mid
            lane = lax.broadcasted_iota(jnp.int32, (QUERY_BLOCK, 128), 1)
            packed = jnp.where(lane == 0, high, jnp.where(lane == 1, mid, jnp.where(lane == 2, low, 0.0)))
            stat_ref[lo : lo + QUERY_BLOCK, :] = packed
    select = (
        lax.broadcasted_iota(jnp.int32, (16, 128), 0) == lax.broadcasted_iota(jnp.int32, (16, 128), 1)
    ).astype(jnp.bfloat16)
    for b in range(out_ref.shape[0]):
        offset = before(row_ref, 2 * b) * HALF
        out_ref[b, 0 : BLOCK_ROWS - 16, :] = get_rows(wide_ref, offset, BLOCK_ROWS - 16).astype(jnp.bfloat16)
        levels = stat_ref[pl.ds(offset, BLOCK_ROWS), :].astype(jnp.bfloat16)
        out_ref[b, BLOCK_ROWS - 16 : BLOCK_ROWS, :] = lax.dot_general(
            select, levels, (((1,), (1,)), ((), ())), preferred_element_type=jnp.float32
        ).astype(jnp.bfloat16)


def merge_kernel(
    place_ref, row_ref, col_ref, part_ref, frame_ref, vw_ref, ow_ref, gain_ref, mine_ref, other_ref, wide_ref
):
    groups = part_ref.shape[0]
    core = place_ref[2]
    y_at = place_ref[0] // 2
    ones = (lax.broadcasted_iota(jnp.int32, (16, 128), 0) < 3).astype(jnp.bfloat16)
    levels = [
        lax.dot_general(
            part_ref[g, BLOCK_ROWS - 16 : BLOCK_ROWS, :], ones, (((0,), (0,)), ((), ())), preferred_element_type=jnp.float32
        )
        for g in range(groups)
    ]
    best = levels[0]
    for g in range(1, groups):
        best = jnp.maximum(best, levels[g])
    weights = [jnp.exp2(level - best) for level in levels]
    total = weights[0]
    for g in range(1, groups):
        total = total + weights[g]
    merged = None
    for g in range(groups):
        share = weights[g] / total
        term = part_ref[g].astype(jnp.float32) * jnp.concatenate([share] * 3, axis=1)
        merged = term if merged is None else merged + term
    merged = merged.astype(jnp.bfloat16)
    attention = jnp.dot(merged, vw_ref[...], preferred_element_type=jnp.float32).astype(jnp.bfloat16)
    projected = jnp.dot(attention, ow_ref[...], preferred_element_type=jnp.float32)
    mixed = (frame_ref[...].astype(jnp.float32) + projected).astype(jnp.bfloat16)
    act = silu(rms_scale(mixed, gain_ref[...]))
    slot = lax.broadcasted_iota(jnp.int32, (BLOCK_ROWS, 128), 0)
    row = jnp.right_shift(slot * 43691, 19)
    at_row = before(row_ref, 2 * y_at) - HALO + row
    at_col = before(col_ref, place_ref[1]) - HALO + slot - row * HALF + core * HALF
    inside = (at_row >= 0) & (at_row < LAT_ROWS) & (at_col >= 0) & (at_col < LAT_COLS)
    for g in range(3):
        wide_ref[g] = jnp.where(inside, act[:, g * 128 : (g + 1) * 128], 0.0)
    upper = row_ref[2 * y_at] * HALF
    mine_ref[...] = get_rows(wide_ref, core * upper, HALF_ROWS).astype(jnp.bfloat16)
    other_ref[...] = get_rows(wide_ref, (1 - core) * upper, HALF_ROWS).astype(jnp.bfloat16)


def tail_kernel(
    place_ref, row_ref, col_ref, mine_ref, other_ref, sum_one_ref, sum_two_ref, one_ref, two_ref, gain_ref, out_ref,
    half_ref, act_ref, first_ref, up_ref, fine_ref, part_ref,
):
    core = place_ref[2]
    tall = row_ref[place_ref[0]]
    wide = col_ref[place_ref[1]]
    for side, ref in ((core, mine_ref), (1 - core, other_ref)):
        put_rows(half_ref, 0, ref[...].astype(jnp.float32))
        for i in range(EXT_ROWS):
            put_rows(act_ref, i * EXT_COLS + side * HALF, get_rows(half_ref, i * HALF, HALF))
    for i in range(EXT_ROWS):
        first_ref[i] = get_rows(act_ref, i * EXT_COLS, EXT_COLS).astype(jnp.bfloat16)
    rows = TILE_ROWS + 2
    left = jnp.concatenate([first_ref[a : a + rows].reshape(rows * EXT_COLS, 384) for a in range(3)], axis=1)
    total = shifted_sum(left, lambda b: jnp.concatenate([one_ref[0, a, b] for a in range(3)], axis=0), part_ref, 3)
    y_one = (total + sum_one_ref[...]).astype(jnp.bfloat16)
    act = silu(rms_scale(y_one, gain_ref[...])).astype(jnp.bfloat16).astype(jnp.float32)
    slot = lax.broadcasted_iota(jnp.int32, (rows * EXT_COLS, 128), 0)
    row = jnp.right_shift(slot * 43691, 20)
    at_row = before(row_ref, place_ref[0]) - 1 + row
    at_col = before(col_ref, place_ref[1]) - 1 + slot - row * EXT_COLS
    inside = (at_row >= 0) & (at_row < LAT_ROWS) & (at_col >= 0) & (at_col < LAT_COLS)
    for g in range(3):
        act_ref[g, 0 : rows * EXT_COLS, :] = jnp.where(inside, act[:, g * 128 : (g + 1) * 128], 0.0)
    for i in range(rows):
        small = get_rows(act_ref, i * EXT_COLS, EXT_COLS)
        put_strided(up_ref, 7, 2, small)
        put_strided(up_ref, 8, 2, small)
        fine = get_rows(up_ref, 8, FINE_PITCH).astype(jnp.bfloat16)
        for f in (2 * i - 1, 2 * i):
            if 0 <= f < FINE_ROWS + 2:
                fine_ref[f] = fine
    step = 13
    col = lax.broadcasted_iota(jnp.int32, (FINE_COLS, 192), 0)
    for r in range(0, FINE_ROWS, step):
        left = jnp.concatenate([fine_ref[r + a : r + a + step].reshape(step * FINE_PITCH, 384) for a in range(3)], axis=1)
        y_two = shifted_sum(left, lambda b: jnp.concatenate([two_ref[0, a, b] for a in range(3)], axis=0), part_ref, 2)[:, 0:192]
        y_two = y_two + sum_two_ref[r * FINE_PITCH : (r + step) * FINE_PITCH, :]
        for i in range(step):
            line = y_two[i * FINE_PITCH : i * FINE_PITCH + FINE_COLS, :]
            usable = (col < 2 * wide) & (r + i < 2 * tall)
            out_ref[r + i] = jnp.where(usable, line, 0.0).astype(jnp.bfloat16)


def call(body, inputs, outs, scratch, smem_count, name, flops=0):
    smem = pl.BlockSpec(memory_space=pltpu.SMEM)
    vmem = pl.BlockSpec(memory_space=pltpu.VMEM)
    moved = sum(math.prod(v.shape) * v.dtype.itemsize for v in list(inputs) + list(outs))
    return pl.pallas_call(
        body,
        in_specs=[smem] * smem_count + [vmem] * (len(inputs) - smem_count),
        out_specs=[vmem] * len(outs),
        out_shape=outs,
        scratch_shapes=scratch,
        compiler_params=pltpu.CompilerParams(vmem_limit_bytes=VMEM_BYTES),
        cost_estimate=pl.CostEstimate(flops=int(flops), transcendentals=0, bytes_accessed=int(moved)),
        name=name,
    )(*inputs)


def local(
    tokens, row_sizes, col_sizes, norm_gain, query_weight, key_weight, value_weight, out_weight,
    cache_one, gain_one, conv_one, cache_two, gain_two, conv_two,
):
    channels = tokens.shape[2]
    n_row = row_sizes.shape[0]
    n_col = col_sizes.shape[0]
    n_y = lax.axis_size("y")
    core = lax.axis_index("core")
    row_at = lax.axis_index("y") * lax.axis_size("core") + core
    col_at = lax.axis_index("x") * lax.axis_size("z") + lax.axis_index("z")
    place = jnp.stack([row_at, col_at, core]).astype(jnp.int32)
    shape = lambda *dims: jax.ShapeDtypeStruct(dims, jnp.bfloat16)
    wide_shape = lambda *dims: jax.ShapeDtypeStruct(dims, jnp.float32)
    scratch = lambda *dims: pltpu.VMEM(dims, jnp.float32)
    narrow = lambda *dims: pltpu.VMEM(dims, jnp.bfloat16)
    message = 160
    own_keys, to_right, to_left, to_right_far, to_left_far = call(
        prepare_kernel,
        [place, row_sizes, col_sizes, tokens, cache_one, cache_two, norm_gain[None]],
        [shape(KEY_TILE, channels), shape(message, channels), shape(message, channels), shape(NEAR, channels), shape(NEAR, channels)],
        [scratch(3, 304, 128), scratch(3, 3 * TILE_ROWS * 24, 128), scratch(3, 2 * FINE_ROWS * FINE_COLS, 128)],
        3, "prepare",
    )
    tiles = lax.all_gather(own_keys, ("core", "x", "z"), axis=0, tiled=False)
    from_left = hop(to_right, COLS, n_col, 1)
    from_right = hop(to_left, COLS, n_col, -1)
    from_left_far = hop(to_right_far, COLS, n_col, 2)
    from_right_far = hop(to_left_far, COLS, n_col, -2)
    mine, other, prior, fine, down, up, down_far, up_far = call(
        columns_kernel,
        [place, row_sizes, col_sizes, tokens, cache_one, cache_two, from_left, from_right, from_left_far, from_right_far],
        [
            shape(TALL_TILE, channels), shape(TALL_TILE, channels), shape(2 * TILE_ROWS, EXT_COLS, channels),
            shape(2 * FINE_ROWS, FINE_PITCH, channels), shape(8, EXT_COLS, channels), shape(8, EXT_COLS, channels),
            shape(2, EXT_COLS, channels), shape(2, EXT_COLS, channels),
        ],
        [scratch(3, 3 * TILE_ROWS * EXT_COLS, 128), scratch(3, 2 * FINE_ROWS * FINE_PITCH, 128), scratch(3, TALL_TILE, 128)],
        3, "columns",
    )
    swap = [(0, 1), (1, 0)]
    sibling = lax.ppermute(other, "core", swap)
    pair = jnp.where(core == 0, jnp.stack([mine, sibling]), jnp.stack([sibling, mine]))
    strips = [pair] + [lax.ppermute(pair, "y", [(i, (i + k) % n_y) for i in range(n_y)]) for k in range(1, n_y)]
    scale = math.log2(math.e) / math.sqrt(channels)

    def query_body(*refs):
        query_kernel(*refs, scale=scale)

    queries, frame = call(
        query_body,
        [place, row_sizes, *strips, norm_gain[None], query_weight, key_weight],
        [shape(LAT_ROWS * HALF, channels), shape(BLOCK_ROWS, channels)],
        [scratch(3, WIDE_ROWS, 128)],
        2, "queries", 4 * LAT_ROWS * HALF * channels * channels,
    )
    from_up = hop(down, ROWS, n_row, 1)
    from_down = hop(up, ROWS, n_row, -1)
    from_up_far = hop(down_far, ROWS, n_row, 2)
    from_down_far = hop(up_far, ROWS, n_row, -2)
    (parts,) = call(
        attention_kernel,
        [place, row_sizes, col_sizes, queries, tiles.reshape(2 * n_col, KEY_TILE, channels)],
        [shape(n_y, BLOCK_ROWS, channels)],
        [
            narrow(KEY_ROWS, channels), scratch(MAX_CHUNKS, 1, KEY_CHUNK), scratch(2, MAX_CHUNKS, QUERY_BLOCK, KEY_CHUNK),
            scratch(2, QUERY_BLOCK, 128), scratch(QUERY_BLOCK, 128), scratch(QUERY_BLOCK, channels),
            scratch(3, WIDE_ROWS, 128), scratch(WIDE_ROWS, 128),
        ],
        3, "attention", 4 * LAT_ROWS * HALF * channels * KEY_ROWS,
    )
    parts = lax.all_to_all(parts, "y", 0, 0)
    sum_one, sum_two = call(
        prior_kernel,
        [place, row_sizes, prior, fine, from_up, from_down, from_up_far, from_down_far, conv_one[:2], conv_two[:2]],
        [wide_shape((TILE_ROWS + 2) * EXT_COLS, channels), wide_shape(FINE_ROWS * FINE_PITCH, conv_two.shape[-1])],
        [narrow(2, EXT_ROWS, EXT_COLS, channels), narrow(2, FINE_ROWS + 2, FINE_PITCH, channels), scratch(3, 640, 128)],
        2, "prior", 2 * 18 * channels * (360 * 384 + 1248 * 192),
    )
    half_mine, half_other = call(
        merge_kernel,
        [place, row_sizes, col_sizes, parts, frame, value_weight, out_weight, gain_one[None]],
        [shape(HALF_ROWS, channels), shape(HALF_ROWS, channels)],
        [scratch(3, BLOCK_ROWS, 128)],
        3, "merge",
    )
    half_other = lax.ppermute(half_other, "core", swap)
    (decoded,) = call(
        tail_kernel,
        [place, row_sizes, col_sizes, half_mine, half_other, sum_one, sum_two, conv_one[2:], conv_two[2:], gain_two[None]],
        [shape(FINE_ROWS, FINE_COLS, conv_two.shape[-1])],
        [
            scratch(3, HALF_ROWS, 128), scratch(3, EXT_ROWS * EXT_COLS, 128), narrow(EXT_ROWS, EXT_COLS, channels),
            scratch(3, 64, 128), narrow(FINE_ROWS + 2, FINE_PITCH, channels), scratch(3, 640, 128),
        ],
        3, "tail",
    )
    return decoded


def solution(mesh):
    grid = Mesh(mesh.devices.reshape(4, 2, 4, 4), ("y", "core", "x", "z"))
    placed = (
        P(ROWS, COLS, None), P(), P(), P(), P(), P(), P(), P(),
        P(None, ROWS, COLS, None), P(), P(), P(None, ROWS, COLS, None), P(), P(),
    )
    return jax.shard_map(local, mesh=grid, in_specs=placed, out_specs=P(ROWS, COLS, None), check_vma=False)
```

time: 190 us -> 170 us (0.89); the launches traced: 186 us -> 169 us
  Pallas kernels: 37.2 us -> 69.3 us
  matrix products: 23.8 us -> 0 us
  waiting for transfers between devices: 3.04 us -> 21.2 us
  other arithmetic: 17 us -> 1.68 us
  between operations: 26.4 us -> 13.6 us
  blocking collectives: 12.3 us -> 0 us
  local copies, waits for them, and re-layouts: 29.6 us -> 26.7 us
    pallas_call x3 -> x7, Pallas kernels: 37.2 us -> 69.3 us  [call(): pl.pallas_call(body, in_specs=[smem] * smem_count + [vmem] * (len(inputs)...]
    conv_general_dilated x6 -> x0, matrix products: 22.9 us -> none  [conv(): lax.conv_general_dilated(frames[t][None], kernel[t], (1, 1), 'VALID', dim...]
    all_gather x1 -> x0, blocking collectives: 12.3 us -> none  [local(): lax.all_gather(two.reshape(2 * tall_tile, channels), 'y', axis=0, tiled=T...]
    ppermute x2 -> x5, waiting for transfers between devices: 0.01 us -> 11.1 us  [the longest x3 9.91 us: local(): lax.ppermute(pair, 'y', [(i, (i + k) % n_y) for i in range(n_y)])]
    unnamed x37 -> x43, local copies, waits for them, and re-layouts: 2.99 us -> 13.8 us
    ppermute x8, waiting for transfers between devices: 0.02 us -> 5.86 us  [hop(): return lax.ppermute(value, axes, pairs)]
    concatenate x12 -> x0, other arithmetic: 5.43 us -> none  [the longest x1 2.32 us: local(): jnp.concatenate([fine_line(from_left[2 * near:]), cache_two, fine_line(jn...]
    conv_general_dilated x15 -> x0, local copies, waits for them, and re-layouts: 4.71 us -> none  [conv(): lax.conv_general_dilated(frames[t][None], kernel[t], (1, 1), 'VALID', dim...]
  transfers between devices with their start and end apart: 12 -> 15, of which waited for: 1 -> 6; matrix products, arithmetic and copies ran while one was open for 23% -> 12% of each run, Pallas kernels for 2% -> 15%
where the time goes in v2:
time: 170 us; the launch traced here: 169 us
  Pallas kernels  69.3 us (41%)
  starting transfers between devices  36.3 us (21%)
  local copies, waits for them, and re-layouts  26.7 us (16%)
  waiting for transfers between devices  21.2 us (12%)
  between operations  13.6 us (8%)
    pallas_call x7, Pallas kernels, call(): pl.pallas_call(body, in_specs=[smem] * smem_count + [vmem] * (len(inputs)...  69.3 us
    ppermute x8, starting transfers between devices, hop(): return lax.ppermute(value, axes, pairs)  23.5 us
    unnamed x43, local copies, waits for them, and re-layouts  13.8 us
    ppermute x3, waiting for transfers between devices, local(): lax.ppermute(pair, 'y', [(i, (i + k) % n_y) for i in range(n_y)])  9.91 us
    ppermute x8, waiting for transfers between devices, hop(): return lax.ppermute(value, axes, pairs)  5.86 us
    all_to_all x1, starting transfers between devices, local(): parts = lax.all_to_all(parts, 'y', 0, 0)  5.69 us
    slice x1, local copies, waits for them, and re-layouts, local(): conv_one[:2]  5.61 us
    ppermute x3, starting transfers between devices, local(): lax.ppermute(pair, 'y', [(i, (i + k) % n_y) for i in range(n_y)])  5.05 us
  transfers between devices with their start and end apart: 15, of which 6 were waited for; matrix products, arithmetic and copies ran while one was open for 12% of the time, Pallas kernels for 15%

profile of v2, /device:TPU:1, one launch (start us, length us, event | category | flops | bytes accessed | tf_op | source)
XLA Modules:
  0.0 168.8 jit_solution(11317582205564154567)
XLA Ops:
  6.5 1.8 %copy.16.one_ref = bf16[2,13,20,384]{3,2,1,0:T(8,128)(2,1)} copy(bf16[2,13,20,384]{3,0,2,1:T(2,128)(2,1)} %param.22) | data formatting | bytes 798720 | tf_op args[8]
  10.3 3.2 %prepare.1 = (bf16[272,384]{1,0:T(8,128)(2,1)}, bf16[160,384]{1,0:T(8,128)(2,1)}, bf16[160,384]{1,0:T(8,128)(2,1)}, bf16[48,384]{1,0:T(8,128)(2,1)}, bf16[48,384]{1,0:T(8,128)(2,1)}) custom-call(s32[3]{0:T(128)} %pad_add_fusion.place_ref.refs_0_, s32[8]{0:T(128)} %row_ref.11, s32[16]{0:T(128)} %col_ref.9, bf16[13,20,384]{2,1,0:T(8,128)(2,1)} %token_ref.3, ...), custom_call_target="tpu_custom_call" | custom-call | bytes 2726508 | tf_op jit(solution)/shard_map/prepare/pallas_call | solution.py:448
  13.5 4.4 %collective-permute-start = (bf16[160,384]{1,0:T(8,128)(2,1)}, bf16[160,384]{1,0:T(8,128)(2,1)S(1)}, u32[]{:S(2)}, u32[]{:S(2)}) collective-permute-start(bf16[160,384]{1,0:T(8,128)(2,1)} %get-tuple-element.24), channel_id=1, source_target_pairs={{0,1},{1,2},{2,3},{3,4},{4,5},{5,6},{6,7},{7,8},{8,9},{9,10},{10,1... | collective-permute-start | bytes 368648 | tf_op jit(solution)/shard_map/ppermute | solution.py:51
  19.2 5.9 %collective-permute-start.2 = (bf16[48,384]{1,0:T(8,128)(2,1)}, bf16[48,384]{1,0:T(8,128)(2,1)S(1)}, u32[]{:S(2)}, u32[]{:S(2)}) collective-permute-start(bf16[48,384]{1,0:T(8,128)(2,1)} %get-tuple-element.26), channel_id=1, source_target_pairs={{0,2},{1,3},{2,4},{3,5},{4,6},{5,7},{6,8},{7,9},{8,10},{9,11},{10,... | collective-permute-start | bytes 110600 | tf_op jit(solution)/shard_map/ppermute | solution.py:51
  26.5 5.8 %collective-permute-done.3.from_right_far_ref = bf16[48,384]{1,0:T(8,128)(2,1)S(1)} collective-permute-done((bf16[48,384]{1,0:T(8,128)(2,1)}, bf16[48,384]{1,0:T(8,128)(2,1)S(1)}, u32[]{:S(2)}, u32[]{:S(2)}) %collective-permute-start.3) | collective-permute-done | bytes 36896 | tf_op jit(solution)/shard_map/ppermute | solution.py:51
  33.6 4.9 %columns.1 = (bf16[160,384]{1,0:T(8,128)(2,1)}, bf16[160,384]{1,0:T(8,128)(2,1)}, bf16[26,24,384]{2,1,0:T(8,128)(2,1)}, bf16[52,48,384]{2,1,0:T(8,128)(2,1)}, bf...) custom-call(s32[3]{0:T(128)} %pad_add_fusion.place_ref.refs_0_, ...), custom_call_target="tpu_custom_call" | custom-call | bytes 5526636 | tf_op jit(solution)/shard_map/columns/pallas_call | solution.py:448
  38.5 2.0 %collective-permute-start.4 = (bf16[160,384]{1,0:T(8,128)(2,1)}, bf16[160,384]{1,0:T(8,128)(2,1)S(1)}, u32[]{:S(2)}, u32[]{:S(2)}) collective-permute-start(bf16[160,384]{1,0:T(8,128)(2,1)} %get-tuple-element.29), channel_id=1, source_target_pairs={{0,16},{16,0},{1,17},{17,1},{2,18},{18,2},{3,19},{19,3},{4,20},{20... | collective-permute-start | bytes 368648 | tf_op jit(solution)/shard_map/ppermute | solution.py:501
  44.1 2.6 %collective-permute-start.6 = (bf16[2,160,384]{2,1,0:T(8,128)(2,1)S(1)}, bf16[2,160,384]{2,1,0:T(8,128)(2,1)S(1)}, u32[]{:S(2)}, u32[]{:S(2)}) collective-permute-start(bf16[2,160,384]{2,1,0:T(8,128)(2,1)S(1)} %maximum_select_fusion.refs_2_), channel_id=1, source_target_pairs={{0,64},{32,96},{64,0},{96,32},{1,65},{33,97},{65,1},{97,33},{2,66}... | collective-permute-start | bytes 737288 | tf_op jit(solution)/shard_map/ppermute | solution.py:503
  47.8 3.5 %collective-permute-done.5.refs_3_ = bf16[2,160,384]{2,1,0:T(8,128)(2,1)S(1)} collective-permute-done((bf16[2,160,384]{2,1,0:T(8,128)(2,1)S(1)}, bf16[2,160,384]{2,1,0:T(8,128)(2,1)S(1)}, u32[]{:S(2)}, u32[]{:S(2)}) %collective-permute-start.5) | collective-permute-done | bytes 245792 | tf_op jit(solution)/shard_map/ppermute | solution.py:503
  51.3 6.4 %collective-permute-done.6.refs_4_ = bf16[2,160,384]{2,1,0:T(8,128)(2,1)S(1)} collective-permute-done((bf16[2,160,384]{2,1,0:T(8,128)(2,1)S(1)}, bf16[2,160,384]{2,1,0:T(8,128)(2,1)S(1)}, u32[]{:S(2)}, u32[]{:S(2)}) %collective-permute-start.6) | collective-permute-done | bytes 245792 | tf_op jit(solution)/shard_map/ppermute | solution.py:503
  59.1 4.3 %queries.1 = (bf16[1056,384]{1,0:T(8,128)(2,1)}, bf16[384,384]{1,0:T(8,128)(2,1)}) custom-call(s32[3]{0:T(128)} %pad_add_fusion.place_ref.refs_0_, s32[8]{0:T(128)} %row_ref.11, bf16[2,160,384]{2,1,0:T(8,128)(2,1)} %copy-done.1, bf16[2,160,384]{2,1,0:T(8,128)(2,1)} %copy-done.9, bf16[2,160,384]{2,1,0:T(8,128)(2,1)} %copy-done.10, ...), custom_call_target="tpu_custom_call" | custom-call | flops 622854144 | bytes 2680364 | tf_op jit(solution)/shard_map/queries/pallas_call | solution.py:448
  63.3 4.3 %all-gather.3.cloned.1.call-done = bf16[8704,384]{1,0:T(8,128)(2,1)} async-done(((bf16[272,384]{1,0:T(8,128)(2,1)}), bf16[8704,384]{1,0:T(8,128)(2,1)}) %all-gather.3.cloned.1.call-update) | async-done | bytes 6684688 | tf_op jit(solution)/shard_map/all_gather | solution.py:484
  67.6 31.6 %attention.1 = bf16[4,384,384]{2,1,0:T(8,128)(2,1)} custom-call(s32[3]{0:T(128)} %pad_add_fusion.place_ref.refs_0_, s32[8]{0:T(128)} %row_ref.11, s32[16]{0:T(128)} %col_ref.9, bf16[1056,384]{1,0:T(8,128)(2,1)} %get-tuple-element.30.query_ref, bf16[32,272,384]{2,1,0:T(8,128)(2,1)} %bitcast.8), custom_call_target="tpu_custom_call" | custom-call | flops 12457082880 | bytes 8675436 | tf_op jit(solution)/shard_map/attention/pallas_call | solution.py:448
  99.2 5.7 %all-to-all-start = ((bf16[4,384,384]{2,1,0:T(8,128)(2,1)}), bf16[4,384,384]{2,1,0:T(8,128)(2,1)}, u32[]{:S(2)}, u32[]{:S(2)}) async-start(bf16[4,384,384]{2,1,0:T(8,128)(2,1)} %attention.1), calls=%async_computation | async-start | bytes 2359296 | tf_op jit(solution)/shard_map/all_to_all | solution.py:531
  104.9 2.4 %collective-permute-start.10 = (bf16[8,24,384]{2,1,0:T(8,128)(2,1)S(1)}, bf16[8,24,384]{2,1,0:T(8,128)(2,1)S(1)}, u32[]{:S(2)}, u32[]{:S(2)}) collective-permute-start(bf16[8,24,384]{2,1,0:T(8,128)(2,1)S(1)} %copy-done.13), channel_id=1, source_target_pairs={{16,0},{32,16},{48,32},{64,48},{80,64},{96,80},{112,96},{17,1},{33... | collective-permute-start | bytes 442376 | tf_op jit(solution)/shard_map/ppermute | solution.py:51
  107.3 3.5 %collective-permute-start.9 = (bf16[8,24,384]{2,1,0:T(8,128)(2,1)S(1)}, bf16[8,24,384]{2,1,0:T(8,128)(2,1)S(1)}, u32[]{:S(2)}, u32[]{:S(2)}) collective-permute-start(bf16[8,24,384]{2,1,0:T(8,128)(2,1)S(1)} %copy-done.12), channel_id=1, source_target_pairs={{0,16},{16,32},{32,48},{48,64},{64,80},{80,96},{96,112},{1,17},{17... | collective-permute-start | bytes 442376 | tf_op jit(solution)/shard_map/ppermute | solution.py:51
  110.9 3.1 %collective-permute-start.11 = (bf16[2,24,384]{2,1,0:T(8,128)(2,1)S(1)}, bf16[2,24,384]{2,1,0:T(8,128)(2,1)S(1)}, u32[]{:S(2)}, u32[]{:S(2)}) collective-permute-start(bf16[2,24,384]{2,1,0:T(8,128)(2,1)S(1)} %copy-done.17), channel_id=1, source_target_pairs={{0,32},{16,48},{32,64},{48,80},{64,96},{80,112},{1,33},{17,49},{33... | collective-permute-start | bytes 110600 | tf_op jit(solution)/shard_map/ppermute | solution.py:51
  117.4 5.6 %slice.12.one_ref = bf16[2,3,3,384,384]{4,3,2,1,0:T(8,128)(2,1)} slice(bf16[3,3,3,384,384]{4,3,2,1,0:T(8,128)(2,1)} %param.24), slice={[0:2], [0:3], [0:3], [0:384], [0:384]} | slice | bytes 10616832 | tf_op jit(solution)/shard_map/slice | solution.py:534
  123.0 3.7 %slice.14.one_ref = bf16[1,3,3,384,384]{4,3,2,1,0:T(8,128)(2,1)} slice(bf16[3,3,3,384,384]{4,3,2,1,0:T(8,128)(2,1)} %param.24), slice={[2:3], [0:3], [0:3], [0:384], [0:384]} | slice | bytes 5308416 | tf_op jit(solution)/shard_map/slice | solution.py:549
  126.6 3.7 %copy.19.two_ref = bf16[2,3,3,384,192]{4,3,2,1,0:T(8,128)(2,1)} copy(bf16[2,3,3,384,192]{3,4,2,1,0:T(8,128)(2,1)S(1)} %slice-done) | data formatting | bytes 5308416
  130.9 3.6 %copy.20.two_ref = bf16[1,3,3,384,192]{4,3,2,1,0:T(8,128)(2,1)} copy(bf16[1,3,3,384,192]{3,4,2,1,0:T(8,128)(2,1)} %slice.15) | data formatting | bytes 2654208
  135.1 3.5 %merge.1 = (bf16[208,384]{1,0:T(8,128)(2,1)}, bf16[208,384]{1,0:T(8,128)(2,1)}) custom-call(s32[3]{0:T(128)} %pad_add_fusion.place_ref.refs_0_, s32[8]{0:T(128)} %row_ref.11, s32[16]{0:T(128)} %col_ref.9, bf16[4,384,384]{2,1,0:T(8,128)(2,1)} %all-to-all-done.part_ref, bf16[384,384]{1,0:T(8,128)(2,1)} %get-tuple-element.32.frame_ref, ...), custom_call_target="tpu_custom_call" | custom-call | bytes 2385516 | tf_op jit(solution)/shard_map/merge/pallas_call | solution.py:448
  139.4 13.2 %prior.1 = (f32[360,384]{1,0:T(8,128)}, f32[1248,192]{1,0:T(8,128)}) custom-call(s32[3]{0:T(128)} %pad_add_fusion.place_ref.refs_0_, s32[8]{0:T(128)} %row_ref.11, bf16[26,24,384]{2,1,0:T(8,128)(2,1)} %get-tuple-element.35.prior_ref, bf16[52,48,384]{2,1,0:T(8,128)(2,1)} %get-tuple-element.36.fine_ref, bf16[8,24,384]{2,1,0:T(8,128)(2,1)} %copy-done.15, ...), custom_call_target="tpu_custom_call" | custom-call | flops 5223481344 | bytes 12238892 | tf_op jit(solution)/shard_map/prior/pallas_call | solution.py:448
  153.3 8.6 %tail.1 = bf16[26,40,192]{2,1,0:T(8,128)(2,1)} custom-call(s32[3]{0:T(128)} %pad_add_fusion.place_ref.refs_0_, s32[8]{0:T(128)} %row_ref.11, s32[16]{0:T(128)} %col_ref.9, bf16[208,384]{1,0:T(8,128)(2,1)} %get-tuple-element.33.mine_ref, bf16[208,384]{1,0:T(8,128)(2,1)} %copy-done.2, f32[360,384]{1,0:T(8,128)} %get-tuple-element.41.sum_one_ref, ...), custom_call_target="tpu_custom_call" | custom-call | bytes 6213228 | tf_op jit(solution)/shard_map/tail/pallas_call | solution.py:448
  (67 shorter events, 17.8 us)
Async XLA Ops:
  6.5 61.1 %all-gather.3.cloned.1.call-start = ((), (), s32[]{:S(2)}) async-start(), calls=%async_computation.1 | async-start | bytes 6893568 | tf_op jit(solution)/shard_map/all_gather | solution.py:484
  13.5 18.8 %collective-permute-start = (bf16[160,384]{1,0:T(8,128)(2,1)}, bf16[160,384]{1,0:T(8,128)(2,1)S(1)}, u32[]{:S(2)}, u32[]{:S(2)}) collective-permute-start(bf16[160,384]{1,0:T(8,128)(2,1)} %get-tuple-element.24), channel_id=1, source_target_pairs={{0,1},{1,2},{2,3},{3,4},{4,5},{5,6},{6,7},{7,8},{8,9},{9,10},{10,1... | collective-permute-start | bytes 368648 | tf_op jit(solution)/shard_map/ppermute | solution.py:51
  17.9 14.4 %collective-permute-start.1 = (bf16[160,384]{1,0:T(8,128)(2,1)}, bf16[160,384]{1,0:T(8,128)(2,1)S(1)}, u32[]{:S(2)}, u32[]{:S(2)}) collective-permute-start(bf16[160,384]{1,0:T(8,128)(2,1)} %get-tuple-element.25), channel_id=1, source_target_pairs={{1,0},{2,1},{3,2},{4,3},{5,4},{6,5},{7,6},{8,7},{9,8},{10,9},{11,1... | collective-permute-start | bytes 368648 | tf_op jit(solution)/shard_map/ppermute | solution.py:51
  19.2 7.3 %collective-permute-start.2 = (bf16[48,384]{1,0:T(8,128)(2,1)}, bf16[48,384]{1,0:T(8,128)(2,1)S(1)}, u32[]{:S(2)}, u32[]{:S(2)}) collective-permute-start(bf16[48,384]{1,0:T(8,128)(2,1)} %get-tuple-element.26), channel_id=1, source_target_pairs={{0,2},{1,3},{2,4},{3,5},{4,6},{5,7},{6,8},{7,9},{8,10},{9,11},{10,... | collective-permute-start | bytes 110600 | tf_op jit(solution)/shard_map/ppermute | solution.py:51
  25.1 7.1 %collective-permute-start.3 = (bf16[48,384]{1,0:T(8,128)(2,1)}, bf16[48,384]{1,0:T(8,128)(2,1)S(1)}, u32[]{:S(2)}, u32[]{:S(2)}) collective-permute-start(bf16[48,384]{1,0:T(8,128)(2,1)} %get-tuple-element.27), channel_id=1, source_target_pairs={{2,0},{3,1},{4,2},{5,3},{6,4},{7,5},{8,6},{9,7},{10,8},{11,9},{12,... | collective-permute-start | bytes 110600 | tf_op jit(solution)/shard_map/ppermute | solution.py:51
  26.5 5.8 %copy-start.5 = (bf16[48,384]{1,0:T(8,128)(2,1)}, bf16[48,384]{1,0:T(8,128)(2,1)S(1)}, u32[]{:S(2)}) copy-start(bf16[48,384]{1,0:T(8,128)(2,1)S(1)} %collective-permute-done.2.from_left_far_ref) | copy-start | bytes 110596
  38.5 3.2 %collective-permute-start.4 = (bf16[160,384]{1,0:T(8,128)(2,1)}, bf16[160,384]{1,0:T(8,128)(2,1)S(1)}, u32[]{:S(2)}, u32[]{:S(2)}) collective-permute-start(bf16[160,384]{1,0:T(8,128)(2,1)} %get-tuple-element.29), channel_id=1, source_target_pairs={{0,16},{16,0},{1,17},{17,1},{2,18},{18,2},{3,19},{19,3},{4,20},{20... | collective-permute-start | bytes 368648 | tf_op jit(solution)/shard_map/ppermute | solution.py:501
  42.7 15.0 %copy-start.1 = (bf16[2,160,384]{2,1,0:T(8,128)(2,1)}, bf16[2,160,384]{2,1,0:T(8,128)(2,1)S(1)}, u32[]{:S(2)}) copy-start(bf16[2,160,384]{2,1,0:T(8,128)(2,1)S(1)} %maximum_select_fusion.refs_2_) | copy-start | bytes 737284
  42.7 8.6 %collective-permute-start.5 = (bf16[2,160,384]{2,1,0:T(8,128)(2,1)S(1)}, bf16[2,160,384]{2,1,0:T(8,128)(2,1)S(1)}, u32[]{:S(2)}, u32[]{:S(2)}) collective-permute-start(bf16[2,160,384]{2,1,0:T(8,128)(2,1)S(1)} %maximum_select_fusion.refs_2_), channel_id=1, source_target_pairs={{0,32},{32,64},{64,96},{96,0},{1,33},{33,65},{65,97},{97,1},{2,34}... | collective-permute-start | bytes 737288 | tf_op jit(solution)/shard_map/ppermute | solution.py:503
  44.1 13.6 %collective-permute-start.6 = (bf16[2,160,384]{2,1,0:T(8,128)(2,1)S(1)}, bf16[2,160,384]{2,1,0:T(8,128)(2,1)S(1)}, u32[]{:S(2)}, u32[]{:S(2)}) collective-permute-start(bf16[2,160,384]{2,1,0:T(8,128)(2,1)S(1)} %maximum_select_fusion.refs_2_), channel_id=1, source_target_pairs={{0,64},{32,96},{64,0},{96,32},{1,65},{33,97},{65,1},{97,33},{2,66}... | collective-permute-start | bytes 737288 | tf_op jit(solution)/shard_map/ppermute | solution.py:503
  46.7 11.0 %collective-permute-start.7 = (bf16[2,160,384]{2,1,0:T(8,128)(2,1)S(1)}, bf16[2,160,384]{2,1,0:T(8,128)(2,1)S(1)}, u32[]{:S(2)}, u32[]{:S(2)}) collective-permute-start(bf16[2,160,384]{2,1,0:T(8,128)(2,1)S(1)} %maximum_select_fusion.refs_2_), channel_id=1, source_target_pairs={{0,96},{32,0},{64,32},{96,64},{1,97},{33,1},{65,33},{97,65},{2,98}... | collective-permute-start | bytes 737288 | tf_op jit(solution)/shard_map/ppermute | solution.py:503
  51.3 6.4 %copy-start.9 = (bf16[2,160,384]{2,1,0:T(8,128)(2,1)}, bf16[2,160,384]{2,1,0:T(8,128)(2,1)S(1)}, u32[]{:S(2)}) copy-start(bf16[2,160,384]{2,1,0:T(8,128)(2,1)S(1)} %collective-permute-done.5.refs_3_) | copy-start | bytes 737284
  67.6 37.3 %copy-start.13 = (bf16[8,24,384]{2,1,0:T(8,128)(2,1)S(1)}, bf16[8,24,384]{2,1,0:T(8,128)(2,1)}, u32[]{:S(2)}) copy-start(bf16[8,24,384]{2,1,0:T(8,128)(2,1)} %get-tuple-element.38) | copy-start | bytes 442372
  67.6 39.7 %copy-start.12 = (bf16[8,24,384]{2,1,0:T(8,128)(2,1)S(1)}, bf16[8,24,384]{2,1,0:T(8,128)(2,1)}, u32[]{:S(2)}) copy-start(bf16[8,24,384]{2,1,0:T(8,128)(2,1)} %get-tuple-element.37) | copy-start | bytes 442372
  67.6 43.3 %copy-start.17 = (bf16[2,24,384]{2,1,0:T(8,128)(2,1)S(1)}, bf16[2,24,384]{2,1,0:T(8,128)(2,1)}, u32[]{:S(2)}) copy-start(bf16[2,24,384]{2,1,0:T(8,128)(2,1)} %get-tuple-element.39) | copy-start | bytes 110596
  67.6 46.4 %copy-start.16 = (bf16[2,24,384]{2,1,0:T(8,128)(2,1)S(1)}, bf16[2,24,384]{2,1,0:T(8,128)(2,1)}, u32[]{:S(2)}) copy-start(bf16[2,24,384]{2,1,0:T(8,128)(2,1)} %get-tuple-element.40) | copy-start | bytes 110596
  99.2 35.9 %all-to-all-start = ((bf16[4,384,384]{2,1,0:T(8,128)(2,1)}), bf16[4,384,384]{2,1,0:T(8,128)(2,1)}, u32[]{:S(2)}, u32[]{:S(2)}) async-start(bf16[4,384,384]{2,1,0:T(8,128)(2,1)} %attention.1), calls=%async_computation | async-start | bytes 2359296 | tf_op jit(solution)/shard_map/all_to_all | solution.py:531
  104.9 33.8 %collective-permute-start.10 = (bf16[8,24,384]{2,1,0:T(8,128)(2,1)S(1)}, bf16[8,24,384]{2,1,0:T(8,128)(2,1)S(1)}, u32[]{:S(2)}, u32[]{:S(2)}) collective-permute-start(bf16[8,24,384]{2,1,0:T(8,128)(2,1)S(1)} %copy-done.13), channel_id=1, source_target_pairs={{16,0},{32,16},{48,32},{64,48},{80,64},{96,80},{112,96},{17,1},{33... | collective-permute-start | bytes 442376 | tf_op jit(solution)/shard_map/ppermute | solution.py:51
  107.3 31.4 %collective-permute-start.9 = (bf16[8,24,384]{2,1,0:T(8,128)(2,1)S(1)}, bf16[8,24,384]{2,1,0:T(8,128)(2,1)S(1)}, u32[]{:S(2)}, u32[]{:S(2)}) collective-permute-start(bf16[8,24,384]{2,1,0:T(8,128)(2,1)S(1)} %copy-done.12), channel_id=1, source_target_pairs={{0,16},{16,32},{32,48},{48,64},{64,80},{80,96},{96,112},{1,17},{17... | collective-permute-start | bytes 442376 | tf_op jit(solution)/shard_map/ppermute | solution.py:51
  110.9 27.8 %collective-permute-start.11 = (bf16[2,24,384]{2,1,0:T(8,128)(2,1)S(1)}, bf16[2,24,384]{2,1,0:T(8,128)(2,1)S(1)}, u32[]{:S(2)}, u32[]{:S(2)}) collective-permute-start(bf16[2,24,384]{2,1,0:T(8,128)(2,1)S(1)} %copy-done.17), channel_id=1, source_target_pairs={{0,32},{16,48},{32,64},{48,80},{64,96},{80,112},{1,33},{17,49},{33... | collective-permute-start | bytes 110600 | tf_op jit(solution)/shard_map/ppermute | solution.py:51
  114.0 24.7 %collective-permute-start.12 = (bf16[2,24,384]{2,1,0:T(8,128)(2,1)S(1)}, bf16[2,24,384]{2,1,0:T(8,128)(2,1)S(1)}, u32[]{:S(2)}, u32[]{:S(2)}) collective-permute-start(bf16[2,24,384]{2,1,0:T(8,128)(2,1)S(1)} %copy-done.16), channel_id=1, source_target_pairs={{32,0},{48,16},{64,32},{80,48},{96,64},{112,80},{33,1},{49,17},{65... | collective-permute-start | bytes 110600 | tf_op jit(solution)/shard_map/ppermute | solution.py:51
  126.6 3.7 %copy-start.7 = (f32[384]{0:T(512)S(1)}, f32[384]{0:T(512)}, u32[]{:S(2)}) copy-start(f32[384]{0:T(512)} %param.23) | copy-start | bytes 4612
  130.4 4.2 %copy-start.8 = (f32[384]{0:T(512)S(1)}, f32[384]{0:T(512)}, u32[]{:S(2)}) copy-start(f32[384]{0:T(512)} %param.26) | copy-start | bytes 4612
  138.7 14.0 %collective-permute-start.8 = (bf16[208,384]{1,0:T(8,128)(2,1)}, bf16[208,384]{1,0:T(8,128)(2,1)S(1)}, u32[]{:S(2)}, u32[]{:S(2)}) collective-permute-start(bf16[208,384]{1,0:T(8,128)(2,1)} %get-tuple-element.34), channel_id=1, source_target_pairs={{0,16},{16,0},{1,17},{17,1},{2,18},{18,2},{3,19},{19,3},{4,20},{20... | collective-permute-start | bytes 479240 | tf_op jit(solution)/shard_map/ppermute | solution.py:546
  (12 other events, 12.3 us)
Sparse Core Ops, SparseCore 0:
  13.6 53.9 all-gather.2

commit v3 on v2

--- a/solution.py
+++ b/solution.py
@@ -25,13 +25,14 @@
 FINE_COLS = 2 * TILE_COLS
 FINE_PITCH = 48
 KEY_TILE = 272
-KEY_CHUNK = 512
-MAX_CHUNKS = 14
+KEY_CHUNK = 1024
+MAX_CHUNKS = 7
 KEY_ROWS = MAX_CHUNKS * KEY_CHUNK + KEY_CHUNK
-QUERY_BLOCK = 352
-BLOCK_ROWS = 384
+QUERY_BLOCK = 1056
 HALF_ROWS = 208
-WIDE_ROWS = LAT_ROWS * HALF + BLOCK_ROWS
+BLOCK_ROWS = HALF_ROWS + 16
+WIDE_ROWS = LAT_ROWS * HALF + 384
+FINE_STEP = 13
 TALL_TILE = 160
 VMEM_BYTES = 60 * 1024 * 1024
 NEAR = 48
@@ -78,20 +79,24 @@
     return jnp.where(inside, size_ref[jnp.clip(index, 0, count - 1)], 0)
 
 
-def prepare_kernel(
-    place_ref, row_ref, col_ref, token_ref, one_ref, two_ref, gain_ref,
-    key_ref, right_ref, left_ref, right_far_ref, left_far_ref, pack_ref, coarse_ref, fine_ref,
-):
+def keys_kernel(place_ref, row_ref, col_ref, token_ref, gain_ref, key_ref, pack_ref):
     wide = col_ref[place_ref[1]]
     pack_ref[...] = jnp.zeros_like(pack_ref)
+    gain = gain_ref[...][None]
     for i in range(TILE_ROWS):
-        raw = token_ref[i].astype(jnp.float32)
-        put_rows(coarse_ref, (2 * TILE_ROWS + i) * 24, raw)
-        put_rows(pack_ref, i * wide, rms_scale(raw, gain_ref[...]))
+        put_rows(pack_ref, i * wide, rms_scale(token_ref[i].astype(jnp.float32), gain))
     key_ref[...] = get_rows(pack_ref, 0, KEY_TILE).astype(jnp.bfloat16)
+
+
+def edges_kernel(
+    place_ref, row_ref, col_ref, token_ref, one_ref, two_ref, right_ref, left_ref, right_far_ref, left_far_ref, coarse_ref, fine_ref
+):
+    wide = col_ref[place_ref[1]]
+    for f in range(3):
+        for i in range(TILE_ROWS):
+            row = one_ref[f, i] if f < 2 else token_ref[i]
+            put_rows(coarse_ref, (f * TILE_ROWS + i) * 24, row.astype(jnp.float32))
     for f in range(2):
-        for i in range(TILE_ROWS):
-            put_rows(coarse_ref, (f * TILE_ROWS + i) * 24, one_ref[f, i].astype(jnp.float32))
 
         def copy_fine(i, carry):
             put_rows(fine_ref, pl.multiple_of((f * FINE_ROWS + i) * FINE_COLS, 8), two_ref[f, i].astype(jnp.float32))
@@ -180,8 +185,12 @@
 
 def prior_kernel(
     place_ref, row_ref, prior_ref, fine_ref, from_up_ref, from_down_ref, from_up_far_ref, from_down_far_ref, one_ref, two_ref,
-    sum_one_ref, sum_two_ref, coarse_ref, wide_ref, part_ref,
-):
+    sum_one_ref, sum_two_ref, coarse_ref, wide_ref, part_ref, weight_one_ref, weight_two_ref, sem_ref,
+):
+    fetch_one = pltpu.make_async_copy(one_ref.at[pl.ds(0, 2)], weight_one_ref, sem_ref.at[0])
+    fetch_two = pltpu.make_async_copy(two_ref.at[pl.ds(0, 2)], weight_two_ref, sem_ref.at[1])
+    fetch_one.start()
+    fetch_two.start()
     tall = row_ref[place_ref[0]]
     up_tall = size_at(row_ref, place_ref[0] - 1)
     down_tall = size_at(row_ref, place_ref[0] + 1)
@@ -203,37 +212,52 @@
         lax.fori_loop(0, FINE_ROWS, copy_fine, 0)
         wide_ref[f, FINE_ROWS + 1] = jnp.zeros((FINE_PITCH, 384), jnp.bfloat16)
         wide_ref[f, 2 * tall + 1] = jnp.concatenate([from_down_ref[4 + 2 * f], from_down_ref[5 + 2 * f]], axis=0)
+    fetch_one.wait()
+    sum_one_ref[...] = coarse_conv(lambda f, a, n: coarse_ref[f, a : a + n], weight_one_ref, part_ref, 2)
+    fetch_two.wait()
+    for r in range(0, FINE_ROWS, FINE_STEP):
+        sum_two_ref[r * FINE_PITCH : (r + FINE_STEP) * FINE_PITCH, :] = fine_conv(
+            lambda f, a, n: wide_ref[f, r + a : r + a + n], weight_two_ref, part_ref, 2
+        )
+
+
+def coarse_conv(rows_of, weight_ref, part_ref, depth):
     rows = TILE_ROWS + 2
-    left = jnp.concatenate(
-        [coarse_ref[f, a : a + rows].reshape(rows * EXT_COLS, 384) for f in range(2) for a in range(3)], axis=1
-    )
-    sum_one_ref[...] = shifted_sum(left, lambda b: jnp.concatenate([one_ref[f, a, b] for f in range(2) for a in range(3)], axis=0), part_ref, 3)
-    step = 13
-    for r in range(0, FINE_ROWS, step):
-        left = jnp.concatenate(
-            [wide_ref[f, r + a : r + a + step].reshape(step * FINE_PITCH, 384) for f in range(2) for a in range(3)], axis=1
+    taps = [(f, a) for f in range(depth) for a in range(3)]
+    left = jnp.concatenate([rows_of(f, a, rows).reshape(rows * EXT_COLS, 384) for f, a in taps], axis=1)
+    right = jnp.concatenate([jnp.concatenate([weight_ref[f, a, b] for b in range(3)], axis=1) for f, a in taps], axis=0)
+    product = jnp.dot(left, right, preferred_element_type=jnp.float32)
+    return shifted_sum([product[:, b * 384 : (b + 1) * 384] for b in range(3)], part_ref)
+
+
+def fine_conv(rows_of, weight_ref, part_ref, depth):
+    taps = [(f, a) for f in range(depth) for a in range(3)]
+    left = jnp.concatenate([rows_of(f, a, FINE_STEP).reshape(FINE_STEP * FINE_PITCH, 384) for f, a in taps], axis=1)
+    products = [
+        lax.dot_general(
+            left, jnp.concatenate([weight_ref[f, a, b] for f, a in taps], axis=1), (((1,), (1,)), ((), ())),
+            preferred_element_type=jnp.float32,
         )
-        sum_two_ref[r * FINE_PITCH : (r + step) * FINE_PITCH, :] = shifted_sum(
-            left, lambda b: jnp.concatenate([two_ref[f, a, b] for f in range(2) for a in range(3)], axis=0), part_ref, 2
-        )[:, 0:192]
-
-
-def shifted_sum(left, weight_of, part_ref, groups):
-    count = left.shape[0]
-    total = jnp.dot(left, weight_of(0), preferred_element_type=jnp.float32)
+        for b in range(3)
+    ]
+    return shifted_sum(products, part_ref)
+
+
+def shifted_sum(products, part_ref):
+    total = products[0]
+    count, width = total.shape
+    groups = -(-width // 128)
     for b in (1, 2):
-        product = jnp.dot(left, weight_of(b), preferred_element_type=jnp.float32)
-        width = product.shape[1]
         for g in range(groups):
             hi = min((g + 1) * 128, width)
-            part_ref[g, 0:count, 0 : hi - g * 128] = product[:, g * 128 : hi]
+            part_ref[g, 0:count, 0 : hi - g * 128] = products[b][:, g * 128 : hi]
         moved = jnp.concatenate([part_ref[g, b : b + count, :] for g in range(groups)], axis=1)
         total = total + moved[:, 0:width]
     return total
 
 
 def query_kernel(
-    place_ref, row_ref, own_ref, one_ref, two_ref, three_ref, gain_ref, qw_ref, kw_ref, query_ref, frame_ref, wide_ref, *, scale
+    place_ref, row_ref, own_ref, one_ref, two_ref, three_ref, gain_ref, qw_ref, kw_ref, query_ref, frame_ref, frame_other_ref, wide_ref, *, scale
 ):
     y_at = place_ref[0] // 2
     wide_ref[...] = jnp.zeros_like(wide_ref)
@@ -248,13 +272,16 @@
                 held = wide_ref[g, pl.ds(start, TALL_TILE), :]
                 wide_ref[g, pl.ds(start, TALL_TILE), :] = jnp.where(usable, part[:, g * 128 : (g + 1) * 128], held)
     count = LAT_ROWS * HALF
-    frame_ref[...] = get_rows(wide_ref, before(row_ref, 2 * y_at) * HALF, BLOCK_ROWS).astype(jnp.bfloat16)
-    for i in range(count // QUERY_BLOCK):
-        raw = get_rows(wide_ref, FRONT + i * QUERY_BLOCK, QUERY_BLOCK)
-        normed = rms_scale(raw, gain_ref[...]).astype(jnp.bfloat16)
+    frame_ref[...] = get_rows(wide_ref, before(row_ref, place_ref[0]) * HALF, HALF_ROWS).astype(jnp.bfloat16)
+    sibling = place_ref[0] + 1 - 2 * place_ref[2]
+    frame_other_ref[...] = get_rows(wide_ref, before(row_ref, sibling) * HALF, HALF_ROWS).astype(jnp.bfloat16)
+    step = count // 3
+    for i in range(3):
+        raw = get_rows(wide_ref, FRONT + i * step, step)
+        normed = rms_scale(raw, gain_ref[...][None]).astype(jnp.bfloat16)
         query = jnp.dot(normed, qw_ref[...], preferred_element_type=jnp.float32).astype(jnp.bfloat16)
         turned = lax.dot_general(query, kw_ref[...], (((1,), (1,)), ((), ())), preferred_element_type=jnp.float32)
-        query_ref[i * QUERY_BLOCK : (i + 1) * QUERY_BLOCK, :] = (turned * scale).astype(jnp.bfloat16)
+        query_ref[i * step : (i + 1) * step, :] = (turned * scale).astype(jnp.bfloat16)
 
 
 def attention_kernel(
@@ -293,7 +320,7 @@
         return key_ref[pl.ds(pl.multiple_of(j * KEY_CHUNK, KEY_CHUNK), KEY_CHUNK), :]
 
     def score_step(i, j):
-        slot = i % 2
+        slot = 0
         query = query_ref[i * QUERY_BLOCK : (i + 1) * QUERY_BLOCK, :]
         s = lax.dot_general(query, keys_at(j), (((1,), (1,)), ((), ())), preferred_element_type=jnp.float32)
         s = s + bias_ref[j]
@@ -304,7 +331,7 @@
         top_ref[slot] = jnp.maximum(top_ref[slot], best)
 
     def value_step(i, j):
-        slot = i % 2
+        slot = 0
         top = top_ref[slot]
         p = jnp.exp2(score_ref[slot, j] - jnp.concatenate([top] * lane_groups, axis=1))
         part = p[:, 0:128]
@@ -315,9 +342,9 @@
 
     for i in range(blocks + 1):
         if i < blocks:
-            top_ref[i % 2] = jnp.full((QUERY_BLOCK, 128), masked_score, jnp.float32)
+            top_ref[0] = jnp.full((QUERY_BLOCK, 128), masked_score, jnp.float32)
         if i > 0:
-            last = (i - 1) % 2
+            last = 0
             best = jnp.max(top_ref[last], axis=1, keepdims=True)
             top_ref[last] = jnp.broadcast_to(best, (QUERY_BLOCK, 128))
             sum_ref[...] = jnp.zeros_like(sum_ref)
@@ -335,7 +362,7 @@
             denominator = jnp.sum(sum_ref[...], axis=1, keepdims=True)
             lo = FRONT + (i - 1) * QUERY_BLOCK
             put_rows(wide_ref, lo, acc_ref[...] / denominator)
-            level = top_ref[(i - 1) % 2] + jnp.log2(jnp.broadcast_to(denominator, (QUERY_BLOCK, 128)))
+            level = top_ref[0] + jnp.log2(jnp.broadcast_to(denominator, (QUERY_BLOCK, 128)))
             high = level.astype(jnp.bfloat16).astype(jnp.float32)
             mid = (level - high).astype(jnp.bfloat16).astype(jnp.float32)
             low = level - high - mid
@@ -346,108 +373,101 @@
         lax.broadcasted_iota(jnp.int32, (16, 128), 0) == lax.broadcasted_iota(jnp.int32, (16, 128), 1)
     ).astype(jnp.bfloat16)
     for b in range(out_ref.shape[0]):
-        offset = before(row_ref, 2 * b) * HALF
-        out_ref[b, 0 : BLOCK_ROWS - 16, :] = get_rows(wide_ref, offset, BLOCK_ROWS - 16).astype(jnp.bfloat16)
-        levels = stat_ref[pl.ds(offset, BLOCK_ROWS), :].astype(jnp.bfloat16)
-        out_ref[b, BLOCK_ROWS - 16 : BLOCK_ROWS, :] = lax.dot_general(
+        offset = before(row_ref, b) * HALF
+        out_ref[b, 0:HALF_ROWS, :] = get_rows(wide_ref, offset, HALF_ROWS).astype(jnp.bfloat16)
+        levels = stat_ref[pl.ds(offset, 384), :].astype(jnp.bfloat16)
+        out_ref[b, HALF_ROWS:BLOCK_ROWS, :] = lax.dot_general(
             select, levels, (((1,), (1,)), ((), ())), preferred_element_type=jnp.float32
         ).astype(jnp.bfloat16)
 
 
-def merge_kernel(
-    place_ref, row_ref, col_ref, part_ref, frame_ref, vw_ref, ow_ref, gain_ref, mine_ref, other_ref, wide_ref
-):
-    groups = part_ref.shape[0]
-    core = place_ref[2]
-    y_at = place_ref[0] // 2
-    ones = (lax.broadcasted_iota(jnp.int32, (16, 128), 0) < 3).astype(jnp.bfloat16)
-    levels = [
-        lax.dot_general(
-            part_ref[g, BLOCK_ROWS - 16 : BLOCK_ROWS, :], ones, (((0,), (0,)), ((), ())), preferred_element_type=jnp.float32
-        )
-        for g in range(groups)
-    ]
-    best = levels[0]
-    for g in range(1, groups):
-        best = jnp.maximum(best, levels[g])
-    weights = [jnp.exp2(level - best) for level in levels]
-    total = weights[0]
-    for g in range(1, groups):
-        total = total + weights[g]
-    merged = None
-    for g in range(groups):
-        share = weights[g] / total
-        term = part_ref[g].astype(jnp.float32) * jnp.concatenate([share] * 3, axis=1)
-        merged = term if merged is None else merged + term
-    merged = merged.astype(jnp.bfloat16)
-    attention = jnp.dot(merged, vw_ref[...], preferred_element_type=jnp.float32).astype(jnp.bfloat16)
-    projected = jnp.dot(attention, ow_ref[...], preferred_element_type=jnp.float32)
-    mixed = (frame_ref[...].astype(jnp.float32) + projected).astype(jnp.bfloat16)
-    act = silu(rms_scale(mixed, gain_ref[...]))
-    slot = lax.broadcasted_iota(jnp.int32, (BLOCK_ROWS, 128), 0)
-    row = jnp.right_shift(slot * 43691, 19)
-    at_row = before(row_ref, 2 * y_at) - HALO + row
-    at_col = before(col_ref, place_ref[1]) - HALO + slot - row * HALF + core * HALF
-    inside = (at_row >= 0) & (at_row < LAT_ROWS) & (at_col >= 0) & (at_col < LAT_COLS)
-    for g in range(3):
-        wide_ref[g] = jnp.where(inside, act[:, g * 128 : (g + 1) * 128], 0.0)
-    upper = row_ref[2 * y_at] * HALF
-    mine_ref[...] = get_rows(wide_ref, core * upper, HALF_ROWS).astype(jnp.bfloat16)
-    other_ref[...] = get_rows(wide_ref, (1 - core) * upper, HALF_ROWS).astype(jnp.bfloat16)
-
-
-def tail_kernel(
-    place_ref, row_ref, col_ref, mine_ref, other_ref, sum_one_ref, sum_two_ref, one_ref, two_ref, gain_ref, out_ref,
-    half_ref, act_ref, first_ref, up_ref, fine_ref, part_ref,
-):
+def finish_kernel(
+    place_ref, row_ref, col_ref, part_ref, mine_ref, other_ref, vw_ref, ow_ref, gain_one_ref, sum_one_ref, sum_two_ref, one_ref, two_ref,
+    gain_two_ref, out_ref, act_ref, first_ref, up_ref, fine_ref, shift_ref, weight_one_ref, weight_two_ref, sem_ref,
+):
+    fetch_one = pltpu.make_async_copy(one_ref.at[pl.ds(2, 1)], weight_one_ref, sem_ref.at[0])
+    fetch_two = pltpu.make_async_copy(two_ref.at[pl.ds(2, 1)], weight_two_ref, sem_ref.at[1])
+    fetch_one.start()
+    fetch_two.start()
     core = place_ref[2]
     tall = row_ref[place_ref[0]]
     wide = col_ref[place_ref[1]]
-    for side, ref in ((core, mine_ref), (1 - core, other_ref)):
-        put_rows(half_ref, 0, ref[...].astype(jnp.float32))
+    ones = (lax.broadcasted_iota(jnp.int32, (16, 128), 0) < 3).astype(jnp.bfloat16)
+    halves = []
+    for side in range(2):
+        sources = range(side, part_ref.shape[0], 2)
+        levels = [
+            lax.dot_general(
+                part_ref[g, HALF_ROWS:BLOCK_ROWS, 0:256], ones, (((0,), (0,)), ((), ())), preferred_element_type=jnp.float32
+            )[0:HALF_ROWS]
+            for g in sources
+        ]
+        best = jnp.maximum(jnp.maximum(levels[0], levels[1]), jnp.maximum(levels[2], levels[3]))
+        weights = [jnp.exp2(level - best) for level in levels]
+        total = (weights[0] + weights[1]) + (weights[2] + weights[3])
+        merged = None
+        for weight, g in zip(weights, sources):
+            share = weight / total
+            term = part_ref[g, 0:HALF_ROWS, :].astype(jnp.float32) * jnp.concatenate([share] * 3, axis=1)
+            merged = term if merged is None else merged + term
+        halves.append(merged.astype(jnp.bfloat16))
+    merged = jnp.concatenate(halves, axis=0)
+    attention = jnp.dot(merged, vw_ref[...], preferred_element_type=jnp.float32).astype(jnp.bfloat16)
+    projected = jnp.dot(attention, ow_ref[...], preferred_element_type=jnp.float32)
+    mine = mine_ref[...].astype(jnp.float32)
+    other = other_ref[...].astype(jnp.float32)
+    frame = jnp.concatenate([jnp.where(core == 0, mine, other), jnp.where(core == 0, other, mine)], axis=0)
+    mixed = (frame + projected).astype(jnp.bfloat16)
+    put_rows(shift_ref, 0, silu(rms_scale(mixed, gain_one_ref[...][None])))
+    row_start = before(row_ref, place_ref[0])
+    col_start = before(col_ref, place_ref[1])
+    for side in range(2):
         for i in range(EXT_ROWS):
-            put_rows(act_ref, i * EXT_COLS + side * HALF, get_rows(half_ref, i * HALF, HALF))
+            put_rows(act_ref, i * EXT_COLS + side * HALF, get_rows(shift_ref, side * HALF_ROWS + i * HALF, HALF))
+    at_col = col_start - HALO + lax.broadcasted_iota(jnp.int32, (EXT_COLS, 384), 0)
+    col_inside = (at_col >= 0) & (at_col < LAT_COLS)
     for i in range(EXT_ROWS):
-        first_ref[i] = get_rows(act_ref, i * EXT_COLS, EXT_COLS).astype(jnp.bfloat16)
+        at_row = row_start - HALO + i
+        inside = col_inside & (at_row >= 0) & (at_row < LAT_ROWS)
+        first_ref[i] = jnp.where(inside, get_rows(act_ref, i * EXT_COLS, EXT_COLS), 0.0).astype(jnp.bfloat16)
     rows = TILE_ROWS + 2
-    left = jnp.concatenate([first_ref[a : a + rows].reshape(rows * EXT_COLS, 384) for a in range(3)], axis=1)
-    total = shifted_sum(left, lambda b: jnp.concatenate([one_ref[0, a, b] for a in range(3)], axis=0), part_ref, 3)
+    fetch_one.wait()
+    total = coarse_conv(lambda f, a, n: first_ref[a : a + n], weight_one_ref, shift_ref, 1)
     y_one = (total + sum_one_ref[...]).astype(jnp.bfloat16)
-    act = silu(rms_scale(y_one, gain_ref[...])).astype(jnp.bfloat16).astype(jnp.float32)
-    slot = lax.broadcasted_iota(jnp.int32, (rows * EXT_COLS, 128), 0)
-    row = jnp.right_shift(slot * 43691, 20)
-    at_row = before(row_ref, place_ref[0]) - 1 + row
-    at_col = before(col_ref, place_ref[1]) - 1 + slot - row * EXT_COLS
-    inside = (at_row >= 0) & (at_row < LAT_ROWS) & (at_col >= 0) & (at_col < LAT_COLS)
-    for g in range(3):
-        act_ref[g, 0 : rows * EXT_COLS, :] = jnp.where(inside, act[:, g * 128 : (g + 1) * 128], 0.0)
+    act = silu(rms_scale(y_one, gain_two_ref[...][None])).astype(jnp.bfloat16).astype(jnp.float32)
+    put_rows(act_ref, 0, act)
+    at_col = col_start - 1 + lax.broadcasted_iota(jnp.int32, (EXT_COLS, 384), 0)
+    col_inside = (at_col >= 0) & (at_col < LAT_COLS)
     for i in range(rows):
-        small = get_rows(act_ref, i * EXT_COLS, EXT_COLS)
+        at_row = row_start - 1 + i
+        inside = col_inside & (at_row >= 0) & (at_row < LAT_ROWS)
+        small = jnp.where(inside, get_rows(act_ref, i * EXT_COLS, EXT_COLS), 0.0)
         put_strided(up_ref, 7, 2, small)
         put_strided(up_ref, 8, 2, small)
         fine = get_rows(up_ref, 8, FINE_PITCH).astype(jnp.bfloat16)
         for f in (2 * i - 1, 2 * i):
             if 0 <= f < FINE_ROWS + 2:
                 fine_ref[f] = fine
-    step = 13
     col = lax.broadcasted_iota(jnp.int32, (FINE_COLS, 192), 0)
-    for r in range(0, FINE_ROWS, step):
-        left = jnp.concatenate([fine_ref[r + a : r + a + step].reshape(step * FINE_PITCH, 384) for a in range(3)], axis=1)
-        y_two = shifted_sum(left, lambda b: jnp.concatenate([two_ref[0, a, b] for a in range(3)], axis=0), part_ref, 2)[:, 0:192]
-        y_two = y_two + sum_two_ref[r * FINE_PITCH : (r + step) * FINE_PITCH, :]
-        for i in range(step):
+    fetch_two.wait()
+    for r in range(0, FINE_ROWS, FINE_STEP):
+        y_two = fine_conv(lambda f, a, n: fine_ref[r + a : r + a + n], weight_two_ref, shift_ref, 1)
+        y_two = y_two + sum_two_ref[r * FINE_PITCH : (r + FINE_STEP) * FINE_PITCH, :]
+        for i in range(FINE_STEP):
             line = y_two[i * FINE_PITCH : i * FINE_PITCH + FINE_COLS, :]
             usable = (col < 2 * wide) & (r + i < 2 * tall)
             out_ref[r + i] = jnp.where(usable, line, 0.0).astype(jnp.bfloat16)
 
 
-def call(body, inputs, outs, scratch, smem_count, name, flops=0):
+def call(body, inputs, outs, scratch, smem_count, name, flops=0, far=()):
     smem = pl.BlockSpec(memory_space=pltpu.SMEM)
     vmem = pl.BlockSpec(memory_space=pltpu.VMEM)
     moved = sum(math.prod(v.shape) * v.dtype.itemsize for v in list(inputs) + list(outs))
     return pl.pallas_call(
         body,
-        in_specs=[smem] * smem_count + [vmem] * (len(inputs) - smem_count),
+        in_specs=[
+            smem if i < smem_count else pl.BlockSpec(memory_space=pl.ANY) if i in far else vmem for i in range(len(inputs))
+        ],
         out_specs=[vmem] * len(outs),
         out_shape=outs,
         scratch_shapes=scratch,
@@ -455,6 +475,24 @@
         cost_estimate=pl.CostEstimate(flops=int(flops), transcendentals=0, bytes_accessed=int(moved)),
         name=name,
     )(*inputs)
+
+
+def attend(place, row_sizes, col_sizes, queries, tiles):
+    channels = queries.shape[1]
+    scratch = lambda *dims: pltpu.VMEM(dims, jnp.float32)
+    (parts,) = call(
+        attention_kernel,
+        [place, row_sizes, col_sizes, queries, tiles],
+        [jax.ShapeDtypeStruct((8, BLOCK_ROWS, channels), jnp.bfloat16)],
+        [
+            pltpu.VMEM((KEY_ROWS, channels), jnp.bfloat16), scratch(MAX_CHUNKS, 1, KEY_CHUNK),
+            scratch(1, MAX_CHUNKS, QUERY_BLOCK, KEY_CHUNK),
+            scratch(1, QUERY_BLOCK, 128), scratch(QUERY_BLOCK, 128), scratch(QUERY_BLOCK, channels),
+            scratch(3, WIDE_ROWS, 128), scratch(WIDE_ROWS, 128),
+        ],
+        3, "attention", 4 * LAT_ROWS * HALF * channels * KEY_ROWS,
+    )
+    return parts
 
 
 def local(
@@ -474,21 +512,25 @@
     scratch = lambda *dims: pltpu.VMEM(dims, jnp.float32)
     narrow = lambda *dims: pltpu.VMEM(dims, jnp.bfloat16)
     message = 160
-    own_keys, to_right, to_left, to_right_far, to_left_far = call(
-        prepare_kernel,
-        [place, row_sizes, col_sizes, tokens, cache_one, cache_two, norm_gain[None]],
-        [shape(KEY_TILE, channels), shape(message, channels), shape(message, channels), shape(NEAR, channels), shape(NEAR, channels)],
-        [scratch(3, 304, 128), scratch(3, 3 * TILE_ROWS * 24, 128), scratch(3, 2 * FINE_ROWS * FINE_COLS, 128)],
-        3, "prepare",
+    place_args = [place, row_sizes, col_sizes]
+    (own_keys,) = call(
+        keys_kernel, [*place_args, tokens, norm_gain], [shape(KEY_TILE, channels)], [scratch(3, 304, 128)], 3, "keys"
     )
     tiles = lax.all_gather(own_keys, ("core", "x", "z"), axis=0, tiled=False)
+    to_right, to_left, to_right_far, to_left_far = call(
+        edges_kernel,
+        [*place_args, tokens, cache_one, cache_two],
+        [shape(message, channels), shape(message, channels), shape(NEAR, channels), shape(NEAR, channels)],
+        [scratch(3, 3 * TILE_ROWS * 24, 128), scratch(3, 2 * FINE_ROWS * FINE_COLS, 128)],
+        3, "edges",
+    )
     from_left = hop(to_right, COLS, n_col, 1)
     from_right = hop(to_left, COLS, n_col, -1)
     from_left_far = hop(to_right_far, COLS, n_col, 2)
     from_right_far = hop(to_left_far, COLS, n_col, -2)
     mine, other, prior, fine, down, up, down_far, up_far = call(
         columns_kernel,
-        [place, row_sizes, col_sizes, tokens, cache_one, cache_two, from_left, from_right, from_left_far, from_right_far],
+        [*place_args, tokens, cache_one, cache_two, from_left, from_right, from_left_far, from_right_far],
         [
             shape(TALL_TILE, channels), shape(TALL_TILE, channels), shape(2 * TILE_ROWS, EXT_COLS, channels),
             shape(2 * FINE_ROWS, FINE_PITCH, channels), shape(8, EXT_COLS, channels), shape(8, EXT_COLS, channels),
@@ -501,58 +543,47 @@
     sibling = lax.ppermute(other, "core", swap)
     pair = jnp.where(core == 0, jnp.stack([mine, sibling]), jnp.stack([sibling, mine]))
     strips = [pair] + [lax.ppermute(pair, "y", [(i, (i + k) % n_y) for i in range(n_y)]) for k in range(1, n_y)]
+    around = [hop(down, ROWS, n_row, 1), hop(up, ROWS, n_row, -1), hop(down_far, ROWS, n_row, 2), hop(up_far, ROWS, n_row, -2)]
+    strips, around = lax.optimization_barrier((strips, around))
     scale = math.log2(math.e) / math.sqrt(channels)
 
     def query_body(*refs):
         query_kernel(*refs, scale=scale)
 
-    queries, frame = call(
+    queries, frame, frame_other = call(
         query_body,
-        [place, row_sizes, *strips, norm_gain[None], query_weight, key_weight],
-        [shape(LAT_ROWS * HALF, channels), shape(BLOCK_ROWS, channels)],
+        [place, row_sizes, *strips, norm_gain, query_weight, key_weight],
+        [shape(LAT_ROWS * HALF, channels), shape(HALF_ROWS, channels), shape(HALF_ROWS, channels)],
         [scratch(3, WIDE_ROWS, 128)],
         2, "queries", 4 * LAT_ROWS * HALF * channels * channels,
     )
-    from_up = hop(down, ROWS, n_row, 1)
-    from_down = hop(up, ROWS, n_row, -1)
-    from_up_far = hop(down_far, ROWS, n_row, 2)
-    from_down_far = hop(up_far, ROWS, n_row, -2)
-    (parts,) = call(
-        attention_kernel,
-        [place, row_sizes, col_sizes, queries, tiles.reshape(2 * n_col, KEY_TILE, channels)],
-        [shape(n_y, BLOCK_ROWS, channels)],
-        [
-            narrow(KEY_ROWS, channels), scratch(MAX_CHUNKS, 1, KEY_CHUNK), scratch(2, MAX_CHUNKS, QUERY_BLOCK, KEY_CHUNK),
-            scratch(2, QUERY_BLOCK, 128), scratch(QUERY_BLOCK, 128), scratch(QUERY_BLOCK, channels),
-            scratch(3, WIDE_ROWS, 128), scratch(WIDE_ROWS, 128),
-        ],
-        3, "attention", 4 * LAT_ROWS * HALF * channels * KEY_ROWS,
-    )
-    parts = lax.all_to_all(parts, "y", 0, 0)
+    frame_other = lax.ppermute(frame_other, "core", swap)
+    parts = attend(place, row_sizes, col_sizes, queries, tiles.reshape(2 * n_col, KEY_TILE, channels))
+    parts = lax.all_to_all(parts, ROWS, 0, 0)
+    conv_two = jnp.swapaxes(conv_two, 3, 4)
+    channels_out = conv_two.shape[3]
     sum_one, sum_two = call(
         prior_kernel,
-        [place, row_sizes, prior, fine, from_up, from_down, from_up_far, from_down_far, conv_one[:2], conv_two[:2]],
-        [wide_shape((TILE_ROWS + 2) * EXT_COLS, channels), wide_shape(FINE_ROWS * FINE_PITCH, conv_two.shape[-1])],
-        [narrow(2, EXT_ROWS, EXT_COLS, channels), narrow(2, FINE_ROWS + 2, FINE_PITCH, channels), scratch(3, 640, 128)],
-        2, "prior", 2 * 18 * channels * (360 * 384 + 1248 * 192),
-    )
-    half_mine, half_other = call(
-        merge_kernel,
-        [place, row_sizes, col_sizes, parts, frame, value_weight, out_weight, gain_one[None]],
-        [shape(HALF_ROWS, channels), shape(HALF_ROWS, channels)],
-        [scratch(3, BLOCK_ROWS, 128)],
-        3, "merge",
-    )
-    half_other = lax.ppermute(half_other, "core", swap)
+        [place, row_sizes, prior, fine, *around, conv_one, conv_two],
+        [wide_shape((TILE_ROWS + 2) * EXT_COLS, channels), wide_shape(FINE_ROWS * FINE_PITCH, channels_out)],
+        [
+            narrow(2, EXT_ROWS, EXT_COLS, channels), narrow(2, FINE_ROWS + 2, FINE_PITCH, channels), scratch(3, 640, 128),
+            narrow(2, 3, 3, channels, channels), narrow(2, 3, 3, channels_out, channels), pltpu.SemaphoreType.DMA((2,)),
+        ],
+        2, "prior", 2 * 18 * channels * (360 * 384 + 1248 * 192), (8, 9),
+    )
     (decoded,) = call(
-        tail_kernel,
-        [place, row_sizes, col_sizes, half_mine, half_other, sum_one, sum_two, conv_one[2:], conv_two[2:], gain_two[None]],
-        [shape(FINE_ROWS, FINE_COLS, conv_two.shape[-1])],
+        finish_kernel,
         [
-            scratch(3, HALF_ROWS, 128), scratch(3, EXT_ROWS * EXT_COLS, 128), narrow(EXT_ROWS, EXT_COLS, channels),
+            *place_args, parts, frame, frame_other, value_weight, out_weight, gain_one, sum_one, sum_two, conv_one, conv_two, gain_two,
+        ],
+        [shape(FINE_ROWS, FINE_COLS, channels_out)],
+        [
+            scratch(3, EXT_ROWS * EXT_COLS, 128), narrow(EXT_ROWS, EXT_COLS, channels),
             scratch(3, 64, 128), narrow(FINE_ROWS + 2, FINE_PITCH, channels), scratch(3, 640, 128),
+            narrow(1, 3, 3, channels, channels), narrow(1, 3, 3, channels_out, channels), pltpu.SemaphoreType.DMA((2,)),
         ],
-        3, "tail",
+        3, "finish", 0, (11, 12),
     )
     return decoded
 

time: 170 us -> 140 us (0.82)
  local copies, waits for them, and re-layouts: 26.7 us -> 5.77 us
  Pallas kernels: 69.3 us -> 58.1 us
  starting transfers between devices: 36.3 us -> 40 us
    pallas_call x7, Pallas kernels: 69.3 us -> 58.1 us  [call(): pl.pallas_call(body, in_specs=[smem if i < smem_count else pl.BlockSpec(m...]
    slice x5 -> x0, local copies, waits for them, and re-layouts: 10.5 us -> none  [the longest x1 5.61 us: local(): conv_one[:2]]
    ppermute x3, waiting for transfers between devices: 9.91 us -> 0.01 us  [local(): lax.ppermute(pair, 'y', [(i, (i + k) % n_y) for i in range(n_y)])]
    unnamed x43 -> x31, local copies, waits for them, and re-layouts: 13.8 us -> 5.77 us
    ppermute x8, waiting for transfers between devices: 5.86 us -> 13.8 us  [hop(): return lax.ppermute(value, axes, pairs)]
    all_to_all x1, waiting for transfers between devices: 0.01 us -> 5.01 us  [local(): parts = lax.all_to_all(parts, ROWS, 0, 0)]
    all_gather x1, waiting for transfers between devices: 4.26 us -> 0.01 us  [local(): tiles = lax.all_gather(own_keys, ('core', 'x', 'z'), axis=0, tiled=False)]
    all_to_all x1, starting transfers between devices: 5.69 us -> 8.43 us  [local(): parts = lax.all_to_all(parts, ROWS, 0, 0)]
  transfers between devices with their start and end apart: 15 -> 15, of which waited for: 6 -> 7; matrix products, arithmetic and copies ran while one was open for 12% -> 2% of each run, Pallas kernels for 15% -> 18%
where the time goes in v3:
time: 140 us; the launch traced here: 139 us
  Pallas kernels  58.1 us (42%)
  starting transfers between devices  40 us (29%)
  waiting for transfers between devices  20 us (14%)
  between operations  13.6 us (10%)
  local copies, waits for them, and re-layouts  5.77 us (4%)
  other arithmetic  1.67 us (1%)
    pallas_call x7, Pallas kernels, call(): pl.pallas_call(body, in_specs=[smem if i < smem_count else pl.BlockSpec(m...  58.1 us
    ppermute x8, starting transfers between devices, hop(): return lax.ppermute(value, axes, pairs)  23.5 us
    ppermute x8, waiting for transfers between devices, hop(): return lax.ppermute(value, axes, pairs)  13.8 us
    all_to_all x1, starting transfers between devices, local(): parts = lax.all_to_all(parts, ROWS, 0, 0)  8.43 us
    unnamed x31, local copies, waits for them, and re-layouts  5.77 us
    all_to_all x1, waiting for transfers between devices, local(): parts = lax.all_to_all(parts, ROWS, 0, 0)  5.01 us
    ppermute x3, starting transfers between devices, local(): lax.ppermute(pair, 'y', [(i, (i + k) % n_y) for i in range(n_y)])  4.99 us
    ppermute x1, starting transfers between devices, local(): sibling = lax.ppermute(other, 'core', swap)  2.82 us
  transfers between devices with their start and end apart: 15, of which 7 were waited for; matrix products, arithmetic and copies ran while one was open for 2% of the time, Pallas kernels for 18%

profile of v3, /device:TPU:1, one launch (start us, length us, event | category | flops | bytes accessed | tf_op | source)
XLA Modules:
  0.0 139.2 jit_solution(7793198567531280807)
XLA Ops:
  7.2 1.8 %keys.1 = bf16[272,384]{1,0:T(8,128)(2,1)} custom-call(s32[3]{0:T(128)} %pad_add_fusion.place_ref.refs_0_, s32[8]{0:T(128)} %row_ref.11, s32[16]{0:T(128)} %col_ref.9, bf16[13,20,384]{2,1,0:T(8,128)(2,1)} %token_ref.5, f32[384]{0:T(512)} %gain_ref.1), custom_call_target="tpu_custom_call" | custom-call | bytes 410220 | tf_op jit(solution)/shard_map/keys/pallas_call | solution.py:466
  9.0 1.8 %copy.16.one_ref = bf16[2,13,20,384]{3,2,1,0:T(8,128)(2,1)} copy(bf16[2,13,20,384]{3,0,2,1:T(2,128)(2,1)} %param.22) | data formatting | bytes 798720 | tf_op args[8]
  10.9 3.0 %edges.1 = (bf16[160,384]{1,0:T(8,128)(2,1)}, bf16[160,384]{1,0:T(8,128)(2,1)}, bf16[48,384]{1,0:T(8,128)(2,1)}, bf16[48,384]{1,0:T(8,128)(2,1)}) custom-call(s32[3]{0:T(128)} %pad_add_fusion.place_ref.refs_0_, s32[8]{0:T(128)} %row_ref.11, s32[16]{0:T(128)} %col_ref.9, bf16[13,20,384]{2,1,0:T(8,128)(2,1)} %token_ref.5, ...), custom_call_target="tpu_custom_call" | custom-call | bytes 2516076 | tf_op jit(solution)/shard_map/edges/pallas_call | solution.py:466
  13.8 4.4 %collective-permute-start = (bf16[160,384]{1,0:T(8,128)(2,1)}, bf16[160,384]{1,0:T(8,128)(2,1)S(1)}, u32[]{:S(2)}, u32[]{:S(2)}) collective-permute-start(bf16[160,384]{1,0:T(8,128)(2,1)} %get-tuple-element.30), channel_id=1, source_target_pairs={{0,1},{1,2},{2,3},{3,4},{4,5},{5,6},{6,7},{7,8},{8,9},{9,10},{10,1... | collective-permute-start | bytes 368648 | tf_op jit(solution)/shard_map/ppermute | solution.py:52
  18.2 1.3 collective-permute-start.1
  19.5 5.9 %collective-permute-start.2 = (bf16[48,384]{1,0:T(8,128)(2,1)}, bf16[48,384]{1,0:T(8,128)(2,1)S(1)}, u32[]{:S(2)}, u32[]{:S(2)}) collective-permute-start(bf16[48,384]{1,0:T(8,128)(2,1)} %get-tuple-element.32), channel_id=1, source_target_pairs={{0,2},{1,3},{2,4},{3,5},{4,6},{5,7},{6,8},{7,9},{8,10},{9,11},{10,... | collective-permute-start | bytes 110600 | tf_op jit(solution)/shard_map/ppermute | solution.py:52
  25.5 1.3 collective-permute-start.3
  26.8 5.1 %collective-permute-done.3.from_right_far_ref = bf16[48,384]{1,0:T(8,128)(2,1)S(1)} collective-permute-done((bf16[48,384]{1,0:T(8,128)(2,1)}, bf16[48,384]{1,0:T(8,128)(2,1)S(1)}, u32[]{:S(2)}, u32[]{:S(2)}) %collective-permute-start.3) | collective-permute-done | bytes 36896 | tf_op jit(solution)/shard_map/ppermute | solution.py:52
  33.2 4.9 %columns.1 = (bf16[160,384]{1,0:T(8,128)(2,1)}, bf16[160,384]{1,0:T(8,128)(2,1)}, bf16[26,24,384]{2,1,0:T(8,128)(2,1)}, bf16[52,48,384]{2,1,0:T(8,128)(2,1)}, bf...) custom-call(s32[3]{0:T(128)} %pad_add_fusion.place_ref.refs_0_, ...), custom_call_target="tpu_custom_call" | custom-call | bytes 5526636 | tf_op jit(solution)/shard_map/columns/pallas_call | solution.py:466
  38.1 2.8 %collective-permute-start.4 = (bf16[160,384]{1,0:T(8,128)(2,1)}, bf16[160,384]{1,0:T(8,128)(2,1)S(1)}, u32[]{:S(2)}, u32[]{:S(2)}) collective-permute-start(bf16[160,384]{1,0:T(8,128)(2,1)} %get-tuple-element.35), channel_id=1, source_target_pairs={{0,16},{16,0},{1,17},{17,1},{2,18},{18,2},{3,19},{19,3},{4,20},{20... | collective-permute-start | bytes 368648 | tf_op jit(solution)/shard_map/ppermute | solution.py:543
  43.1 1.4 collective-permute-start.5
  44.5 2.6 %collective-permute-start.6 = (bf16[2,160,384]{2,1,0:T(8,128)(2,1)S(1)}, bf16[2,160,384]{2,1,0:T(8,128)(2,1)S(1)}, u32[]{:S(2)}, u32[]{:S(2)}) collective-permute-start(bf16[2,160,384]{2,1,0:T(8,128)(2,1)S(1)} %maximum_select_fusion.refs_2_), channel_id=1, source_target_pairs={{0,64},{32,96},{64,0},{96,32},{1,65},{33,97},{65,1},{97,33},{2,66}... | collective-permute-start | bytes 737288 | tf_op jit(solution)/shard_map/ppermute | solution.py:545
  48.1 2.3 %collective-permute-start.10 = (bf16[2,24,384]{2,1,0:T(8,128)(2,1)}, bf16[2,24,384]{2,1,0:T(8,128)(2,1)S(1)}, u32[]{:S(2)}, u32[]{:S(2)}) collective-permute-start(bf16[2,24,384]{2,1,0:T(8,128)(2,1)} %get-tuple-element.38), channel_id=1, source_target_pairs={{0,32},{16,48},{32,64},{48,80},{64,96},{80,112},{1,33},{17,49},{33... | collective-permute-start | bytes 110600 | tf_op jit(solution)/shard_map/ppermute | solution.py:52
  50.5 1.3 collective-permute-start.11
  51.8 3.9 %collective-permute-done.10.from_up_far_ref = bf16[2,24,384]{2,1,0:T(8,128)(2,1)S(1)} collective-permute-done((bf16[2,24,384]{2,1,0:T(8,128)(2,1)}, bf16[2,24,384]{2,1,0:T(8,128)(2,1)S(1)}, u32[]{:S(2)}, u32[]{:S(2)}) %collective-permute-start.10) | collective-permute-done | bytes 36896 | tf_op jit(solution)/shard_map/ppermute | solution.py:52
  55.7 5.1 %collective-permute-start.8 = (bf16[8,24,384]{2,1,0:T(8,128)(2,1)}, bf16[8,24,384]{2,1,0:T(8,128)(2,1)S(1)}, u32[]{:S(2)}, u32[]{:S(2)}) collective-permute-start(bf16[8,24,384]{2,1,0:T(8,128)(2,1)} %get-tuple-element.36), channel_id=1, source_target_pairs={{0,16},{16,32},{32,48},{48,64},{64,80},{80,96},{96,112},{1,17},{17... | collective-permute-start | bytes 442376 | tf_op jit(solution)/shard_map/ppermute | solution.py:52
  60.8 1.9 %collective-permute-start.9 = (bf16[8,24,384]{2,1,0:T(8,128)(2,1)}, bf16[8,24,384]{2,1,0:T(8,128)(2,1)S(1)}, u32[]{:S(2)}, u32[]{:S(2)}) collective-permute-start(bf16[8,24,384]{2,1,0:T(8,128)(2,1)} %get-tuple-element.37), channel_id=1, source_target_pairs={{16,0},{32,16},{48,32},{64,48},{80,64},{96,80},{112,96},{17,1},{33... | collective-permute-start | bytes 442376 | tf_op jit(solution)/shard_map/ppermute | solution.py:52
  63.2 4.3 %collective-permute-done.9.from_down_ref = bf16[8,24,384]{2,1,0:T(8,128)(2,1)S(1)} collective-permute-done((bf16[8,24,384]{2,1,0:T(8,128)(2,1)}, bf16[8,24,384]{2,1,0:T(8,128)(2,1)S(1)}, u32[]{:S(2)}, u32[]{:S(2)}) %collective-permute-start.9) | collective-permute-done | bytes 147488 | tf_op jit(solution)/shard_map/ppermute | solution.py:52
  69.0 4.2 %queries.1 = (bf16[1056,384]{1,0:T(8,128)(2,1)}, bf16[208,384]{1,0:T(8,128)(2,1)}, bf16[208,384]{1,0:T(8,128)(2,1)}) custom-call(s32[3]{0:T(128)} %pad_add_fusion.place_ref.refs_0_, s32[8]{0:T(128)} %row_ref.11, bf16[2,160,384]{2,1,0:T(8,128)(2,1)} %copy-done.1, bf16[2,160,384]{2,1,0:T(8,128)(2,1)} %copy-done.7, bf16[2,160,384]{2,1,0:T(8,128)(2,1)} %copy-done.8, ...), custom_call_target="tpu_custom_call" | custom-call | flops 622854144 | bytes 2704940 | tf_op jit(solution)/shard_map/queries/pallas_call | solution.py:466
  73.2 20.0 %attention.1 = bf16[8,224,384]{2,1,0:T(8,128)(2,1)} custom-call(s32[3]{0:T(128)} %pad_add_fusion.place_ref.refs_0_, s32[8]{0:T(128)} %row_ref.11, s32[16]{0:T(128)} %col_ref.9, bf16[1056,384]{1,0:T(8,128)(2,1)} %get-tuple-element.44.query_ref, bf16[32,272,384]{2,1,0:T(8,128)(2,1)} %bitcast.11), custom_call_target="tpu_custom_call" | custom-call | flops 13287555072 | bytes 8872044 | tf_op jit(solution)/shard_map/attention/pallas_call | solution.py:466
  93.2 8.4 %all-to-all-start = ((bf16[8,224,384]{2,1,0:T(8,128)(2,1)}), bf16[8,224,384]{2,1,0:T(8,128)(2,1)S(1)}, u32[]{:S(2)}, u32[]{:S(2)}) async-start(bf16[8,224,384]{2,1,0:T(8,128)(2,1)} %attention.1), calls=%async_computation | async-start | bytes 2752512 | tf_op jit(solution)/shard_map/all_to_all | solution.py:562
  101.9 13.3 %prior.1 = (f32[360,384]{1,0:T(8,128)}, f32[1248,192]{1,0:T(8,128)}) custom-call(s32[3]{0:T(128)} %pad_add_fusion.place_ref.refs_0_, s32[8]{0:T(128)} %row_ref.11, bf16[26,24,384]{2,1,0:T(8,128)(2,1)} %get-tuple-element.47.prior_ref, bf16[52,48,384]{2,1,0:T(8,128)(2,1)} %get-tuple-element.48.fine_ref, bf16[8,24,384]{2,1,0:T(8,128)(2,1)} %copy-done.11, ...), custom_call_target="tpu_custom_call" | custom-call | flops 5223481344 | bytes 16220204 | tf_op jit(solution)/shard_map/prior/pallas_call | solution.py:466
  115.2 5.0 %all-to-all-done.part_ref = bf16[8,224,384]{2,1,0:T(8,128)(2,1)S(1)} async-done(((bf16[8,224,384]{2,1,0:T(8,128)(2,1)}), bf16[8,224,384]{2,1,0:T(8,128)(2,1)S(1)}, u32[]{:S(2)}, u32[]{:S(2)}) %all-to-all-start) | async-done | bytes 1376288 | tf_op jit(solution)/shard_map/all_to_all | solution.py:562
  121.3 11.0 %finish.1 = bf16[26,40,192]{2,1,0:T(8,128)(2,1)} custom-call(s32[3]{0:T(128)} %pad_add_fusion.place_ref.refs_0_, s32[8]{0:T(128)} %row_ref.11, s32[16]{0:T(128)} %col_ref.9, bf16[8,224,384]{2,1,0:T(8,128)(2,1)} %copy-done, bf16[208,384]{1,0:T(8,128)(2,1)} %get-tuple-element.45.mine_ref, bf16[208,384]{1,0:T(8,128)(2,1)} %copy-done.2, ...), custom_call_target="tpu_custom_call" | custom-call | bytes 16143468 | tf_op jit(solution)/shard_map/finish/pallas_call | solution.py:466
  (47 shorter events, 8.6 us)
Async XLA Ops:
  6.5 66.7 %all-gather.3.cloned.1.call-start = ((), (), s32[]{:S(2)}) async-start(), calls=%async_computation.1 | async-start | bytes 6893568 | tf_op jit(solution)/shard_map/all_gather | solution.py:519
  13.8 18.1 %collective-permute-start = (bf16[160,384]{1,0:T(8,128)(2,1)}, bf16[160,384]{1,0:T(8,128)(2,1)S(1)}, u32[]{:S(2)}, u32[]{:S(2)}) collective-permute-start(bf16[160,384]{1,0:T(8,128)(2,1)} %get-tuple-element.30), channel_id=1, source_target_pairs={{0,1},{1,2},{2,3},{3,4},{4,5},{5,6},{6,7},{7,8},{8,9},{9,10},{10,1... | collective-permute-start | bytes 368648 | tf_op jit(solution)/shard_map/ppermute | solution.py:52
  18.2 13.7 %collective-permute-start.1 = (bf16[160,384]{1,0:T(8,128)(2,1)}, bf16[160,384]{1,0:T(8,128)(2,1)S(1)}, u32[]{:S(2)}, u32[]{:S(2)}) collective-permute-start(bf16[160,384]{1,0:T(8,128)(2,1)} %get-tuple-element.31), channel_id=1, source_target_pairs={{1,0},{2,1},{3,2},{4,3},{5,4},{6,5},{7,6},{8,7},{9,8},{10,9},{11,1... | collective-permute-start | bytes 368648 | tf_op jit(solution)/shard_map/ppermute | solution.py:52
  19.5 7.3 %collective-permute-start.2 = (bf16[48,384]{1,0:T(8,128)(2,1)}, bf16[48,384]{1,0:T(8,128)(2,1)S(1)}, u32[]{:S(2)}, u32[]{:S(2)}) collective-permute-start(bf16[48,384]{1,0:T(8,128)(2,1)} %get-tuple-element.32), channel_id=1, source_target_pairs={{0,2},{1,3},{2,4},{3,5},{4,6},{5,7},{6,8},{7,9},{8,10},{9,11},{10,... | collective-permute-start | bytes 110600 | tf_op jit(solution)/shard_map/ppermute | solution.py:52
  25.5 6.4 %collective-permute-start.3 = (bf16[48,384]{1,0:T(8,128)(2,1)}, bf16[48,384]{1,0:T(8,128)(2,1)S(1)}, u32[]{:S(2)}, u32[]{:S(2)}) collective-permute-start(bf16[48,384]{1,0:T(8,128)(2,1)} %get-tuple-element.33), channel_id=1, source_target_pairs={{2,0},{3,1},{4,2},{5,3},{6,4},{7,5},{8,6},{9,7},{10,8},{11,9},{12,... | collective-permute-start | bytes 110600 | tf_op jit(solution)/shard_map/ppermute | solution.py:52
  26.8 5.1 %copy-start.5 = (bf16[48,384]{1,0:T(8,128)(2,1)}, bf16[48,384]{1,0:T(8,128)(2,1)S(1)}, u32[]{:S(2)}) copy-start(bf16[48,384]{1,0:T(8,128)(2,1)S(1)} %collective-permute-done.2.from_left_far_ref) | copy-start | bytes 110596
  38.1 4.0 %collective-permute-start.4 = (bf16[160,384]{1,0:T(8,128)(2,1)}, bf16[160,384]{1,0:T(8,128)(2,1)S(1)}, u32[]{:S(2)}, u32[]{:S(2)}) collective-permute-start(bf16[160,384]{1,0:T(8,128)(2,1)} %get-tuple-element.35), channel_id=1, source_target_pairs={{0,16},{16,0},{1,17},{17,1},{2,18},{18,2},{3,19},{19,3},{4,20},{20... | collective-permute-start | bytes 368648 | tf_op jit(solution)/shard_map/ppermute | solution.py:543
  43.1 24.4 %copy-start.1 = (bf16[2,160,384]{2,1,0:T(8,128)(2,1)}, bf16[2,160,384]{2,1,0:T(8,128)(2,1)S(1)}, u32[]{:S(2)}) copy-start(bf16[2,160,384]{2,1,0:T(8,128)(2,1)S(1)} %maximum_select_fusion.refs_2_) | copy-start | bytes 737284
  43.1 24.3 %collective-permute-start.5 = (bf16[2,160,384]{2,1,0:T(8,128)(2,1)S(1)}, bf16[2,160,384]{2,1,0:T(8,128)(2,1)S(1)}, u32[]{:S(2)}, u32[]{:S(2)}) collective-permute-start(bf16[2,160,384]{2,1,0:T(8,128)(2,1)S(1)} %maximum_select_fusion.refs_2_), channel_id=1, source_target_pairs={{0,32},{32,64},{64,96},{96,0},{1,33},{33,65},{65,97},{97,1},{2,34}... | collective-permute-start | bytes 737288 | tf_op jit(solution)/shard_map/ppermute | solution.py:545
  44.5 23.0 %collective-permute-start.6 = (bf16[2,160,384]{2,1,0:T(8,128)(2,1)S(1)}, bf16[2,160,384]{2,1,0:T(8,128)(2,1)S(1)}, u32[]{:S(2)}, u32[]{:S(2)}) collective-permute-start(bf16[2,160,384]{2,1,0:T(8,128)(2,1)S(1)} %maximum_select_fusion.refs_2_), channel_id=1, source_target_pairs={{0,64},{32,96},{64,0},{96,32},{1,65},{33,97},{65,1},{97,33},{2,66}... | collective-permute-start | bytes 737288 | tf_op jit(solution)/shard_map/ppermute | solution.py:545
  47.1 20.4 %collective-permute-start.7 = (bf16[2,160,384]{2,1,0:T(8,128)(2,1)S(1)}, bf16[2,160,384]{2,1,0:T(8,128)(2,1)S(1)}, u32[]{:S(2)}, u32[]{:S(2)}) collective-permute-start(bf16[2,160,384]{2,1,0:T(8,128)(2,1)S(1)} %maximum_select_fusion.refs_2_), channel_id=1, source_target_pairs={{0,96},{32,0},{64,32},{96,64},{1,97},{33,1},{65,33},{97,65},{2,98}... | collective-permute-start | bytes 737288 | tf_op jit(solution)/shard_map/ppermute | solution.py:545
  48.1 7.6 %collective-permute-start.10 = (bf16[2,24,384]{2,1,0:T(8,128)(2,1)}, bf16[2,24,384]{2,1,0:T(8,128)(2,1)S(1)}, u32[]{:S(2)}, u32[]{:S(2)}) collective-permute-start(bf16[2,24,384]{2,1,0:T(8,128)(2,1)} %get-tuple-element.38), channel_id=1, source_target_pairs={{0,32},{16,48},{32,64},{48,80},{64,96},{80,112},{1,33},{17,49},{33... | collective-permute-start | bytes 110600 | tf_op jit(solution)/shard_map/ppermute | solution.py:52
  50.5 10.3 %collective-permute-start.11 = (bf16[2,24,384]{2,1,0:T(8,128)(2,1)}, bf16[2,24,384]{2,1,0:T(8,128)(2,1)S(1)}, u32[]{:S(2)}, u32[]{:S(2)}) collective-permute-start(bf16[2,24,384]{2,1,0:T(8,128)(2,1)} %get-tuple-element.39), channel_id=1, source_target_pairs={{32,0},{48,16},{64,32},{80,48},{96,64},{112,80},{33,1},{49,17},{65... | collective-permute-start | bytes 110600 | tf_op jit(solution)/shard_map/ppermute | solution.py:52
  55.7 37.5 %copy-start.13 = (bf16[2,24,384]{2,1,0:T(8,128)(2,1)}, bf16[2,24,384]{2,1,0:T(8,128)(2,1)S(1)}, u32[]{:S(2)}) copy-start(bf16[2,24,384]{2,1,0:T(8,128)(2,1)S(1)} %collective-permute-done.10.from_up_far_ref) | copy-start | bytes 110596
  55.7 7.5 %collective-permute-start.8 = (bf16[8,24,384]{2,1,0:T(8,128)(2,1)}, bf16[8,24,384]{2,1,0:T(8,128)(2,1)S(1)}, u32[]{:S(2)}, u32[]{:S(2)}) collective-permute-start(bf16[8,24,384]{2,1,0:T(8,128)(2,1)} %get-tuple-element.36), channel_id=1, source_target_pairs={{0,16},{16,32},{32,48},{48,64},{64,80},{80,96},{96,112},{1,17},{17... | collective-permute-start | bytes 442376 | tf_op jit(solution)/shard_map/ppermute | solution.py:52
  60.8 32.4 %copy-start.14 = (bf16[2,24,384]{2,1,0:T(8,128)(2,1)}, bf16[2,24,384]{2,1,0:T(8,128)(2,1)S(1)}, u32[]{:S(2)}) copy-start(bf16[2,24,384]{2,1,0:T(8,128)(2,1)S(1)} %collective-permute-done.11.from_down_far_ref) | copy-start | bytes 110596
  60.8 6.7 %collective-permute-start.9 = (bf16[8,24,384]{2,1,0:T(8,128)(2,1)}, bf16[8,24,384]{2,1,0:T(8,128)(2,1)S(1)}, u32[]{:S(2)}, u32[]{:S(2)}) collective-permute-start(bf16[8,24,384]{2,1,0:T(8,128)(2,1)} %get-tuple-element.37), channel_id=1, source_target_pairs={{16,0},{32,16},{48,32},{64,48},{80,64},{96,80},{112,96},{17,1},{33... | collective-permute-start | bytes 442376 | tf_op jit(solution)/shard_map/ppermute | solution.py:52
  63.2 30.0 %copy-start.11 = (bf16[8,24,384]{2,1,0:T(8,128)(2,1)}, bf16[8,24,384]{2,1,0:T(8,128)(2,1)S(1)}, u32[]{:S(2)}) copy-start(bf16[8,24,384]{2,1,0:T(8,128)(2,1)S(1)} %collective-permute-done.8.from_up_ref) | copy-start | bytes 442372
  67.5 25.7 %copy-start.12 = (bf16[8,24,384]{2,1,0:T(8,128)(2,1)}, bf16[8,24,384]{2,1,0:T(8,128)(2,1)S(1)}, u32[]{:S(2)}) copy-start(bf16[8,24,384]{2,1,0:T(8,128)(2,1)S(1)} %collective-permute-done.9.from_down_ref) | copy-start | bytes 442372
  93.2 8.4 %copy-start.10 = (bf16[208,384]{1,0:T(8,128)(2,1)S(1)}, bf16[208,384]{1,0:T(8,128)(2,1)}, u32[]{:S(2)}) copy-start(bf16[208,384]{1,0:T(8,128)(2,1)} %get-tuple-element.46) | copy-start | bytes 479236
  93.2 27.0 %all-to-all-start = ((bf16[8,224,384]{2,1,0:T(8,128)(2,1)}), bf16[8,224,384]{2,1,0:T(8,128)(2,1)S(1)}, u32[]{:S(2)}, u32[]{:S(2)}) async-start(bf16[8,224,384]{2,1,0:T(8,128)(2,1)} %attention.1), calls=%async_computation | async-start | bytes 2752512 | tf_op jit(solution)/shard_map/all_to_all | solution.py:562
  101.6 13.6 %collective-permute-start.12 = (bf16[208,384]{1,0:T(8,128)(2,1)S(1)}, bf16[208,384]{1,0:T(8,128)(2,1)S(1)}, u32[]{:S(2)}, u32[]{:S(2)}) collective-permute-start(bf16[208,384]{1,0:T(8,128)(2,1)S(1)} %copy-done.10), channel_id=1, source_target_pairs={{0,16},{16,0},{1,17},{17,1},{2,18},{18,2},{3,19},{19,3},{4,20},{20... | collective-permute-start | bytes 479240 | tf_op jit(solution)/shard_map/ppermute | solution.py:560
  115.2 5.0 %copy-start.2 = (bf16[208,384]{1,0:T(8,128)(2,1)}, bf16[208,384]{1,0:T(8,128)(2,1)S(1)}, u32[]{:S(2)}) copy-start(bf16[208,384]{1,0:T(8,128)(2,1)S(1)} %collective-permute-done.12.other_ref) | copy-start | bytes 479236
  120.2 1.1 copy-start
  (6 other events, 4.2 us)
Sparse Core Ops, SparseCore 0:
  9.7 53.6 all-gather.2

commit v4 on v3

--- a/solution.py
+++ b/solution.py
@@ -30,7 +30,7 @@
 KEY_ROWS = MAX_CHUNKS * KEY_CHUNK + KEY_CHUNK
 QUERY_BLOCK = 1056
 HALF_ROWS = 208
-BLOCK_ROWS = HALF_ROWS + 16
+STAT_ROW = EXT_ROWS * HALF - (HALF_ROWS - 16)
 WIDE_ROWS = LAT_ROWS * HALF + 384
 FINE_STEP = 13
 TALL_TILE = 160
@@ -50,6 +50,15 @@
 def hop(value, axes, count, step):
     pairs = [(i, i + step) for i in range(count) if 0 <= i + step < count]
     return lax.ppermute(value, axes, pairs)
+
+
+def far_hops(needed, ahead, back, axes, count):
+    return lax.cond(
+        needed,
+        lambda a, b: [hop(a, axes, count, 2), hop(b, axes, count, -2)],
+        lambda a, b: [a, b],
+        ahead, back,
+    )
 
 
 def put_rows(ref, start, value):
@@ -137,8 +146,8 @@
         for i in range(TILE_ROWS):
             row = one_ref[f, i] if f < 2 else token_ref[i]
             put_rows(coarse_ref, (f * TILE_ROWS + i) * EXT_COLS + HALO, row.astype(jnp.float32))
-    left_two = jnp.where(left_wide >= 2, from_left_ref[NEAR : NEAR + near, :], from_left_far_ref[0:near, :])
-    right_two = jnp.where(right_wide >= 2, from_right_ref[NEAR : NEAR + near, :], from_right_far_ref[0:near, :])
+    left_two = jnp.where(left_wide == 1, from_left_far_ref[0:near, :], from_left_ref[NEAR : NEAR + near, :])
+    right_two = jnp.where(right_wide == 1, from_right_far_ref[0:near, :], from_right_ref[NEAR : NEAR + near, :])
     put_strided(coarse_ref, 0, EXT_COLS, left_two.astype(jnp.float32))
     put_strided(coarse_ref, 1, EXT_COLS, from_left_ref[0:near, :].astype(jnp.float32))
     put_strided(coarse_ref, wide + 2, EXT_COLS, from_right_ref[0:near, :].astype(jnp.float32))
@@ -185,24 +194,24 @@
 
 def prior_kernel(
     place_ref, row_ref, prior_ref, fine_ref, from_up_ref, from_down_ref, from_up_far_ref, from_down_far_ref, one_ref, two_ref,
-    sum_one_ref, sum_two_ref, coarse_ref, wide_ref, part_ref, weight_one_ref, weight_two_ref, sem_ref,
+    sum_one_ref, sum_two_ref, phase_ref, coarse_ref, wide_ref, part_ref, weight_one_ref, weight_two_ref, sem_ref,
 ):
     fetch_one = pltpu.make_async_copy(one_ref.at[pl.ds(0, 2)], weight_one_ref, sem_ref.at[0])
-    fetch_two = pltpu.make_async_copy(two_ref.at[pl.ds(0, 2)], weight_two_ref, sem_ref.at[1])
+    fetch_two = pltpu.make_async_copy(two_ref, weight_two_ref, sem_ref.at[1])
     fetch_one.start()
     fetch_two.start()
     tall = row_ref[place_ref[0]]
     up_tall = size_at(row_ref, place_ref[0] - 1)
     down_tall = size_at(row_ref, place_ref[0] + 1)
     for f in range(2):
-        coarse_ref[f, 0] = jnp.where(up_tall >= 2, from_up_ref[2 + f], from_up_far_ref[f])
+        coarse_ref[f, 0] = jnp.where(up_tall == 1, from_up_far_ref[f], from_up_ref[2 + f])
         coarse_ref[f, 1] = from_up_ref[f]
         for i in range(TILE_ROWS):
             coarse_ref[f, HALO + i] = prior_ref[f * TILE_ROWS + i]
         for i in (TILE_ROWS + 2, TILE_ROWS + 3):
             coarse_ref[f, i] = jnp.zeros((EXT_COLS, 384), jnp.bfloat16)
         coarse_ref[f, tall + 2] = from_down_ref[f]
-        coarse_ref[f, tall + 3] = jnp.where(down_tall >= 2, from_down_ref[2 + f], from_down_far_ref[f])
+        coarse_ref[f, tall + 3] = jnp.where(down_tall == 1, from_down_far_ref[f], from_down_ref[2 + f])
         wide_ref[f, 0] = jnp.concatenate([from_up_ref[4 + 2 * f], from_up_ref[5 + 2 * f]], axis=0)
 
         def copy_fine(i, carry):
@@ -219,6 +228,14 @@
         sum_two_ref[r * FINE_PITCH : (r + FINE_STEP) * FINE_PITCH, :] = fine_conv(
             lambda f, a, n: wide_ref[f, r + a : r + a + n], weight_two_ref, part_ref, 2
         )
+    taps = ((0,), (1, 2), (0, 1), (2,))
+    for u in range(4):
+        rows = []
+        for b in range(3):
+            tap = sum(weight_two_ref[2, a, b].astype(jnp.float32) for a in taps[u])
+            rows.append(tap)
+        for v in range(4):
+            phase_ref[u, v] = sum(rows[b] for b in taps[v]).astype(jnp.bfloat16)
 
 
 def coarse_conv(rows_of, weight_ref, part_ref, depth):
@@ -369,36 +386,39 @@
             lane = lax.broadcasted_iota(jnp.int32, (QUERY_BLOCK, 128), 1)
             packed = jnp.where(lane == 0, high, jnp.where(lane == 1, mid, jnp.where(lane == 2, low, 0.0)))
             stat_ref[lo : lo + QUERY_BLOCK, :] = packed
+    body = HALF_ROWS - 16
     select = (
-        lax.broadcasted_iota(jnp.int32, (16, 128), 0) == lax.broadcasted_iota(jnp.int32, (16, 128), 1)
+        lax.broadcasted_iota(jnp.int32, (16, 128), 0) - STAT_ROW == lax.broadcasted_iota(jnp.int32, (16, 128), 1)
     ).astype(jnp.bfloat16)
+    is_stat = lax.broadcasted_iota(jnp.int32, (16, 384), 0) >= STAT_ROW
     for b in range(out_ref.shape[0]):
         offset = before(row_ref, b) * HALF
-        out_ref[b, 0:HALF_ROWS, :] = get_rows(wide_ref, offset, HALF_ROWS).astype(jnp.bfloat16)
+        out_ref[b, 0:body, :] = get_rows(wide_ref, offset, body).astype(jnp.bfloat16)
         levels = stat_ref[pl.ds(offset, 384), :].astype(jnp.bfloat16)
-        out_ref[b, HALF_ROWS:BLOCK_ROWS, :] = lax.dot_general(
-            select, levels, (((1,), (1,)), ((), ())), preferred_element_type=jnp.float32
-        ).astype(jnp.bfloat16)
+        levels = lax.dot_general(select, levels, (((1,), (1,)), ((), ())), preferred_element_type=jnp.float32)
+        last = jnp.where(is_stat, levels, get_rows(wide_ref, offset + body, 16))
+        out_ref[b, body:HALF_ROWS, :] = last.astype(jnp.bfloat16)
 
 
 def finish_kernel(
     place_ref, row_ref, col_ref, part_ref, mine_ref, other_ref, vw_ref, ow_ref, gain_one_ref, sum_one_ref, sum_two_ref, one_ref, two_ref,
-    gain_two_ref, out_ref, act_ref, first_ref, up_ref, fine_ref, shift_ref, weight_one_ref, weight_two_ref, sem_ref,
+    gain_two_ref, out_ref, act_ref, first_ref, shift_ref, product_ref, fine_ref, weight_one_ref, phase_ref, sem_ref,
 ):
     fetch_one = pltpu.make_async_copy(one_ref.at[pl.ds(2, 1)], weight_one_ref, sem_ref.at[0])
-    fetch_two = pltpu.make_async_copy(two_ref.at[pl.ds(2, 1)], weight_two_ref, sem_ref.at[1])
+    fetch_two = pltpu.make_async_copy(two_ref, phase_ref, sem_ref.at[1])
     fetch_one.start()
     fetch_two.start()
     core = place_ref[2]
     tall = row_ref[place_ref[0]]
     wide = col_ref[place_ref[1]]
-    ones = (lax.broadcasted_iota(jnp.int32, (16, 128), 0) < 3).astype(jnp.bfloat16)
+    stat = lax.broadcasted_iota(jnp.int32, (16, 128), 0)
+    ones = ((stat >= STAT_ROW) & (stat < STAT_ROW + 3)).astype(jnp.bfloat16)
     halves = []
     for side in range(2):
         sources = range(side, part_ref.shape[0], 2)
         levels = [
             lax.dot_general(
-                part_ref[g, HALF_ROWS:BLOCK_ROWS, 0:256], ones, (((0,), (0,)), ((), ())), preferred_element_type=jnp.float32
+                part_ref[g, HALF_ROWS - 16 : HALF_ROWS, 0:256], ones, (((0,), (0,)), ((), ())), preferred_element_type=jnp.float32
             )[0:HALF_ROWS]
             for g in sources
         ]
@@ -441,22 +461,29 @@
     for i in range(rows):
         at_row = row_start - 1 + i
         inside = col_inside & (at_row >= 0) & (at_row < LAT_ROWS)
-        small = jnp.where(inside, get_rows(act_ref, i * EXT_COLS, EXT_COLS), 0.0)
-        put_strided(up_ref, 7, 2, small)
-        put_strided(up_ref, 8, 2, small)
-        fine = get_rows(up_ref, 8, FINE_PITCH).astype(jnp.bfloat16)
-        for f in (2 * i - 1, 2 * i):
-            if 0 <= f < FINE_ROWS + 2:
-                fine_ref[f] = fine
+        first_ref[i] = jnp.where(inside, get_rows(act_ref, i * EXT_COLS, EXT_COLS), 0.0).astype(jnp.bfloat16)
+    fetch_two.wait()
+    count = TILE_ROWS * EXT_COLS
+    for p in range(2):
+        left = jnp.concatenate(
+            [first_ref[p + u : p + u + TILE_ROWS].reshape(count, 384) for u in range(2)], axis=1
+        )
+        for q in range(2):
+            for v in range(2):
+                right = jnp.concatenate([phase_ref[2 * p + u, 2 * q + v] for u in range(2)], axis=1)
+                product = lax.dot_general(left, right, (((1,), (1,)), ((), ())), preferred_element_type=jnp.float32)
+                product_ref[2 * q + v, 0, 0:count, :] = product[:, 0:128]
+                product_ref[2 * q + v, 1, 0:count, 0:64] = product[:, 128:192]
+            for i in range(TILE_ROWS):
+                for g in range(2):
+                    near = product_ref[2 * q, g, pl.ds(i * EXT_COLS + q, EXT_COLS), :]
+                    next_ = product_ref[2 * q + 1, g, pl.ds(i * EXT_COLS + q + 1, EXT_COLS), :]
+                    fine_ref[g, pl.ds((2 * i + p) * FINE_PITCH + q, EXT_COLS, 2), :] = near + next_
     col = lax.broadcasted_iota(jnp.int32, (FINE_COLS, 192), 0)
-    fetch_two.wait()
-    for r in range(0, FINE_ROWS, FINE_STEP):
-        y_two = fine_conv(lambda f, a, n: fine_ref[r + a : r + a + n], weight_two_ref, shift_ref, 1)
-        y_two = y_two + sum_two_ref[r * FINE_PITCH : (r + FINE_STEP) * FINE_PITCH, :]
-        for i in range(FINE_STEP):
-            line = y_two[i * FINE_PITCH : i * FINE_PITCH + FINE_COLS, :]
-            usable = (col < 2 * wide) & (r + i < 2 * tall)
-            out_ref[r + i] = jnp.where(usable, line, 0.0).astype(jnp.bfloat16)
+    for r in range(FINE_ROWS):
+        line = get_rows(fine_ref, r * FINE_PITCH, FINE_COLS)[:, 0:192] + sum_two_ref[r * FINE_PITCH : r * FINE_PITCH + FINE_COLS, :]
+        usable = (col < 2 * wide) & (r < 2 * tall)
+        out_ref[r] = jnp.where(usable, line, 0.0).astype(jnp.bfloat16)
 
 
 def call(body, inputs, outs, scratch, smem_count, name, flops=0, far=()):
@@ -483,7 +510,7 @@
     (parts,) = call(
         attention_kernel,
         [place, row_sizes, col_sizes, queries, tiles],
-        [jax.ShapeDtypeStruct((8, BLOCK_ROWS, channels), jnp.bfloat16)],
+        [jax.ShapeDtypeStruct((8, HALF_ROWS, channels), jnp.bfloat16)],
         [
             pltpu.VMEM((KEY_ROWS, channels), jnp.bfloat16), scratch(MAX_CHUNKS, 1, KEY_CHUNK),
             scratch(1, MAX_CHUNKS, QUERY_BLOCK, KEY_CHUNK),
@@ -526,8 +553,7 @@
     )
     from_left = hop(to_right, COLS, n_col, 1)
     from_right = hop(to_left, COLS, n_col, -1)
-    from_left_far = hop(to_right_far, COLS, n_col, 2)
-    from_right_far = hop(to_left_far, COLS, n_col, -2)
+    from_left_far, from_right_far = far_hops(jnp.any(col_sizes == 1), to_right_far, to_left_far, COLS, n_col)
     mine, other, prior, fine, down, up, down_far, up_far = call(
         columns_kernel,
         [*place_args, tokens, cache_one, cache_two, from_left, from_right, from_left_far, from_right_far],
@@ -543,7 +569,8 @@
     sibling = lax.ppermute(other, "core", swap)
     pair = jnp.where(core == 0, jnp.stack([mine, sibling]), jnp.stack([sibling, mine]))
     strips = [pair] + [lax.ppermute(pair, "y", [(i, (i + k) % n_y) for i in range(n_y)]) for k in range(1, n_y)]
-    around = [hop(down, ROWS, n_row, 1), hop(up, ROWS, n_row, -1), hop(down_far, ROWS, n_row, 2), hop(up_far, ROWS, n_row, -2)]
+    around = [hop(down, ROWS, n_row, 1), hop(up, ROWS, n_row, -1)]
+    around += far_hops(jnp.any(row_sizes == 1), down_far, up_far, ROWS, n_row)
     strips, around = lax.optimization_barrier((strips, around))
     scale = math.log2(math.e) / math.sqrt(channels)
 
@@ -562,26 +589,29 @@
     parts = lax.all_to_all(parts, ROWS, 0, 0)
     conv_two = jnp.swapaxes(conv_two, 3, 4)
     channels_out = conv_two.shape[3]
-    sum_one, sum_two = call(
+    sum_one, sum_two, phases = call(
         prior_kernel,
         [place, row_sizes, prior, fine, *around, conv_one, conv_two],
-        [wide_shape((TILE_ROWS + 2) * EXT_COLS, channels), wide_shape(FINE_ROWS * FINE_PITCH, channels_out)],
+        [
+            wide_shape((TILE_ROWS + 2) * EXT_COLS, channels), wide_shape(FINE_ROWS * FINE_PITCH, channels_out),
+            shape(4, 4, channels_out, channels),
+        ],
         [
             narrow(2, EXT_ROWS, EXT_COLS, channels), narrow(2, FINE_ROWS + 2, FINE_PITCH, channels), scratch(3, 640, 128),
-            narrow(2, 3, 3, channels, channels), narrow(2, 3, 3, channels_out, channels), pltpu.SemaphoreType.DMA((2,)),
+            narrow(2, 3, 3, channels, channels), narrow(3, 3, 3, channels_out, channels), pltpu.SemaphoreType.DMA((2,)),
         ],
         2, "prior", 2 * 18 * channels * (360 * 384 + 1248 * 192), (8, 9),
     )
     (decoded,) = call(
         finish_kernel,
         [
-            *place_args, parts, frame, frame_other, value_weight, out_weight, gain_one, sum_one, sum_two, conv_one, conv_two, gain_two,
+            *place_args, parts, frame, frame_other, value_weight, out_weight, gain_one, sum_one, sum_two, conv_one, phases, gain_two,
         ],
         [shape(FINE_ROWS, FINE_COLS, channels_out)],
         [
-            scratch(3, EXT_ROWS * EXT_COLS, 128), narrow(EXT_ROWS, EXT_COLS, channels),
-            scratch(3, 64, 128), narrow(FINE_ROWS + 2, FINE_PITCH, channels), scratch(3, 640, 128),
-            narrow(1, 3, 3, channels, channels), narrow(1, 3, 3, channels_out, channels), pltpu.SemaphoreType.DMA((2,)),
+            scratch(3, EXT_ROWS * EXT_COLS, 128), narrow(EXT_ROWS, EXT_COLS, channels), scratch(3, 640, 128),
+            scratch(4, 2, TILE_ROWS * EXT_COLS + 8, 128), scratch(2, FINE_ROWS * FINE_PITCH, 128),
+            narrow(1, 3, 3, channels, channels), narrow(4, 4, channels_out, channels), pltpu.SemaphoreType.DMA((2,)),
         ],
         3, "finish", 0, (11, 12),
     )

time: 140 us -> 129 us (0.921)
  starting transfers between devices: 40 us -> 22.9 us
  Pallas kernels: 58.1 us -> 63.1 us
  local copies, waits for them, and re-layouts: 5.77 us -> 4.27 us
    ppermute x8 -> x4, starting transfers between devices: 23.5 us -> 12.4 us  [hop(): return lax.ppermute(value, axes, pairs)]
    all_gather x1, waiting for transfers between devices: 0.01 us -> 6.77 us  [local(): tiles = lax.all_gather(own_keys, ('core', 'x', 'z'), axis=0, tiled=False)]
    pallas_call x7, Pallas kernels: 58.1 us -> 63.1 us  [call(): pl.pallas_call(body, in_specs=[smem if i < smem_count else pl.BlockSpec(m...]
    ppermute x8 -> x4, waiting for transfers between devices: 13.8 us -> 8.86 us  [hop(): return lax.ppermute(value, axes, pairs)]
    all_to_all x1, starting transfers between devices: 8.43 us -> 4.69 us  [local(): parts = lax.all_to_all(parts, ROWS, 0, 0)]
    all_to_all x1, waiting for transfers between devices: 5.01 us -> 2.92 us  [local(): parts = lax.all_to_all(parts, ROWS, 0, 0)]
    unnamed x31 -> x27, local copies, waits for them, and re-layouts: 5.77 us -> 4.27 us
  transfers between devices with their start and end apart: 15 -> 11, of which waited for: 7 -> 7; matrix products, arithmetic and copies ran while one was open for 2% -> 3% of each run, Pallas kernels for 18% -> 21%
where the time goes in v4:
time: 129 us; the launch traced here: 128 us
  Pallas kernels  63.1 us (49%)
  starting transfers between devices  22.9 us (18%)
  waiting for transfers between devices  20.3 us (16%)
  between operations  14.8 us (11%)
  local copies, waits for them, and re-layouts  4.27 us (3%)
  other arithmetic  2.93 us (2%)
    pallas_call x7, Pallas kernels, call(): pl.pallas_call(body, in_specs=[smem if i < smem_count else pl.BlockSpec(m...  63.1 us
    ppermute x4, starting transfers between devices, hop(): return lax.ppermute(value, axes, pairs)  12.4 us
    ppermute x4, waiting for transfers between devices, hop(): return lax.ppermute(value, axes, pairs)  8.86 us
    all_gather x1, waiting for transfers between devices, local(): tiles = lax.all_gather(own_keys, ('core', 'x', 'z'), axis=0, tiled=False)  6.77 us
    all_to_all x1, starting transfers between devices, local(): parts = lax.all_to_all(parts, ROWS, 0, 0)  4.69 us
    unnamed x27, local copies, waits for them, and re-layouts  4.27 us
    ppermute x3, starting transfers between devices, local(): lax.ppermute(pair, 'y', [(i, (i + k) % n_y) for i in range(n_y)])  3.89 us
    all_to_all x1, waiting for transfers between devices, local(): parts = lax.all_to_all(parts, ROWS, 0, 0)  2.92 us
  transfers between devices with their start and end apart: 11, of which 7 were waited for; matrix products, arithmetic and copies ran while one was open for 3% of the time, Pallas kernels for 21%

profile of v4, /device:TPU:1, one launch (start us, length us, event | category | flops | bytes accessed | tf_op | source)
XLA Modules:
  0.0 128.3 jit_solution(17941051245213142774)
XLA Ops:
  7.1 1.8 %keys.1 = bf16[272,384]{1,0:T(8,128)(2,1)} custom-call(s32[3]{0:T(128)} %pad_add_fusion.place_ref.refs_0_, s32[8]{0:T(128)} %row_ref.11, s32[16]{0:T(128)} %col_ref.9, bf16[13,20,384]{2,1,0:T(8,128)(2,1)} %token_ref.5, f32[384]{0:T(512)} %gain_ref.1), custom_call_target="tpu_custom_call" | custom-call | bytes 410220 | tf_op jit(solution)/shard_map/keys/pallas_call | solution.py:493
  9.0 1.8 %copy.16.one_ref = bf16[2,13,20,384]{3,2,1,0:T(8,128)(2,1)} copy(bf16[2,13,20,384]{3,0,2,1:T(2,128)(2,1)} %param.26) | data formatting | bytes 798720 | tf_op args[8]
  10.8 3.0 %edges.1 = (bf16[160,384]{1,0:T(8,128)(2,1)}, bf16[160,384]{1,0:T(8,128)(2,1)}, bf16[48,384]{1,0:T(8,128)(2,1)S(1)}, bf16[48,384]{1,0:T(8,128)(2,1)S(1)}) custom-call(s32[3]{0:T(128)} %pad_add_fusion.place_ref.refs_0_, s32[8]{0:T(128)} %row_ref.11, s32[16]{0:T(128)} %col_ref.9, bf16[13,20,384]{2,1,0:T(8,128)(2,1)} %token_ref.5, ...), custom_call_target="tpu_custom_call" | custom-call | bytes 2516076 | tf_op jit(solution)/shard_map/edges/pallas_call | solution.py:493
  13.8 4.5 %collective-permute-start.4 = (bf16[160,384]{1,0:T(8,128)(2,1)}, bf16[160,384]{1,0:T(8,128)(2,1)S(1)}, u32[]{:S(2)}, u32[]{:S(2)}) collective-permute-start(bf16[160,384]{1,0:T(8,128)(2,1)} %get-tuple-element.55), channel_id=1, source_target_pairs={{0,1},{1,2},{2,3},{3,4},{4,5},{5,6},{6,7},{7,8},{8,9},{9,10},{10,1... | collective-permute-start | bytes 368648 | tf_op jit(solution)/shard_map/ppermute | solution.py:52
  18.3 1.3 %collective-permute-start.5 = (bf16[160,384]{1,0:T(8,128)(2,1)}, bf16[160,384]{1,0:T(8,128)(2,1)S(1)}, u32[]{:S(2)}, u32[]{:S(2)}) collective-permute-start(bf16[160,384]{1,0:T(8,128)(2,1)} %get-tuple-element.56), channel_id=1, source_target_pairs={{1,0},{2,1},{3,2},{4,3},{5,4},{6,5},{7,6},{8,7},{9,8},{10,9},{11,1... | collective-permute-start | bytes 368648 | tf_op jit(solution)/shard_map/ppermute | solution.py:52
  21.0 3.7 %collective-permute-done.5.from_right_ref = bf16[160,384]{1,0:T(8,128)(2,1)S(1)} collective-permute-done((bf16[160,384]{1,0:T(8,128)(2,1)}, bf16[160,384]{1,0:T(8,128)(2,1)S(1)}, u32[]{:S(2)}, u32[]{:S(2)}) %collective-permute-start.5) | collective-permute-done | bytes 122912 | tf_op jit(solution)/shard_map/ppermute | solution.py:52
  25.3 4.9 %columns.1 = (bf16[160,384]{1,0:T(8,128)(2,1)}, bf16[160,384]{1,0:T(8,128)(2,1)}, bf16[26,24,384]{2,1,0:T(8,128)(2,1)}, bf16[52,48,384]{2,1,0:T(8,128)(2,1)}, bf...) custom-call(s32[3]{0:T(128)} %pad_add_fusion.place_ref.refs_0_, ...), custom_call_target="tpu_custom_call" | custom-call | bytes 5526636 | tf_op jit(solution)/shard_map/columns/pallas_call | solution.py:493
  30.2 1.7 %collective-permute-start.6 = (bf16[160,384]{1,0:T(8,128)(2,1)}, bf16[160,384]{1,0:T(8,128)(2,1)S(1)}, u32[]{:S(2)}, u32[]{:S(2)}) collective-permute-start(bf16[160,384]{1,0:T(8,128)(2,1)} %get-tuple-element.62), channel_id=1, source_target_pairs={{0,16},{16,0},{1,17},{17,1},{2,18},{18,2},{3,19},{19,3},{4,20},{20... | collective-permute-start | bytes 368648 | tf_op jit(solution)/shard_map/ppermute | solution.py:569
  31.8 1.2 collective-permute-done.6
  33.0 1.0 maximum_select_fusion.refs_2_
  34.1 3.0 %collective-permute-start.9 = (bf16[2,160,384]{2,1,0:T(8,128)(2,1)S(1)}, bf16[2,160,384]{2,1,0:T(8,128)(2,1)S(1)}, u32[]{:S(2)}, u32[]{:S(2)}) collective-permute-start(bf16[2,160,384]{2,1,0:T(8,128)(2,1)S(1)} %maximum_select_fusion.refs_2_), channel_id=1, source_target_pairs={{0,96},{32,0},{64,32},{96,64},{1,97},{33,1},{65,33},{97,65},{2,98}... | collective-permute-start | bytes 737288 | tf_op jit(solution)/shard_map/ppermute | solution.py:571
  37.2 0.7 collective-permute-start.7
  39.3 4.7 %collective-permute-start.10 = (bf16[8,24,384]{2,1,0:T(8,128)(2,1)}, bf16[8,24,384]{2,1,0:T(8,128)(2,1)S(1)}, u32[]{:S(2)}, u32[]{:S(2)}) collective-permute-start(bf16[8,24,384]{2,1,0:T(8,128)(2,1)} %get-tuple-element.63), channel_id=1, source_target_pairs={{0,16},{16,32},{32,48},{48,64},{64,80},{80,96},{96,112},{1,17},{17... | collective-permute-start | bytes 442376 | tf_op jit(solution)/shard_map/ppermute | solution.py:52
  44.0 1.9 %collective-permute-start.11 = (bf16[8,24,384]{2,1,0:T(8,128)(2,1)}, bf16[8,24,384]{2,1,0:T(8,128)(2,1)S(1)}, u32[]{:S(2)}, u32[]{:S(2)}) collective-permute-start(bf16[8,24,384]{2,1,0:T(8,128)(2,1)} %get-tuple-element.64), channel_id=1, source_target_pairs={{16,0},{32,16},{48,32},{64,48},{80,64},{96,80},{112,96},{17,1},{33... | collective-permute-start | bytes 442376 | tf_op jit(solution)/shard_map/ppermute | solution.py:52
  45.9 4.1 %collective-permute-done.10.from_up_ref = bf16[8,24,384]{2,1,0:T(8,128)(2,1)S(1)} collective-permute-done((bf16[8,24,384]{2,1,0:T(8,128)(2,1)}, bf16[8,24,384]{2,1,0:T(8,128)(2,1)S(1)}, u32[]{:S(2)}, u32[]{:S(2)}) %collective-permute-start.10) | collective-permute-done | bytes 147488 | tf_op jit(solution)/shard_map/ppermute | solution.py:52
  50.0 1.1 collective-permute-done.11.from_down_ref
  52.3 4.2 %queries.1 = (bf16[1056,384]{1,0:T(8,128)(2,1)}, bf16[208,384]{1,0:T(8,128)(2,1)}, bf16[208,384]{1,0:T(8,128)(2,1)}) custom-call(s32[3]{0:T(128)} %pad_add_fusion.place_ref.refs_0_, s32[8]{0:T(128)} %row_ref.11, bf16[2,160,384]{2,1,0:T(8,128)(2,1)} %copy-done.1, bf16[2,160,384]{2,1,0:T(8,128)(2,1)} %copy-done.9, bf16[2,160,384]{2,1,0:T(8,128)(2,1)} %copy-done.8, ...), custom_call_target="tpu_custom_call" | custom-call | flops 622854144 | bytes 2704940 | tf_op jit(solution)/shard_map/queries/pallas_call | solution.py:493
  56.5 6.8 %all-gather.3.cloned.1.call-done = bf16[8704,384]{1,0:T(8,128)(2,1)} async-done(((bf16[272,384]{1,0:T(8,128)(2,1)}), bf16[8704,384]{1,0:T(8,128)(2,1)}) %all-gather.3.cloned.1.call-update) | async-done | bytes 6684688 | tf_op jit(solution)/shard_map/all_gather | solution.py:546
  63.3 25.4 %attention.1 = bf16[8,208,384]{2,1,0:T(8,128)(2,1)} custom-call(s32[3]{0:T(128)} %pad_add_fusion.place_ref.refs_0_, s32[8]{0:T(128)} %row_ref.11, s32[16]{0:T(128)} %col_ref.9, bf16[1056,384]{1,0:T(8,128)(2,1)} %get-tuple-element.73.query_ref, bf16[32,272,384]{2,1,0:T(8,128)(2,1)} %bitcast.9), custom_call_target="tpu_custom_call" | custom-call | flops 13287555072 | bytes 8773740 | tf_op jit(solution)/shard_map/attention/pallas_call | solution.py:493
  88.7 4.7 %all-to-all-start = ((bf16[8,208,384]{2,1,0:T(8,128)(2,1)}), bf16[8,208,384]{2,1,0:T(8,128)(2,1)S(1)}, u32[]{:S(2)}, u32[]{:S(2)}) async-start(bf16[8,208,384]{2,1,0:T(8,128)(2,1)} %attention.1), calls=%async_computation | async-start | bytes 2555904 | tf_op jit(solution)/shard_map/all_to_all | solution.py:589
  93.6 14.3 %prior.1 = (f32[360,384]{1,0:T(8,128)}, f32[1248,192]{1,0:T(8,128)}, bf16[4,4,192,384]{3,2,1,0:T(8,128)(2,1)}) custom-call(s32[3]{0:T(128)} %pad_add_fusion.place_ref.refs_0_, s32[8]{0:T(128)} %row_ref.11, bf16[26,24,384]{2,1,0:T(8,128)(2,1)} %get-tuple-element.76.prior_ref, bf16[52,48,384]{2,1,0:T(8,128)(2,1)} %get-tuple-element.77.fine_ref, ...), custom_call_target="tpu_custom_call" | custom-call | flops 5223481344 | bytes 18579500 | tf_op jit(solution)/shard_map/prior/pallas_call | solution.py:493
  108.0 2.9 %all-to-all-done.part_ref = bf16[8,208,384]{2,1,0:T(8,128)(2,1)S(1)} async-done(((bf16[8,208,384]{2,1,0:T(8,128)(2,1)}), bf16[8,208,384]{2,1,0:T(8,128)(2,1)S(1)}, u32[]{:S(2)}, u32[]{:S(2)}) %all-to-all-start) | async-done | bytes 1277984 | tf_op jit(solution)/shard_map/all_to_all | solution.py:589
  110.9 1.0 copy-done
  112.0 9.5 %finish.1 = bf16[26,40,192]{2,1,0:T(8,128)(2,1)} custom-call(s32[3]{0:T(128)} %pad_add_fusion.place_ref.refs_0_, s32[8]{0:T(128)} %row_ref.11, s32[16]{0:T(128)} %col_ref.9, bf16[8,208,384]{2,1,0:T(8,128)(2,1)} %copy-done, bf16[208,384]{1,0:T(8,128)(2,1)} %get-tuple-element.74.mine_ref, bf16[208,384]{1,0:T(8,128)(2,1)} %copy-done.2, ...), custom_call_target="tpu_custom_call" | custom-call | bytes 14423148 | tf_op jit(solution)/shard_map/finish/pallas_call | solution.py:493
  (39 shorter events, 4.3 us)
Async XLA Ops:
  6.5 56.8 %all-gather.3.cloned.1.call-start = ((), (), s32[]{:S(2)}) async-start(), calls=%async_computation.1 | async-start | bytes 6893568 | tf_op jit(solution)/shard_map/all_gather | solution.py:546
  7.1 12.5 %copy-start.6 = (s32[16]{0:T(128)S(1)}, s32[16]{0:T(128)}, u32[]{:S(2)}) copy-start(s32[16]{0:T(128)} %col_ref.9) | copy-start | bytes 196
  13.8 24.2 %copy-start.5 = (s32[8]{0:T(128)S(1)}, s32[8]{0:T(128)}, u32[]{:S(2)}) copy-start(s32[8]{0:T(128)} %row_ref.11) | copy-start | bytes 100
  13.8 7.1 %collective-permute-start.4 = (bf16[160,384]{1,0:T(8,128)(2,1)}, bf16[160,384]{1,0:T(8,128)(2,1)S(1)}, u32[]{:S(2)}, u32[]{:S(2)}) collective-permute-start(bf16[160,384]{1,0:T(8,128)(2,1)} %get-tuple-element.55), channel_id=1, source_target_pairs={{0,1},{1,2},{2,3},{3,4},{4,5},{5,6},{6,7},{7,8},{8,9},{9,10},{10,1... | collective-permute-start | bytes 368648 | tf_op jit(solution)/shard_map/ppermute | solution.py:52
  18.3 6.4 %collective-permute-start.5 = (bf16[160,384]{1,0:T(8,128)(2,1)}, bf16[160,384]{1,0:T(8,128)(2,1)S(1)}, u32[]{:S(2)}, u32[]{:S(2)}) collective-permute-start(bf16[160,384]{1,0:T(8,128)(2,1)} %get-tuple-element.56), channel_id=1, source_target_pairs={{1,0},{2,1},{3,2},{4,3},{5,4},{6,5},{7,6},{8,7},{9,8},{10,9},{11,1... | collective-permute-start | bytes 368648 | tf_op jit(solution)/shard_map/ppermute | solution.py:52
  20.9 3.7 %copy-start.3 = (bf16[160,384]{1,0:T(8,128)(2,1)}, bf16[160,384]{1,0:T(8,128)(2,1)S(1)}, u32[]{:S(2)}) copy-start(bf16[160,384]{1,0:T(8,128)(2,1)S(1)} %collective-permute-done.4.from_left_ref) | copy-start | bytes 368644
  24.7 0.6 copy-start.4
  30.2 2.8 %collective-permute-start.6 = (bf16[160,384]{1,0:T(8,128)(2,1)}, bf16[160,384]{1,0:T(8,128)(2,1)S(1)}, u32[]{:S(2)}, u32[]{:S(2)}) collective-permute-start(bf16[160,384]{1,0:T(8,128)(2,1)} %get-tuple-element.62), channel_id=1, source_target_pairs={{0,16},{16,0},{1,17},{17,1},{2,18},{18,2},{3,19},{19,3},{4,20},{20... | collective-permute-start | bytes 368648 | tf_op jit(solution)/shard_map/ppermute | solution.py:569
  34.0 17.5 %copy-start.1 = (bf16[2,160,384]{2,1,0:T(8,128)(2,1)}, bf16[2,160,384]{2,1,0:T(8,128)(2,1)S(1)}, u32[]{:S(2)}) copy-start(bf16[2,160,384]{2,1,0:T(8,128)(2,1)S(1)} %maximum_select_fusion.refs_2_) | copy-start | bytes 737284
  34.1 17.0 %collective-permute-start.9 = (bf16[2,160,384]{2,1,0:T(8,128)(2,1)S(1)}, bf16[2,160,384]{2,1,0:T(8,128)(2,1)S(1)}, u32[]{:S(2)}, u32[]{:S(2)}) collective-permute-start(bf16[2,160,384]{2,1,0:T(8,128)(2,1)S(1)} %maximum_select_fusion.refs_2_), channel_id=1, source_target_pairs={{0,96},{32,0},{64,32},{96,64},{1,97},{33,1},{65,33},{97,65},{2,98}... | collective-permute-start | bytes 737288 | tf_op jit(solution)/shard_map/ppermute | solution.py:571
  37.0 14.0 %collective-permute-start.8 = (bf16[2,160,384]{2,1,0:T(8,128)(2,1)S(1)}, bf16[2,160,384]{2,1,0:T(8,128)(2,1)S(1)}, u32[]{:S(2)}, u32[]{:S(2)}) collective-permute-start(bf16[2,160,384]{2,1,0:T(8,128)(2,1)S(1)} %maximum_select_fusion.refs_2_), channel_id=1, source_target_pairs={{0,64},{32,96},{64,0},{96,32},{1,65},{33,97},{65,1},{97,33},{2,66}... | collective-permute-start | bytes 737288 | tf_op jit(solution)/shard_map/ppermute | solution.py:571
  37.2 14.4 %collective-permute-start.7 = (bf16[2,160,384]{2,1,0:T(8,128)(2,1)S(1)}, bf16[2,160,384]{2,1,0:T(8,128)(2,1)S(1)}, u32[]{:S(2)}, u32[]{:S(2)}) collective-permute-start(bf16[2,160,384]{2,1,0:T(8,128)(2,1)S(1)} %maximum_select_fusion.refs_2_), channel_id=1, source_target_pairs={{0,32},{32,64},{64,96},{96,0},{1,33},{33,65},{65,97},{97,1},{2,34}... | collective-permute-start | bytes 737288 | tf_op jit(solution)/shard_map/ppermute | solution.py:571
  39.3 10.7 %collective-permute-start.10 = (bf16[8,24,384]{2,1,0:T(8,128)(2,1)}, bf16[8,24,384]{2,1,0:T(8,128)(2,1)S(1)}, u32[]{:S(2)}, u32[]{:S(2)}) collective-permute-start(bf16[8,24,384]{2,1,0:T(8,128)(2,1)} %get-tuple-element.63), channel_id=1, source_target_pairs={{0,16},{16,32},{32,48},{48,64},{64,80},{80,96},{96,112},{1,17},{17... | collective-permute-start | bytes 442376 | tf_op jit(solution)/shard_map/ppermute | solution.py:52
  44.0 7.1 %collective-permute-start.11 = (bf16[8,24,384]{2,1,0:T(8,128)(2,1)}, bf16[8,24,384]{2,1,0:T(8,128)(2,1)S(1)}, u32[]{:S(2)}, u32[]{:S(2)}) collective-permute-start(bf16[8,24,384]{2,1,0:T(8,128)(2,1)} %get-tuple-element.64), channel_id=1, source_target_pairs={{16,0},{32,16},{48,32},{64,48},{80,64},{96,80},{112,96},{17,1},{33... | collective-permute-start | bytes 442376 | tf_op jit(solution)/shard_map/ppermute | solution.py:52
  50.0 38.7 %copy-start.11 = (bf16[8,24,384]{2,1,0:T(8,128)(2,1)}, bf16[8,24,384]{2,1,0:T(8,128)(2,1)S(1)}, u32[]{:S(2)}) copy-start(bf16[8,24,384]{2,1,0:T(8,128)(2,1)S(1)} %collective-permute-done.10.from_up_ref) | copy-start | bytes 442372
  51.0 37.6 %copy-start.12 = (bf16[8,24,384]{2,1,0:T(8,128)(2,1)}, bf16[8,24,384]{2,1,0:T(8,128)(2,1)S(1)}, u32[]{:S(2)}) copy-start(bf16[8,24,384]{2,1,0:T(8,128)(2,1)S(1)} %collective-permute-done.11.from_down_ref) | copy-start | bytes 442372
  51.1 0.7 copy-start.7
  51.1 0.8 copy-start.8
  51.6 0.7 copy-start.9
  88.7 4.7 %copy-start.10 = (bf16[208,384]{1,0:T(8,128)(2,1)S(1)}, bf16[208,384]{1,0:T(8,128)(2,1)}, u32[]{:S(2)}) copy-start(bf16[208,384]{1,0:T(8,128)(2,1)} %get-tuple-element.75) | copy-start | bytes 479236
  88.7 22.2 %all-to-all-start = ((bf16[8,208,384]{2,1,0:T(8,128)(2,1)}), bf16[8,208,384]{2,1,0:T(8,128)(2,1)S(1)}, u32[]{:S(2)}, u32[]{:S(2)}) async-start(bf16[8,208,384]{2,1,0:T(8,128)(2,1)} %attention.1), calls=%async_computation | async-start | bytes 2555904 | tf_op jit(solution)/shard_map/all_to_all | solution.py:589
  93.4 14.6 %collective-permute-start.12 = (bf16[208,384]{1,0:T(8,128)(2,1)S(1)}, bf16[208,384]{1,0:T(8,128)(2,1)S(1)}, u32[]{:S(2)}, u32[]{:S(2)}) collective-permute-start(bf16[208,384]{1,0:T(8,128)(2,1)S(1)} %copy-done.10), channel_id=1, source_target_pairs={{0,16},{16,0},{1,17},{17,1},{2,18},{18,2},{3,19},{19,3},{4,20},{20... | collective-permute-start | bytes 479240 | tf_op jit(solution)/shard_map/ppermute | solution.py:587
  108.0 2.9 %copy-start.2 = (bf16[208,384]{1,0:T(8,128)(2,1)}, bf16[208,384]{1,0:T(8,128)(2,1)S(1)}, u32[]{:S(2)}) copy-start(bf16[208,384]{1,0:T(8,128)(2,1)S(1)} %collective-permute-done.12.other_ref) | copy-start | bytes 479236
  110.9 1.0 copy-start
Sparse Core Ops, SparseCore 0:
  9.7 53.5 all-gather.2

commit v5 on v4

--- a/solution.py
+++ b/solution.py
@@ -26,6 +26,7 @@
 FINE_PITCH = 48
 KEY_TILE = 272
 KEY_CHUNK = 1024
+KEY_GROUPS = 4
 MAX_CHUNKS = 7
 KEY_ROWS = MAX_CHUNKS * KEY_CHUNK + KEY_CHUNK
 QUERY_BLOCK = 1056
@@ -88,8 +89,8 @@
     return jnp.where(inside, size_ref[jnp.clip(index, 0, count - 1)], 0)
 
 
-def keys_kernel(place_ref, row_ref, col_ref, token_ref, gain_ref, key_ref, pack_ref):
-    wide = col_ref[place_ref[1]]
+def keys_kernel(col_ref, token_ref, gain_ref, key_ref, pack_ref):
+    wide = col_ref[lax.axis_index("x") * lax.axis_size("z") + lax.axis_index("z")]
     pack_ref[...] = jnp.zeros_like(pack_ref)
     gain = gain_ref[...][None]
     for i in range(TILE_ROWS):
@@ -303,34 +304,42 @@
 
 def attention_kernel(
     place_ref, row_ref, col_ref, query_ref, tile_ref, out_ref,
-    key_ref, bias_ref, score_ref, top_ref, sum_ref, acc_ref, wide_ref, stat_ref,
+    stage_ref, key_ref, bias_ref, score_ref, top_ref, sum_ref, acc_ref, wide_ref, stat_ref, offset_ref, sem_ref,
 ):
     tiles = tile_ref.shape[0]
+    group = tiles // KEY_GROUPS
+    fetches = [
+        pltpu.make_async_copy(tile_ref.at[pl.ds(n * group, group)], stage_ref.at[pl.ds(n * group, group)], sem_ref.at[n])
+        for n in range(KEY_GROUPS)
+    ]
+    fetches[0].start()
     cols = col_ref.shape[0]
     y_at = place_ref[0] // 2
-    spot = lax.broadcasted_iota(jnp.int32, (16, KEY_CHUNK), 0) * KEY_CHUNK + lax.broadcasted_iota(jnp.int32, (16, KEY_CHUNK), 1)
-
-    def gather(t, carry):
+    spot = lax.broadcasted_iota(jnp.int32, (8, KEY_CHUNK), 0) * KEY_CHUNK + lax.broadcasted_iota(jnp.int32, (8, KEY_CHUNK), 1)
+
+    def locate(t, carry):
         offset, bias = carry
-        offset = pl.multiple_of(offset, 16)
-        key_ref[pl.ds(offset, KEY_TILE), :] = tile_ref[t]
+        offset_ref[t] = offset
         count = row_ref[2 * y_at + t // cols] * col_ref[t % cols]
         bias = jnp.where((spot >= offset) & (spot < offset + count), 0.0, bias)
         return offset + (count + 15) // 16 * 16, bias
 
-    tail, bias = lax.fori_loop(0, tiles, gather, (jnp.int32(0), jnp.full((16, KEY_CHUNK), masked_score, jnp.float32)))
-    tail = pl.multiple_of(tail, 16)
-    key_ref[pl.ds(tail, KEY_CHUNK), :] = jnp.zeros((KEY_CHUNK, key_ref.shape[1]), jnp.bfloat16)
+    tail, bias = lax.fori_loop(0, tiles, locate, (jnp.int32(0), jnp.full((8, KEY_CHUNK), masked_score, jnp.float32)))
+    offset_ref[tiles] = tail
     for j in range(MAX_CHUNKS):
         bias_ref[j] = bias[j : j + 1, :]
     chunk_count = (tail + KEY_CHUNK - 1) // KEY_CHUNK
+
+    def gather(t, carry):
+        key_ref[pl.ds(pl.multiple_of(offset_ref[t], 16), KEY_TILE), :] = stage_ref[t]
+        return carry
+
     total = wide_ref.shape[1]
     count = query_ref.shape[0]
     wide_ref[:, 0:FRONT, :] = jnp.zeros((3, FRONT, 128), jnp.float32)
     wide_ref[:, FRONT + count : total, :] = jnp.zeros((3, total - FRONT - count, 128), jnp.float32)
     stat_ref[0:FRONT, :] = jnp.zeros((FRONT, 128), jnp.float32)
     stat_ref[FRONT + count : total, :] = jnp.zeros((total - FRONT - count, 128), jnp.float32)
-    blocks = count // QUERY_BLOCK
     lane_groups = KEY_CHUNK // 128
 
     def keys_at(j):
@@ -357,35 +366,54 @@
         sum_ref[...] = sum_ref[...] + part
         acc_ref[...] = acc_ref[...] + jnp.dot(p.astype(jnp.bfloat16), keys_at(j), preferred_element_type=jnp.float32)
 
-    for i in range(blocks + 1):
-        if i < blocks:
-            top_ref[0] = jnp.full((QUERY_BLOCK, 128), masked_score, jnp.float32)
-        if i > 0:
-            last = 0
-            best = jnp.max(top_ref[last], axis=1, keepdims=True)
-            top_ref[last] = jnp.broadcast_to(best, (QUERY_BLOCK, 128))
-            sum_ref[...] = jnp.zeros_like(sum_ref)
-            acc_ref[...] = jnp.zeros_like(acc_ref)
-
-        def step(j, carry):
-            if i < blocks:
-                score_step(i, j)
-            if i > 0:
-                value_step(i - 1, j)
+    top_ref[0] = jnp.full((QUERY_BLOCK, 128), masked_score, jnp.float32)
+    done = jnp.int32(0)
+    for n in range(KEY_GROUPS):
+        fetches[n].wait()
+        if n + 1 < KEY_GROUPS:
+            fetches[n + 1].start()
+        lax.fori_loop(n * group, (n + 1) * group, gather, 0)
+        if n + 1 == KEY_GROUPS:
+            key_ref[pl.ds(pl.multiple_of(tail, 16), KEY_CHUNK), :] = jnp.zeros((KEY_CHUNK, key_ref.shape[1]), jnp.bfloat16)
+            ready = chunk_count
+        else:
+            ready = offset_ref[(n + 1) * group] // KEY_CHUNK
+
+        def score_chunk(j, carry):
+            score_step(0, j)
             return carry
 
-        lax.fori_loop(0, chunk_count, step, 0)
-        if i > 0:
-            denominator = jnp.sum(sum_ref[...], axis=1, keepdims=True)
-            lo = FRONT + (i - 1) * QUERY_BLOCK
-            put_rows(wide_ref, lo, acc_ref[...] / denominator)
-            level = top_ref[0] + jnp.log2(jnp.broadcast_to(denominator, (QUERY_BLOCK, 128)))
-            high = level.astype(jnp.bfloat16).astype(jnp.float32)
-            mid = (level - high).astype(jnp.bfloat16).astype(jnp.float32)
-            low = level - high - mid
-            lane = lax.broadcasted_iota(jnp.int32, (QUERY_BLOCK, 128), 1)
-            packed = jnp.where(lane == 0, high, jnp.where(lane == 1, mid, jnp.where(lane == 2, low, 0.0)))
-            stat_ref[lo : lo + QUERY_BLOCK, :] = packed
+        lax.fori_loop(done, ready, score_chunk, 0)
+        done = ready
+    best = jnp.max(top_ref[0], axis=1, keepdims=True)
+    top_ref[0] = jnp.broadcast_to(best, (QUERY_BLOCK, 128))
+    sum_ref[...] = jnp.zeros_like(sum_ref)
+    acc_ref[...] = jnp.zeros_like(acc_ref)
+
+    def value_chunk(j, carry):
+        value_step(0, j)
+        return carry
+
+    def value_pair(j, carry):
+        value_step(0, 2 * j)
+        value_step(0, 2 * j + 1)
+        return carry
+
+    lax.fori_loop(0, chunk_count // 2, value_pair, 0)
+
+    @pl.when(chunk_count % 2 == 1)
+    def _():
+        value_step(0, chunk_count - 1)
+
+    denominator = jnp.sum(sum_ref[...], axis=1, keepdims=True)
+    put_rows(wide_ref, FRONT, acc_ref[...] / denominator)
+    level = top_ref[0] + jnp.log2(jnp.broadcast_to(denominator, (QUERY_BLOCK, 128)))
+    high = level.astype(jnp.bfloat16).astype(jnp.float32)
+    mid = (level - high).astype(jnp.bfloat16).astype(jnp.float32)
+    low = level - high - mid
+    lane = lax.broadcasted_iota(jnp.int32, (QUERY_BLOCK, 128), 1)
+    packed = jnp.where(lane == 0, high, jnp.where(lane == 1, mid, jnp.where(lane == 2, low, 0.0)))
+    stat_ref[FRONT : FRONT + QUERY_BLOCK, :] = packed
     body = HALF_ROWS - 16
     select = (
         lax.broadcasted_iota(jnp.int32, (16, 128), 0) - STAT_ROW == lax.broadcasted_iota(jnp.int32, (16, 128), 1)
@@ -401,9 +429,11 @@
 
 
 def finish_kernel(
-    place_ref, row_ref, col_ref, part_ref, mine_ref, other_ref, vw_ref, ow_ref, gain_one_ref, sum_one_ref, sum_two_ref, one_ref, two_ref,
-    gain_two_ref, out_ref, act_ref, first_ref, shift_ref, product_ref, fine_ref, weight_one_ref, phase_ref, sem_ref,
+    place_ref, row_ref, col_ref, parts_ref, mine_ref, other_ref, vw_ref, ow_ref, gain_one_ref, sum_one_ref, sum_two_ref, one_ref, two_ref,
+    gain_two_ref, out_ref, part_ref, act_ref, first_ref, shift_ref, product_ref, fine_ref, weight_one_ref, phase_ref, sem_ref,
 ):
+    fetch_part = pltpu.make_async_copy(parts_ref, part_ref, sem_ref.at[2])
+    fetch_part.start()
     fetch_one = pltpu.make_async_copy(one_ref.at[pl.ds(2, 1)], weight_one_ref, sem_ref.at[0])
     fetch_two = pltpu.make_async_copy(two_ref, phase_ref, sem_ref.at[1])
     fetch_one.start()
@@ -411,17 +441,18 @@
     core = place_ref[2]
     tall = row_ref[place_ref[0]]
     wide = col_ref[place_ref[1]]
-    stat = lax.broadcasted_iota(jnp.int32, (16, 128), 0)
-    ones = ((stat >= STAT_ROW) & (stat < STAT_ROW + 3)).astype(jnp.bfloat16)
+    groups = part_ref.shape[0]
+    stat = lax.broadcasted_iota(jnp.int32, (16 * groups, 128 * groups), 0)
+    owner = jnp.right_shift(lax.broadcasted_iota(jnp.int32, (16 * groups, 128 * groups), 1), 7)
+    within = stat - owner * 16
+    ones = ((within >= STAT_ROW) & (within < STAT_ROW + 3)).astype(jnp.bfloat16)
+    fetch_part.wait()
+    stacked = jnp.concatenate([part_ref[g, HALF_ROWS - 16 : HALF_ROWS, 0:256] for g in range(groups)], axis=0)
+    spread = lax.dot_general(stacked, ones, (((0,), (0,)), ((), ())), preferred_element_type=jnp.float32)
     halves = []
     for side in range(2):
         sources = range(side, part_ref.shape[0], 2)
-        levels = [
-            lax.dot_general(
-                part_ref[g, HALF_ROWS - 16 : HALF_ROWS, 0:256], ones, (((0,), (0,)), ((), ())), preferred_element_type=jnp.float32
-            )[0:HALF_ROWS]
-            for g in sources
-        ]
+        levels = [spread[0:HALF_ROWS, g * 128 : (g + 1) * 128] for g in sources]
         best = jnp.maximum(jnp.maximum(levels[0], levels[1]), jnp.maximum(levels[2], levels[3]))
         weights = [jnp.exp2(level - best) for level in levels]
         total = (weights[0] + weights[1]) + (weights[2] + weights[3])
@@ -512,12 +543,13 @@
         [place, row_sizes, col_sizes, queries, tiles],
         [jax.ShapeDtypeStruct((8, HALF_ROWS, channels), jnp.bfloat16)],
         [
-            pltpu.VMEM((KEY_ROWS, channels), jnp.bfloat16), scratch(MAX_CHUNKS, 1, KEY_CHUNK),
-            scratch(1, MAX_CHUNKS, QUERY_BLOCK, KEY_CHUNK),
+            pltpu.VMEM(tiles.shape, jnp.bfloat16), pltpu.VMEM((KEY_ROWS, channels), jnp.bfloat16),
+            scratch(MAX_CHUNKS, 1, KEY_CHUNK), scratch(1, MAX_CHUNKS, QUERY_BLOCK, KEY_CHUNK),
             scratch(1, QUERY_BLOCK, 128), scratch(QUERY_BLOCK, 128), scratch(QUERY_BLOCK, channels),
-            scratch(3, WIDE_ROWS, 128), scratch(WIDE_ROWS, 128),
+            scratch(3, WIDE_ROWS, 128), scratch(WIDE_ROWS, 128), pltpu.SMEM((tiles.shape[0] + 1,), jnp.int32),
+            pltpu.SemaphoreType.DMA((KEY_GROUPS,)),
         ],
-        3, "attention", 4 * LAT_ROWS * HALF * channels * KEY_ROWS,
+        3, "attention", 4 * LAT_ROWS * HALF * channels * KEY_ROWS, (4,),
     )
     return parts
 
@@ -541,7 +573,7 @@
     message = 160
     place_args = [place, row_sizes, col_sizes]
     (own_keys,) = call(
-        keys_kernel, [*place_args, tokens, norm_gain], [shape(KEY_TILE, channels)], [scratch(3, 304, 128)], 3, "keys"
+        keys_kernel, [col_sizes, tokens, norm_gain], [shape(KEY_TILE, channels)], [scratch(3, 304, 128)], 1, "keys"
     )
     tiles = lax.all_gather(own_keys, ("core", "x", "z"), axis=0, tiled=False)
     to_right, to_left, to_right_far, to_left_far = call(
@@ -609,11 +641,12 @@
         ],
         [shape(FINE_ROWS, FINE_COLS, channels_out)],
         [
-            scratch(3, EXT_ROWS * EXT_COLS, 128), narrow(EXT_ROWS, EXT_COLS, channels), scratch(3, 640, 128),
+            narrow(8, HALF_ROWS, channels), scratch(3, EXT_ROWS * EXT_COLS, 128), narrow(EXT_ROWS, EXT_COLS, channels),
+            scratch(3, 640, 128),
             scratch(4, 2, TILE_ROWS * EXT_COLS + 8, 128), scratch(2, FINE_ROWS * FINE_PITCH, 128),
-            narrow(1, 3, 3, channels, channels), narrow(4, 4, channels_out, channels), pltpu.SemaphoreType.DMA((2,)),
+            narrow(1, 3, 3, channels, channels), narrow(4, 4, channels_out, channels), pltpu.SemaphoreType.DMA((3,)),
         ],
-        3, "finish", 0, (11, 12),
+        3, "finish", 0, (3, 11, 12),
     )
     return decoded
 

time: 129 us -> 127 us (0.984)
  Pallas kernels: 63.1 us -> 56.3 us
  starting transfers between devices: 22.9 us -> 28 us
    pallas_call x7, Pallas kernels: 63.1 us -> 56.3 us  [call(): pl.pallas_call(body, in_specs=[smem if i < smem_count else pl.BlockSpec(m...]
    all_to_all x1, starting transfers between devices: 4.69 us -> 9.97 us  [local(): parts = lax.all_to_all(parts, ROWS, 0, 0)]
  transfers between devices with their start and end apart: 11 -> 11, of which waited for: 7 -> 7; matrix products, arithmetic and copies ran while one was open for 3% -> 4% of each run, Pallas kernels for 21% -> 21%
where the time goes in v5:
time: 127 us
  Pallas kernels  56.3 us (44%)
  starting transfers between devices  28 us (22%)
  waiting for transfers between devices  20.4 us (16%)
  between operations  14.9 us (12%)
  local copies, waits for them, and re-layouts  4.27 us (3%)
  other arithmetic  2.93 us (2%)
    pallas_call x7, Pallas kernels, call(): pl.pallas_call(body, in_specs=[smem if i < smem_count else pl.BlockSpec(m...  56.3 us
    ppermute x4, starting transfers between devices, hop(): return lax.ppermute(value, axes, pairs)  12.4 us
    all_to_all x1, starting transfers between devices, local(): parts = lax.all_to_all(parts, ROWS, 0, 0)  9.97 us
    ppermute x4, waiting for transfers between devices, hop(): return lax.ppermute(value, axes, pairs)  8.86 us
    all_gather x1, waiting for transfers between devices, local(): tiles = lax.all_gather(own_keys, ('core', 'x', 'z'), axis=0, tiled=False)  6.78 us
    unnamed x27, local copies, waits for them, and re-layouts  4.27 us
    ppermute x3, starting transfers between devices, local(): lax.ppermute(pair, 'y', [(i, (i + k) % n_y) for i in range(n_y)])  3.9 us
    all_to_all x1, waiting for transfers between devices, local(): parts = lax.all_to_all(parts, ROWS, 0, 0)  3.1 us
  transfers between devices with their start and end apart: 11, of which 7 were waited for; matrix products, arithmetic and copies ran while one was open for 4% of the time, Pallas kernels for 21%

profile of v5, /device:TPU:1, one launch (start us, length us, event | category | flops | bytes accessed | tf_op | source)
XLA Modules:
  0.0 126.8 jit_solution(2270868884614097456)
XLA Ops:
  6.5 1.8 %keys.1 = bf16[272,384]{1,0:T(8,128)(2,1)} custom-call(s32[16]{0:T(128)} %col_ref.9, bf16[13,20,384]{2,1,0:T(8,128)(2,1)} %token_ref.5, f32[384]{0:T(512)} %gain_ref.1), custom_call_target="tpu_custom_call" | custom-call | bytes 410176 | tf_op jit(solution)/shard_map/keys/pallas_call | solution.py:524
  8.4 1.8 %copy.16.one_ref = bf16[2,13,20,384]{3,2,1,0:T(8,128)(2,1)} copy(bf16[2,13,20,384]{3,0,2,1:T(2,128)(2,1)} %param.26) | data formatting | bytes 798720 | tf_op args[8]
  10.8 3.0 %edges.1 = (bf16[160,384]{1,0:T(8,128)(2,1)}, bf16[160,384]{1,0:T(8,128)(2,1)}, bf16[48,384]{1,0:T(8,128)(2,1)S(1)}, bf16[48,384]{1,0:T(8,128)(2,1)S(1)}) custom-call(s32[3]{0:T(128)} %pad_add_fusion.place_ref.refs_0_, s32[8]{0:T(128)} %row_ref.9, s32[16]{0:T(128)} %col_ref.9, bf16[13,20,384]{2,1,0:T(8,128)(2,1)} %token_ref.5, ...), custom_call_target="tpu_custom_call" | custom-call | bytes 2516076 | tf_op jit(solution)/shard_map/edges/pallas_call | solution.py:524
  13.8 4.5 %collective-permute-start.4 = (bf16[160,384]{1,0:T(8,128)(2,1)}, bf16[160,384]{1,0:T(8,128)(2,1)S(1)}, u32[]{:S(2)}, u32[]{:S(2)}) collective-permute-start(bf16[160,384]{1,0:T(8,128)(2,1)} %get-tuple-element.55), channel_id=1, source_target_pairs={{0,1},{1,2},{2,3},{3,4},{4,5},{5,6},{6,7},{7,8},{8,9},{9,10},{10,1... | collective-permute-start | bytes 368648 | tf_op jit(solution)/shard_map/ppermute | solution.py:53
  18.3 1.3 %collective-permute-start.5 = (bf16[160,384]{1,0:T(8,128)(2,1)}, bf16[160,384]{1,0:T(8,128)(2,1)S(1)}, u32[]{:S(2)}, u32[]{:S(2)}) collective-permute-start(bf16[160,384]{1,0:T(8,128)(2,1)} %get-tuple-element.56), channel_id=1, source_target_pairs={{1,0},{2,1},{3,2},{4,3},{5,4},{6,5},{7,6},{8,7},{9,8},{10,9},{11,1... | collective-permute-start | bytes 368648 | tf_op jit(solution)/shard_map/ppermute | solution.py:53
  21.0 3.7 %collective-permute-done.5.from_right_ref = bf16[160,384]{1,0:T(8,128)(2,1)S(1)} collective-permute-done((bf16[160,384]{1,0:T(8,128)(2,1)}, bf16[160,384]{1,0:T(8,128)(2,1)S(1)}, u32[]{:S(2)}, u32[]{:S(2)}) %collective-permute-start.5) | collective-permute-done | bytes 122912 | tf_op jit(solution)/shard_map/ppermute | solution.py:53
  25.3 4.9 %columns.1 = (bf16[160,384]{1,0:T(8,128)(2,1)}, bf16[160,384]{1,0:T(8,128)(2,1)}, bf16[26,24,384]{2,1,0:T(8,128)(2,1)}, bf16[52,48,384]{2,1,0:T(8,128)(2,1)}, bf...) custom-call(s32[3]{0:T(128)} %pad_add_fusion.place_ref.refs_0_, ...), custom_call_target="tpu_custom_call" | custom-call | bytes 5526636 | tf_op jit(solution)/shard_map/columns/pallas_call | solution.py:524
  30.2 1.7 %collective-permute-start.6 = (bf16[160,384]{1,0:T(8,128)(2,1)}, bf16[160,384]{1,0:T(8,128)(2,1)S(1)}, u32[]{:S(2)}, u32[]{:S(2)}) collective-permute-start(bf16[160,384]{1,0:T(8,128)(2,1)} %get-tuple-element.62), channel_id=1, source_target_pairs={{0,16},{16,0},{1,17},{17,1},{2,18},{18,2},{3,19},{19,3},{4,20},{20... | collective-permute-start | bytes 368648 | tf_op jit(solution)/shard_map/ppermute | solution.py:601
  31.8 1.2 collective-permute-done.6
  33.0 1.0 maximum_select_fusion.refs_2_
  34.1 3.0 %collective-permute-start.9 = (bf16[2,160,384]{2,1,0:T(8,128)(2,1)S(1)}, bf16[2,160,384]{2,1,0:T(8,128)(2,1)S(1)}, u32[]{:S(2)}, u32[]{:S(2)}) collective-permute-start(bf16[2,160,384]{2,1,0:T(8,128)(2,1)S(1)} %maximum_select_fusion.refs_2_), channel_id=1, source_target_pairs={{0,96},{32,0},{64,32},{96,64},{1,97},{33,1},{65,33},{97,65},{2,98}... | collective-permute-start | bytes 737288 | tf_op jit(solution)/shard_map/ppermute | solution.py:603
  37.2 0.8 collective-permute-start.7
  39.3 4.7 %collective-permute-start.10 = (bf16[8,24,384]{2,1,0:T(8,128)(2,1)}, bf16[8,24,384]{2,1,0:T(8,128)(2,1)S(1)}, u32[]{:S(2)}, u32[]{:S(2)}) collective-permute-start(bf16[8,24,384]{2,1,0:T(8,128)(2,1)} %get-tuple-element.63), channel_id=1, source_target_pairs={{0,16},{16,32},{32,48},{48,64},{64,80},{80,96},{96,112},{1,17},{17... | collective-permute-start | bytes 442376 | tf_op jit(solution)/shard_map/ppermute | solution.py:53
  44.0 1.9 %collective-permute-start.11 = (bf16[8,24,384]{2,1,0:T(8,128)(2,1)}, bf16[8,24,384]{2,1,0:T(8,128)(2,1)S(1)}, u32[]{:S(2)}, u32[]{:S(2)}) collective-permute-start(bf16[8,24,384]{2,1,0:T(8,128)(2,1)} %get-tuple-element.64), channel_id=1, source_target_pairs={{16,0},{32,16},{48,32},{64,48},{80,64},{96,80},{112,96},{17,1},{33... | collective-permute-start | bytes 442376 | tf_op jit(solution)/shard_map/ppermute | solution.py:53
  45.9 4.1 %collective-permute-done.10.from_up_ref = bf16[8,24,384]{2,1,0:T(8,128)(2,1)S(1)} collective-permute-done((bf16[8,24,384]{2,1,0:T(8,128)(2,1)}, bf16[8,24,384]{2,1,0:T(8,128)(2,1)S(1)}, u32[]{:S(2)}, u32[]{:S(2)}) %collective-permute-start.10) | collective-permute-done | bytes 147488 | tf_op jit(solution)/shard_map/ppermute | solution.py:53
  50.0 1.1 collective-permute-done.11.from_down_ref
  52.3 4.2 %queries.1 = (bf16[1056,384]{1,0:T(8,128)(2,1)}, bf16[208,384]{1,0:T(8,128)(2,1)}, bf16[208,384]{1,0:T(8,128)(2,1)}) custom-call(s32[3]{0:T(128)} %pad_add_fusion.place_ref.refs_0_, s32[8]{0:T(128)} %row_ref.9, bf16[2,160,384]{2,1,0:T(8,128)(2,1)} %copy-done.1, bf16[2,160,384]{2,1,0:T(8,128)(2,1)} %copy-done.9, bf16[2,160,384]{2,1,0:T(8,128)(2,1)} %copy-done.8, ...), custom_call_target="tpu_custom_call" | custom-call | flops 622854144 | bytes 2704940 | tf_op jit(solution)/shard_map/queries/pallas_call | solution.py:524
  56.5 6.8 %all-gather.3.cloned.1.call-done = bf16[8704,384]{1,0:T(8,128)(2,1)} async-done(((bf16[272,384]{1,0:T(8,128)(2,1)}), bf16[8704,384]{1,0:T(8,128)(2,1)}) %all-gather.3.cloned.1.call-update) | async-done | bytes 6684688 | tf_op jit(solution)/shard_map/all_gather | solution.py:578
  63.3 19.0 %attention.1 = bf16[8,208,384]{2,1,0:T(8,128)(2,1)} custom-call(s32[3]{0:T(128)} %pad_add_fusion.place_ref.refs_0_, s32[8]{0:T(128)} %row_ref.9, s32[16]{0:T(128)} %col_ref.9, bf16[1056,384]{1,0:T(8,128)(2,1)} %get-tuple-element.73.query_ref, bf16[32,272,384]{2,1,0:T(8,128)(2,1)} %bitcast.9), custom_call_target="tpu_custom_call" | custom-call | flops 13287555072 | bytes 8773740 | tf_op jit(solution)/shard_map/attention/pallas_call | solution.py:524
  82.4 10.0 %all-to-all-start = ((bf16[8,208,384]{2,1,0:T(8,128)(2,1)}), bf16[8,208,384]{2,1,0:T(8,128)(2,1)S(1)}, u32[]{:S(2)}, u32[]{:S(2)}) async-start(bf16[8,208,384]{2,1,0:T(8,128)(2,1)} %attention.1), calls=%async_computation | async-start | bytes 2555904 | tf_op jit(solution)/shard_map/all_to_all | solution.py:621
  92.4 14.3 %prior.1 = (f32[360,384]{1,0:T(8,128)}, f32[1248,192]{1,0:T(8,128)}, bf16[4,4,192,384]{3,2,1,0:T(8,128)(2,1)}) custom-call(s32[3]{0:T(128)} %pad_add_fusion.place_ref.refs_0_, s32[8]{0:T(128)} %row_ref.9, bf16[26,24,384]{2,1,0:T(8,128)(2,1)} %get-tuple-element.76.prior_ref, bf16[52,48,384]{2,1,0:T(8,128)(2,1)} %get-tuple-element.77.fine_ref, ...), custom_call_target="tpu_custom_call" | custom-call | flops 5223481344 | bytes 18579500 | tf_op jit(solution)/shard_map/prior/pallas_call | solution.py:524
  106.8 3.1 %all-to-all-done.parts_ref = bf16[8,208,384]{2,1,0:T(8,128)(2,1)S(1)} async-done(((bf16[8,208,384]{2,1,0:T(8,128)(2,1)}), bf16[8,208,384]{2,1,0:T(8,128)(2,1)S(1)}, u32[]{:S(2)}, u32[]{:S(2)}) %all-to-all-start) | async-done | bytes 1277984 | tf_op jit(solution)/shard_map/all_to_all | solution.py:621
  109.9 1.0 copy-done
  110.9 9.0 %finish.1 = bf16[26,40,192]{2,1,0:T(8,128)(2,1)} custom-call(s32[3]{0:T(128)} %pad_add_fusion.place_ref.refs_0_, s32[8]{0:T(128)} %row_ref.9, s32[16]{0:T(128)} %col_ref.9, bf16[8,208,384]{2,1,0:T(8,128)(2,1)} %copy-done, bf16[208,384]{1,0:T(8,128)(2,1)} %get-tuple-element.74.mine_ref, bf16[208,384]{1,0:T(8,128)(2,1)} %copy-done.2, bf16[384,384]{1,0:T(8,128)(2,1)} %vw_ref.1, ...), custom_call_target="tpu_custom_call" | custom-call | bytes 14423148 | tf_op jit(solution)/shard_map/finish/pallas_call | solution.py:524
  (39 shorter events, 4.1 us)
Async XLA Ops:
  6.5 13.1 %copy-start.5 = (s32[16]{0:T(128)S(1)}, s32[16]{0:T(128)}, u32[]{:S(2)}) copy-start(s32[16]{0:T(128)} %col_ref.9) | copy-start | bytes 196
  6.5 56.8 %all-gather.3.cloned.1.call-start = ((), (), s32[]{:S(2)}) async-start(), calls=%async_computation.1 | async-start | bytes 6893568 | tf_op jit(solution)/shard_map/all_gather | solution.py:578
  13.8 24.2 %copy-start.6 = (s32[8]{0:T(128)S(1)}, s32[8]{0:T(128)}, u32[]{:S(2)}) copy-start(s32[8]{0:T(128)} %row_ref.9) | copy-start | bytes 100
  13.8 7.1 %collective-permute-start.4 = (bf16[160,384]{1,0:T(8,128)(2,1)}, bf16[160,384]{1,0:T(8,128)(2,1)S(1)}, u32[]{:S(2)}, u32[]{:S(2)}) collective-permute-start(bf16[160,384]{1,0:T(8,128)(2,1)} %get-tuple-element.55), channel_id=1, source_target_pairs={{0,1},{1,2},{2,3},{3,4},{4,5},{5,6},{6,7},{7,8},{8,9},{9,10},{10,1... | collective-permute-start | bytes 368648 | tf_op jit(solution)/shard_map/ppermute | solution.py:53
  18.3 6.4 %collective-permute-start.5 = (bf16[160,384]{1,0:T(8,128)(2,1)}, bf16[160,384]{1,0:T(8,128)(2,1)S(1)}, u32[]{:S(2)}, u32[]{:S(2)}) collective-permute-start(bf16[160,384]{1,0:T(8,128)(2,1)} %get-tuple-element.56), channel_id=1, source_target_pairs={{1,0},{2,1},{3,2},{4,3},{5,4},{6,5},{7,6},{8,7},{9,8},{10,9},{11,1... | collective-permute-start | bytes 368648 | tf_op jit(solution)/shard_map/ppermute | solution.py:53
  20.9 3.7 %copy-start.3 = (bf16[160,384]{1,0:T(8,128)(2,1)}, bf16[160,384]{1,0:T(8,128)(2,1)S(1)}, u32[]{:S(2)}) copy-start(bf16[160,384]{1,0:T(8,128)(2,1)S(1)} %collective-permute-done.4.from_left_ref) | copy-start | bytes 368644
  24.7 0.6 copy-start.4
  30.2 2.8 %collective-permute-start.6 = (bf16[160,384]{1,0:T(8,128)(2,1)}, bf16[160,384]{1,0:T(8,128)(2,1)S(1)}, u32[]{:S(2)}, u32[]{:S(2)}) collective-permute-start(bf16[160,384]{1,0:T(8,128)(2,1)} %get-tuple-element.62), channel_id=1, source_target_pairs={{0,16},{16,0},{1,17},{17,1},{2,18},{18,2},{3,19},{19,3},{4,20},{20... | collective-permute-start | bytes 368648 | tf_op jit(solution)/shard_map/ppermute | solution.py:601
  34.1 17.5 %copy-start.1 = (bf16[2,160,384]{2,1,0:T(8,128)(2,1)}, bf16[2,160,384]{2,1,0:T(8,128)(2,1)S(1)}, u32[]{:S(2)}) copy-start(bf16[2,160,384]{2,1,0:T(8,128)(2,1)S(1)} %maximum_select_fusion.refs_2_) | copy-start | bytes 737284
  34.1 17.0 %collective-permute-start.9 = (bf16[2,160,384]{2,1,0:T(8,128)(2,1)S(1)}, bf16[2,160,384]{2,1,0:T(8,128)(2,1)S(1)}, u32[]{:S(2)}, u32[]{:S(2)}) collective-permute-start(bf16[2,160,384]{2,1,0:T(8,128)(2,1)S(1)} %maximum_select_fusion.refs_2_), channel_id=1, source_target_pairs={{0,96},{32,0},{64,32},{96,64},{1,97},{33,1},{65,33},{97,65},{2,98}... | collective-permute-start | bytes 737288 | tf_op jit(solution)/shard_map/ppermute | solution.py:603
  37.0 14.0 %collective-permute-start.8 = (bf16[2,160,384]{2,1,0:T(8,128)(2,1)S(1)}, bf16[2,160,384]{2,1,0:T(8,128)(2,1)S(1)}, u32[]{:S(2)}, u32[]{:S(2)}) collective-permute-start(bf16[2,160,384]{2,1,0:T(8,128)(2,1)S(1)} %maximum_select_fusion.refs_2_), channel_id=1, source_target_pairs={{0,64},{32,96},{64,0},{96,32},{1,65},{33,97},{65,1},{97,33},{2,66}... | collective-permute-start | bytes 737288 | tf_op jit(solution)/shard_map/ppermute | solution.py:603
  37.2 14.3 %collective-permute-start.7 = (bf16[2,160,384]{2,1,0:T(8,128)(2,1)S(1)}, bf16[2,160,384]{2,1,0:T(8,128)(2,1)S(1)}, u32[]{:S(2)}, u32[]{:S(2)}) collective-permute-start(bf16[2,160,384]{2,1,0:T(8,128)(2,1)S(1)} %maximum_select_fusion.refs_2_), channel_id=1, source_target_pairs={{0,32},{32,64},{64,96},{96,0},{1,33},{33,65},{65,97},{97,1},{2,34}... | collective-permute-start | bytes 737288 | tf_op jit(solution)/shard_map/ppermute | solution.py:603
  39.3 10.7 %collective-permute-start.10 = (bf16[8,24,384]{2,1,0:T(8,128)(2,1)}, bf16[8,24,384]{2,1,0:T(8,128)(2,1)S(1)}, u32[]{:S(2)}, u32[]{:S(2)}) collective-permute-start(bf16[8,24,384]{2,1,0:T(8,128)(2,1)} %get-tuple-element.63), channel_id=1, source_target_pairs={{0,16},{16,32},{32,48},{48,64},{64,80},{80,96},{96,112},{1,17},{17... | collective-permute-start | bytes 442376 | tf_op jit(solution)/shard_map/ppermute | solution.py:53
  44.0 7.1 %collective-permute-start.11 = (bf16[8,24,384]{2,1,0:T(8,128)(2,1)}, bf16[8,24,384]{2,1,0:T(8,128)(2,1)S(1)}, u32[]{:S(2)}, u32[]{:S(2)}) collective-permute-start(bf16[8,24,384]{2,1,0:T(8,128)(2,1)} %get-tuple-element.64), channel_id=1, source_target_pairs={{16,0},{32,16},{48,32},{64,48},{80,64},{96,80},{112,96},{17,1},{33... | collective-permute-start | bytes 442376 | tf_op jit(solution)/shard_map/ppermute | solution.py:53
  50.0 32.4 %copy-start.11 = (bf16[8,24,384]{2,1,0:T(8,128)(2,1)}, bf16[8,24,384]{2,1,0:T(8,128)(2,1)S(1)}, u32[]{:S(2)}) copy-start(bf16[8,24,384]{2,1,0:T(8,128)(2,1)S(1)} %collective-permute-done.10.from_up_ref) | copy-start | bytes 442372
  51.1 31.3 %copy-start.12 = (bf16[8,24,384]{2,1,0:T(8,128)(2,1)}, bf16[8,24,384]{2,1,0:T(8,128)(2,1)S(1)}, u32[]{:S(2)}) copy-start(bf16[8,24,384]{2,1,0:T(8,128)(2,1)S(1)} %collective-permute-done.11.from_down_ref) | copy-start | bytes 442372
  51.1 0.7 copy-start.7
  51.1 0.8 copy-start.8
  51.6 0.7 copy-start.9
  82.4 10.0 %copy-start.10 = (bf16[208,384]{1,0:T(8,128)(2,1)S(1)}, bf16[208,384]{1,0:T(8,128)(2,1)}, u32[]{:S(2)}) copy-start(bf16[208,384]{1,0:T(8,128)(2,1)} %get-tuple-element.75) | copy-start | bytes 479236
  82.4 27.5 %all-to-all-start = ((bf16[8,208,384]{2,1,0:T(8,128)(2,1)}), bf16[8,208,384]{2,1,0:T(8,128)(2,1)S(1)}, u32[]{:S(2)}, u32[]{:S(2)}) async-start(bf16[8,208,384]{2,1,0:T(8,128)(2,1)} %attention.1), calls=%async_computation | async-start | bytes 2555904 | tf_op jit(solution)/shard_map/all_to_all | solution.py:621
  92.4 14.4 %collective-permute-start.12 = (bf16[208,384]{1,0:T(8,128)(2,1)S(1)}, bf16[208,384]{1,0:T(8,128)(2,1)S(1)}, u32[]{:S(2)}, u32[]{:S(2)}) collective-permute-start(bf16[208,384]{1,0:T(8,128)(2,1)S(1)} %copy-done.10), channel_id=1, source_target_pairs={{0,16},{16,0},{1,17},{17,1},{2,18},{18,2},{3,19},{19,3},{4,20},{20... | collective-permute-start | bytes 479240 | tf_op jit(solution)/shard_map/ppermute | solution.py:619
  106.8 3.1 %copy-start.2 = (bf16[208,384]{1,0:T(8,128)(2,1)}, bf16[208,384]{1,0:T(8,128)(2,1)S(1)}, u32[]{:S(2)}) copy-start(bf16[208,384]{1,0:T(8,128)(2,1)S(1)} %collective-permute-done.12.other_ref) | copy-start | bytes 479236
  109.9 1.0 copy-start
Sparse Core Ops, SparseCore 0:
  9.7 53.5 all-gather.2

commit v6 on v5

--- a/solution.py
+++ b/solution.py
@@ -36,6 +36,7 @@
 FINE_STEP = 13
 TALL_TILE = 160
 VMEM_BYTES = 60 * 1024 * 1024
+SMALL_BYTES = VMEM_BYTES
 NEAR = 48
 
 
@@ -429,15 +430,17 @@
 
 
 def finish_kernel(
-    place_ref, row_ref, col_ref, parts_ref, mine_ref, other_ref, vw_ref, ow_ref, gain_one_ref, sum_one_ref, sum_two_ref, one_ref, two_ref,
-    gain_two_ref, out_ref, part_ref, act_ref, first_ref, shift_ref, product_ref, fine_ref, weight_one_ref, phase_ref, sem_ref,
+    place_ref, row_ref, col_ref, part_ref, mine_ref, other_ref, vw_ref, ow_ref, gain_one_ref, far_one_ref, far_two_ref, one_ref, two_ref,
+    gain_two_ref, out_ref, act_ref, first_ref, shift_ref, product_ref, fine_ref, weight_one_ref, phase_ref, sum_one_ref, sum_two_ref, sem_ref,
 ):
-    fetch_part = pltpu.make_async_copy(parts_ref, part_ref, sem_ref.at[2])
-    fetch_part.start()
     fetch_one = pltpu.make_async_copy(one_ref.at[pl.ds(2, 1)], weight_one_ref, sem_ref.at[0])
     fetch_two = pltpu.make_async_copy(two_ref, phase_ref, sem_ref.at[1])
+    fetch_sum_one = pltpu.make_async_copy(far_one_ref, sum_one_ref, sem_ref.at[2])
+    fetch_sum_two = pltpu.make_async_copy(far_two_ref, sum_two_ref, sem_ref.at[3])
     fetch_one.start()
+    fetch_sum_one.start()
     fetch_two.start()
+    fetch_sum_two.start()
     core = place_ref[2]
     tall = row_ref[place_ref[0]]
     wide = col_ref[place_ref[1]]
@@ -446,7 +449,6 @@
     owner = jnp.right_shift(lax.broadcasted_iota(jnp.int32, (16 * groups, 128 * groups), 1), 7)
     within = stat - owner * 16
     ones = ((within >= STAT_ROW) & (within < STAT_ROW + 3)).astype(jnp.bfloat16)
-    fetch_part.wait()
     stacked = jnp.concatenate([part_ref[g, HALF_ROWS - 16 : HALF_ROWS, 0:256] for g in range(groups)], axis=0)
     spread = lax.dot_general(stacked, ones, (((0,), (0,)), ((), ())), preferred_element_type=jnp.float32)
     halves = []
@@ -484,6 +486,7 @@
     rows = TILE_ROWS + 2
     fetch_one.wait()
     total = coarse_conv(lambda f, a, n: first_ref[a : a + n], weight_one_ref, shift_ref, 1)
+    fetch_sum_one.wait()
     y_one = (total + sum_one_ref[...]).astype(jnp.bfloat16)
     act = silu(rms_scale(y_one, gain_two_ref[...][None])).astype(jnp.bfloat16).astype(jnp.float32)
     put_rows(act_ref, 0, act)
@@ -511,13 +514,14 @@
                     next_ = product_ref[2 * q + 1, g, pl.ds(i * EXT_COLS + q + 1, EXT_COLS), :]
                     fine_ref[g, pl.ds((2 * i + p) * FINE_PITCH + q, EXT_COLS, 2), :] = near + next_
     col = lax.broadcasted_iota(jnp.int32, (FINE_COLS, 192), 0)
+    fetch_sum_two.wait()
     for r in range(FINE_ROWS):
         line = get_rows(fine_ref, r * FINE_PITCH, FINE_COLS)[:, 0:192] + sum_two_ref[r * FINE_PITCH : r * FINE_PITCH + FINE_COLS, :]
         usable = (col < 2 * wide) & (r < 2 * tall)
         out_ref[r] = jnp.where(usable, line, 0.0).astype(jnp.bfloat16)
 
 
-def call(body, inputs, outs, scratch, smem_count, name, flops=0, far=()):
+def call(body, inputs, outs, scratch, smem_count, name, flops=0, far=(), near=(), limit=SMALL_BYTES):
     smem = pl.BlockSpec(memory_space=pltpu.SMEM)
     vmem = pl.BlockSpec(memory_space=pltpu.VMEM)
     moved = sum(math.prod(v.shape) * v.dtype.itemsize for v in list(inputs) + list(outs))
@@ -529,10 +533,10 @@
         out_specs=[vmem] * len(outs),
         out_shape=outs,
         scratch_shapes=scratch,
-        compiler_params=pltpu.CompilerParams(vmem_limit_bytes=VMEM_BYTES),
+        compiler_params=pltpu.CompilerParams(vmem_limit_bytes=limit),
         cost_estimate=pl.CostEstimate(flops=int(flops), transcendentals=0, bytes_accessed=int(moved)),
         name=name,
-    )(*inputs)
+    )(*[pltpu.with_memory_space_constraint(v, pltpu.VMEM) if i in near else v for i, v in enumerate(inputs)])
 
 
 def attend(place, row_sizes, col_sizes, queries, tiles):
@@ -549,7 +553,7 @@
             scratch(3, WIDE_ROWS, 128), scratch(WIDE_ROWS, 128), pltpu.SMEM((tiles.shape[0] + 1,), jnp.int32),
             pltpu.SemaphoreType.DMA((KEY_GROUPS,)),
         ],
-        3, "attention", 4 * LAT_ROWS * HALF * channels * KEY_ROWS, (4,),
+        3, "attention", 4 * LAT_ROWS * HALF * channels * KEY_ROWS, (4,), (), VMEM_BYTES,
     )
     return parts
 
@@ -595,7 +599,7 @@
             shape(2, EXT_COLS, channels), shape(2, EXT_COLS, channels),
         ],
         [scratch(3, 3 * TILE_ROWS * EXT_COLS, 128), scratch(3, 2 * FINE_ROWS * FINE_PITCH, 128), scratch(3, TALL_TILE, 128)],
-        3, "columns",
+        3, "columns", 0, (), (6, 7),
     )
     swap = [(0, 1), (1, 0)]
     sibling = lax.ppermute(other, "core", swap)
@@ -614,7 +618,7 @@
         [place, row_sizes, *strips, norm_gain, query_weight, key_weight],
         [shape(LAT_ROWS * HALF, channels), shape(HALF_ROWS, channels), shape(HALF_ROWS, channels)],
         [scratch(3, WIDE_ROWS, 128)],
-        2, "queries", 4 * LAT_ROWS * HALF * channels * channels,
+        2, "queries", 4 * LAT_ROWS * HALF * channels * channels, (), (2, 3, 4, 5),
     )
     frame_other = lax.ppermute(frame_other, "core", swap)
     parts = attend(place, row_sizes, col_sizes, queries, tiles.reshape(2 * n_col, KEY_TILE, channels))
@@ -632,7 +636,7 @@
             narrow(2, EXT_ROWS, EXT_COLS, channels), narrow(2, FINE_ROWS + 2, FINE_PITCH, channels), scratch(3, 640, 128),
             narrow(2, 3, 3, channels, channels), narrow(3, 3, 3, channels_out, channels), pltpu.SemaphoreType.DMA((2,)),
         ],
-        2, "prior", 2 * 18 * channels * (360 * 384 + 1248 * 192), (8, 9),
+        2, "prior", 2 * 18 * channels * (360 * 384 + 1248 * 192), (8, 9), (4, 5),
     )
     (decoded,) = call(
         finish_kernel,
@@ -641,12 +645,13 @@
         ],
         [shape(FINE_ROWS, FINE_COLS, channels_out)],
         [
-            narrow(8, HALF_ROWS, channels), scratch(3, EXT_ROWS * EXT_COLS, 128), narrow(EXT_ROWS, EXT_COLS, channels),
+            scratch(3, EXT_ROWS * EXT_COLS, 128), narrow(EXT_ROWS, EXT_COLS, channels),
             scratch(3, 640, 128),
             scratch(4, 2, TILE_ROWS * EXT_COLS + 8, 128), scratch(2, FINE_ROWS * FINE_PITCH, 128),
-            narrow(1, 3, 3, channels, channels), narrow(4, 4, channels_out, channels), pltpu.SemaphoreType.DMA((3,)),
+            narrow(1, 3, 3, channels, channels), narrow(4, 4, channels_out, channels),
+            scratch((TILE_ROWS + 2) * EXT_COLS, channels), scratch(FINE_ROWS * FINE_PITCH, channels_out), pltpu.SemaphoreType.DMA((4,)),
         ],
-        3, "finish", 0, (3, 11, 12),
+        3, "finish", 0, (9, 10, 11, 12), (3, 5),
     )
     return decoded
 

time: 127 us -> 125 us (0.984)
  starting transfers between devices: 28 us -> 22.8 us
  Pallas kernels: 56.3 us -> 61 us
  local copies, waits for them, and re-layouts: 4.27 us -> 1.85 us
  waiting for transfers between devices: 20.4 us -> 21.9 us
    all_to_all x1, starting transfers between devices: 9.97 us -> 4.41 us  [local(): parts = lax.all_to_all(parts, ROWS, 0, 0)]
    pallas_call x7, Pallas kernels: 56.3 us -> 61 us  [call(): pl.pallas_call(body, in_specs=[smem if i < smem_count else pl.BlockSpec(m...]
    unnamed x27 -> x7, local copies, waits for them, and re-layouts: 4.27 us -> 1.85 us
    all_gather x1, waiting for transfers between devices: 6.78 us -> 8.58 us  [local(): tiles = lax.all_gather(own_keys, ('core', 'x', 'z'), axis=0, tiled=False)]
where the time goes in v6:
time: 125 us
  Pallas kernels  61 us (49%)
  starting transfers between devices  22.8 us (18%)
  waiting for transfers between devices  21.9 us (18%)
  between operations  14.8 us (12%)
  other arithmetic  2.94 us (2%)
  local copies, waits for them, and re-layouts  1.85 us (1%)
    pallas_call x7, Pallas kernels, call(): pl.pallas_call(body, in_specs=[smem if i < smem_count else pl.BlockSpec(m...  61 us
    ppermute x4, starting transfers between devices, hop(): return lax.ppermute(value, axes, pairs)  12.6 us
    ppermute x4, waiting for transfers between devices, hop(): return lax.ppermute(value, axes, pairs)  8.9 us
    all_gather x1, waiting for transfers between devices, local(): tiles = lax.all_gather(own_keys, ('core', 'x', 'z'), axis=0, tiled=False)  8.58 us
    all_to_all x1, starting transfers between devices, local(): parts = lax.all_to_all(parts, ROWS, 0, 0)  4.41 us
    ppermute x3, starting transfers between devices, local(): lax.ppermute(pair, 'y', [(i, (i + k) % n_y) for i in range(n_y)])  3.97 us
    all_to_all x1, waiting for transfers between devices, local(): parts = lax.all_to_all(parts, ROWS, 0, 0)  3.07 us
  transfers between devices with their start and end apart: 11, of which 7 were waited for; matrix products, arithmetic and copies ran while one was open for 4% of the time, Pallas kernels for 21%

profile of v6, /device:TPU:1, one launch (start us, length us, event | category | flops | bytes accessed | tf_op | source)
XLA Modules:
  0.0 125.2 jit_solution(14232572128661954368)
XLA Ops:
  6.5 1.8 %keys.1 = bf16[272,384]{1,0:T(8,128)(2,1)} custom-call(s32[16]{0:T(128)} %col_ref.9, bf16[13,20,384]{2,1,0:T(8,128)(2,1)} %token_ref.5, f32[384]{0:T(512)} %gain_ref.1), custom_call_target="tpu_custom_call" | custom-call | bytes 410176 | tf_op jit(solution)/shard_map/keys/pallas_call | solution.py:528
  8.4 1.8 %copy.16.one_ref = bf16[2,13,20,384]{3,2,1,0:T(8,128)(2,1)} copy(bf16[2,13,20,384]{3,0,2,1:T(2,128)(2,1)} %param.26) | data formatting | bytes 798720 | tf_op args[8]
  10.2 0.6 pad_add_fusion.place_ref.refs_0_
  10.9 3.0 %edges.1 = (bf16[160,384]{1,0:T(8,128)(2,1)}, bf16[160,384]{1,0:T(8,128)(2,1)}, bf16[48,384]{1,0:T(8,128)(2,1)S(1)}, bf16[48,384]{1,0:T(8,128)(2,1)S(1)}) custom-call(s32[3]{0:T(128)} %pad_add_fusion.place_ref.refs_0_, s32[8]{0:T(128)} %row_ref.9, s32[16]{0:T(128)} %col_ref.9, bf16[13,20,384]{2,1,0:T(8,128)(2,1)} %token_ref.5, ...), custom_call_target="tpu_custom_call" | custom-call | bytes 2516076 | tf_op jit(solution)/shard_map/edges/pallas_call | solution.py:528
  13.9 4.5 %collective-permute-start.4 = (bf16[160,384]{1,0:T(8,128)(2,1)}, bf16[160,384]{1,0:T(8,128)(2,1)S(1)}, u32[]{:S(2)}, u32[]{:S(2)}) collective-permute-start(bf16[160,384]{1,0:T(8,128)(2,1)} %get-tuple-element.55), channel_id=1, source_target_pairs={{0,1},{1,2},{2,3},{3,4},{4,5},{5,6},{6,7},{7,8},{8,9},{9,10},{10,1... | collective-permute-start | bytes 368648 | tf_op jit(solution)/shard_map/ppermute | solution.py:54
  18.4 1.3 %collective-permute-start.5 = (bf16[160,384]{1,0:T(8,128)(2,1)}, bf16[160,384]{1,0:T(8,128)(2,1)S(1)}, u32[]{:S(2)}, u32[]{:S(2)}) collective-permute-start(bf16[160,384]{1,0:T(8,128)(2,1)} %get-tuple-element.56), channel_id=1, source_target_pairs={{1,0},{2,1},{3,2},{4,3},{5,4},{6,5},{7,6},{8,7},{9,8},{10,9},{11,1... | collective-permute-start | bytes 368648 | tf_op jit(solution)/shard_map/ppermute | solution.py:54
  21.0 3.8 %collective-permute-done.5.from_right_ref = bf16[160,384]{1,0:T(8,128)(2,1)S(1)} collective-permute-done((bf16[160,384]{1,0:T(8,128)(2,1)}, bf16[160,384]{1,0:T(8,128)(2,1)S(1)}, u32[]{:S(2)}, u32[]{:S(2)}) %collective-permute-start.5) | collective-permute-done | bytes 122912 | tf_op jit(solution)/shard_map/ppermute | solution.py:54
  24.7 4.9 %columns.1 = (bf16[160,384]{1,0:T(8,128)(2,1)}, bf16[160,384]{1,0:T(8,128)(2,1)}, bf16[26,24,384]{2,1,0:T(8,128)(2,1)}, bf16[52,48,384]{2,1,0:T(8,128)(2,1)}, bf...) custom-call(s32[3]{0:T(128)} %pad_add_fusion.place_ref.refs_0_, ...), custom_call_target="tpu_custom_call" | custom-call | bytes 5526636 | tf_op jit(solution)/shard_map/columns/pallas_call | solution.py:528
  29.6 1.7 %collective-permute-start.6 = (bf16[160,384]{1,0:T(8,128)(2,1)}, bf16[160,384]{1,0:T(8,128)(2,1)S(1)}, u32[]{:S(2)}, u32[]{:S(2)}) collective-permute-start(bf16[160,384]{1,0:T(8,128)(2,1)} %get-tuple-element.62), channel_id=1, source_target_pairs={{0,16},{16,0},{1,17},{17,1},{2,18},{18,2},{3,19},{19,3},{4,20},{20... | collective-permute-start | bytes 368648 | tf_op jit(solution)/shard_map/ppermute | solution.py:605
  31.3 1.2 collective-permute-done.6
  32.5 1.0 maximum_select_fusion.refs_2_
  33.5 3.2 %collective-permute-start.9 = (bf16[2,160,384]{2,1,0:T(8,128)(2,1)S(1)}, bf16[2,160,384]{2,1,0:T(8,128)(2,1)S(1)}, u32[]{:S(2)}, u32[]{:S(2)}) collective-permute-start(bf16[2,160,384]{2,1,0:T(8,128)(2,1)S(1)} %maximum_select_fusion.refs_2_), channel_id=1, source_target_pairs={{0,96},{32,0},{64,32},{96,64},{1,97},{33,1},{65,33},{97,65},{2,98}... | collective-permute-start | bytes 737288 | tf_op jit(solution)/shard_map/ppermute | solution.py:607
  36.7 0.7 collective-permute-start.7
  38.8 4.9 %collective-permute-start.10 = (bf16[8,24,384]{2,1,0:T(8,128)(2,1)}, bf16[8,24,384]{2,1,0:T(8,128)(2,1)S(1)}, u32[]{:S(2)}, u32[]{:S(2)}) collective-permute-start(bf16[8,24,384]{2,1,0:T(8,128)(2,1)} %get-tuple-element.63), channel_id=1, source_target_pairs={{0,16},{16,32},{32,48},{48,64},{64,80},{80,96},{96,112},{1,17},{17... | collective-permute-start | bytes 442376 | tf_op jit(solution)/shard_map/ppermute | solution.py:54
  43.7 1.9 %collective-permute-start.11 = (bf16[8,24,384]{2,1,0:T(8,128)(2,1)}, bf16[8,24,384]{2,1,0:T(8,128)(2,1)S(1)}, u32[]{:S(2)}, u32[]{:S(2)}) collective-permute-start(bf16[8,24,384]{2,1,0:T(8,128)(2,1)} %get-tuple-element.64), channel_id=1, source_target_pairs={{16,0},{32,16},{48,32},{64,48},{80,64},{96,80},{112,96},{17,1},{33... | collective-permute-start | bytes 442376 | tf_op jit(solution)/shard_map/ppermute | solution.py:54
  45.6 3.9 %collective-permute-done.10.from_up_ref = bf16[8,24,384]{2,1,0:T(8,128)(2,1)S(1)} collective-permute-done((bf16[8,24,384]{2,1,0:T(8,128)(2,1)}, bf16[8,24,384]{2,1,0:T(8,128)(2,1)S(1)}, u32[]{:S(2)}, u32[]{:S(2)}) %collective-permute-start.10) | collective-permute-done | bytes 147488 | tf_op jit(solution)/shard_map/ppermute | solution.py:54
  49.5 1.3 %collective-permute-done.11.from_down_ref = bf16[8,24,384]{2,1,0:T(8,128)(2,1)S(1)} collective-permute-done((bf16[8,24,384]{2,1,0:T(8,128)(2,1)}, bf16[8,24,384]{2,1,0:T(8,128)(2,1)S(1)}, u32[]{:S(2)}, u32[]{:S(2)}) %collective-permute-start.11) | collective-permute-done | bytes 147488 | tf_op jit(solution)/shard_map/ppermute | solution.py:54
  50.9 3.8 %queries.1 = (bf16[1056,384]{1,0:T(8,128)(2,1)}, bf16[208,384]{1,0:T(8,128)(2,1)}, bf16[208,384]{1,0:T(8,128)(2,1)}) custom-call(s32[3]{0:T(128)} %pad_add_fusion.place_ref.refs_0_, s32[8]{0:T(128)} %row_ref.9, bf16[2,160,384]{2,1,0:T(8,128)(2,1)S(1)} %maximum_select_fusion.refs_2_, bf16[2,160,384]{2,1,0:T(8,128)(2,1)S(1)} %collective-permute-done.7.refs_3_, ...), custom_call_target="tpu_custom_call" | custom-call | flops 622854144 | bytes 2704940 | tf_op jit(solution)/shard_map/queries/pallas_call | solution.py:528
  54.7 8.6 %all-gather.3.cloned.1.call-done = bf16[8704,384]{1,0:T(8,128)(2,1)} async-done(((bf16[272,384]{1,0:T(8,128)(2,1)}), bf16[8704,384]{1,0:T(8,128)(2,1)}) %all-gather.3.cloned.1.call-update) | async-done | bytes 6684688 | tf_op jit(solution)/shard_map/all_gather | solution.py:582
  63.3 24.4 %attention.1 = bf16[8,208,384]{2,1,0:T(8,128)(2,1)} custom-call(s32[3]{0:T(128)} %pad_add_fusion.place_ref.refs_0_, s32[8]{0:T(128)} %row_ref.9, s32[16]{0:T(128)} %col_ref.9, bf16[1056,384]{1,0:T(8,128)(2,1)} %get-tuple-element.73.query_ref, bf16[32,272,384]{2,1,0:T(8,128)(2,1)} %bitcast.9), custom_call_target="tpu_custom_call" | custom-call | flops 13287555072 | bytes 8773740 | tf_op jit(solution)/shard_map/attention/pallas_call | solution.py:528
  87.7 4.4 %all-to-all-start = ((bf16[8,208,384]{2,1,0:T(8,128)(2,1)}), bf16[8,208,384]{2,1,0:T(8,128)(2,1)S(1)}, u32[]{:S(2)}, u32[]{:S(2)}) async-start(bf16[8,208,384]{2,1,0:T(8,128)(2,1)} %attention.1), calls=%async_computation | async-start | bytes 2555904 | tf_op jit(solution)/shard_map/all_to_all | solution.py:625
  92.2 14.4 %prior.1 = (f32[360,384]{1,0:T(8,128)}, f32[1248,192]{1,0:T(8,128)}, bf16[4,4,192,384]{3,2,1,0:T(8,128)(2,1)}) custom-call(s32[3]{0:T(128)} %pad_add_fusion.place_ref.refs_0_, s32[8]{0:T(128)} %row_ref.9, bf16[26,24,384]{2,1,0:T(8,128)(2,1)} %get-tuple-element.76.prior_ref, bf16[52,48,384]{2,1,0:T(8,128)(2,1)} %get-tuple-element.77.fine_ref, ...), custom_call_target="tpu_custom_call" | custom-call | flops 5223481344 | bytes 18579500 | tf_op jit(solution)/shard_map/prior/pallas_call | solution.py:528
  106.6 3.1 %all-to-all-done.part_ref = bf16[8,208,384]{2,1,0:T(8,128)(2,1)S(1)} async-done(((bf16[8,208,384]{2,1,0:T(8,128)(2,1)}), bf16[8,208,384]{2,1,0:T(8,128)(2,1)S(1)}, u32[]{:S(2)}, u32[]{:S(2)}) %all-to-all-start) | async-done | bytes 1277984 | tf_op jit(solution)/shard_map/all_to_all | solution.py:625
  109.6 8.7 %finish.1 = bf16[26,40,192]{2,1,0:T(8,128)(2,1)} custom-call(s32[3]{0:T(128)} %pad_add_fusion.place_ref.refs_0_, s32[8]{0:T(128)} %row_ref.9, s32[16]{0:T(128)} %col_ref.9, bf16[8,208,384]{2,1,0:T(8,128)(2,1)S(1)} %all-to-all-done.part_ref, bf16[208,384]{1,0:T(8,128)(2,1)} %get-tuple-element.74.mine_ref, ...), custom_call_target="tpu_custom_call" | custom-call | bytes 14423148 | tf_op jit(solution)/shard_map/finish/pallas_call | solution.py:528
  (19 shorter events, 1.5 us)
Async XLA Ops:
  6.5 13.1 %copy-start = (s32[16]{0:T(128)S(1)}, s32[16]{0:T(128)}, u32[]{:S(2)}) copy-start(s32[16]{0:T(128)} %col_ref.9) | copy-start | bytes 196
  6.5 56.8 %all-gather.3.cloned.1.call-start = ((), (), s32[]{:S(2)}) async-start(), calls=%async_computation.1 | async-start | bytes 6893568 | tf_op jit(solution)/shard_map/all_gather | solution.py:582
  13.9 23.6 %copy-start.1 = (s32[8]{0:T(128)S(1)}, s32[8]{0:T(128)}, u32[]{:S(2)}) copy-start(s32[8]{0:T(128)} %row_ref.9) | copy-start | bytes 100
  13.9 7.1 %collective-permute-start.4 = (bf16[160,384]{1,0:T(8,128)(2,1)}, bf16[160,384]{1,0:T(8,128)(2,1)S(1)}, u32[]{:S(2)}, u32[]{:S(2)}) collective-permute-start(bf16[160,384]{1,0:T(8,128)(2,1)} %get-tuple-element.55), channel_id=1, source_target_pairs={{0,1},{1,2},{2,3},{3,4},{4,5},{5,6},{6,7},{7,8},{8,9},{9,10},{10,1... | collective-permute-start | bytes 368648 | tf_op jit(solution)/shard_map/ppermute | solution.py:54
  18.4 6.4 %collective-permute-start.5 = (bf16[160,384]{1,0:T(8,128)(2,1)}, bf16[160,384]{1,0:T(8,128)(2,1)S(1)}, u32[]{:S(2)}, u32[]{:S(2)}) collective-permute-start(bf16[160,384]{1,0:T(8,128)(2,1)} %get-tuple-element.56), channel_id=1, source_target_pairs={{1,0},{2,1},{3,2},{4,3},{5,4},{6,5},{7,6},{8,7},{9,8},{10,9},{11,1... | collective-permute-start | bytes 368648 | tf_op jit(solution)/shard_map/ppermute | solution.py:54
  29.6 2.8 %collective-permute-start.6 = (bf16[160,384]{1,0:T(8,128)(2,1)}, bf16[160,384]{1,0:T(8,128)(2,1)S(1)}, u32[]{:S(2)}, u32[]{:S(2)}) collective-permute-start(bf16[160,384]{1,0:T(8,128)(2,1)} %get-tuple-element.62), channel_id=1, source_target_pairs={{0,16},{16,0},{1,17},{17,1},{2,18},{18,2},{3,19},{19,3},{4,20},{20... | collective-permute-start | bytes 368648 | tf_op jit(solution)/shard_map/ppermute | solution.py:605
  33.5 17.3 %collective-permute-start.9 = (bf16[2,160,384]{2,1,0:T(8,128)(2,1)S(1)}, bf16[2,160,384]{2,1,0:T(8,128)(2,1)S(1)}, u32[]{:S(2)}, u32[]{:S(2)}) collective-permute-start(bf16[2,160,384]{2,1,0:T(8,128)(2,1)S(1)} %maximum_select_fusion.refs_2_), channel_id=1, source_target_pairs={{0,96},{32,0},{64,32},{96,64},{1,97},{33,1},{65,33},{97,65},{2,98}... | collective-permute-start | bytes 737288 | tf_op jit(solution)/shard_map/ppermute | solution.py:607
  36.7 14.0 %collective-permute-start.8 = (bf16[2,160,384]{2,1,0:T(8,128)(2,1)S(1)}, bf16[2,160,384]{2,1,0:T(8,128)(2,1)S(1)}, u32[]{:S(2)}, u32[]{:S(2)}) collective-permute-start(bf16[2,160,384]{2,1,0:T(8,128)(2,1)S(1)} %maximum_select_fusion.refs_2_), channel_id=1, source_target_pairs={{0,64},{32,96},{64,0},{96,32},{1,65},{33,97},{65,1},{97,33},{2,66}... | collective-permute-start | bytes 737288 | tf_op jit(solution)/shard_map/ppermute | solution.py:607
  36.7 14.1 %collective-permute-start.7 = (bf16[2,160,384]{2,1,0:T(8,128)(2,1)S(1)}, bf16[2,160,384]{2,1,0:T(8,128)(2,1)S(1)}, u32[]{:S(2)}, u32[]{:S(2)}) collective-permute-start(bf16[2,160,384]{2,1,0:T(8,128)(2,1)S(1)} %maximum_select_fusion.refs_2_), channel_id=1, source_target_pairs={{0,32},{32,64},{64,96},{96,0},{1,33},{33,65},{65,97},{97,1},{2,34}... | collective-permute-start | bytes 737288 | tf_op jit(solution)/shard_map/ppermute | solution.py:607
  38.8 10.7 %collective-permute-start.10 = (bf16[8,24,384]{2,1,0:T(8,128)(2,1)}, bf16[8,24,384]{2,1,0:T(8,128)(2,1)S(1)}, u32[]{:S(2)}, u32[]{:S(2)}) collective-permute-start(bf16[8,24,384]{2,1,0:T(8,128)(2,1)} %get-tuple-element.63), channel_id=1, source_target_pairs={{0,16},{16,32},{32,48},{48,64},{64,80},{80,96},{96,112},{1,17},{17... | collective-permute-start | bytes 442376 | tf_op jit(solution)/shard_map/ppermute | solution.py:54
  43.7 7.1 %collective-permute-start.11 = (bf16[8,24,384]{2,1,0:T(8,128)(2,1)}, bf16[8,24,384]{2,1,0:T(8,128)(2,1)S(1)}, u32[]{:S(2)}, u32[]{:S(2)}) collective-permute-start(bf16[8,24,384]{2,1,0:T(8,128)(2,1)} %get-tuple-element.64), channel_id=1, source_target_pairs={{16,0},{32,16},{48,32},{64,48},{80,64},{96,80},{112,96},{17,1},{33... | collective-permute-start | bytes 442376 | tf_op jit(solution)/shard_map/ppermute | solution.py:54
  87.7 4.4 %copy-start.2 = (bf16[208,384]{1,0:T(8,128)(2,1)S(1)}, bf16[208,384]{1,0:T(8,128)(2,1)}, u32[]{:S(2)}) copy-start(bf16[208,384]{1,0:T(8,128)(2,1)} %get-tuple-element.75) | copy-start | bytes 479236
  87.7 22.0 %all-to-all-start = ((bf16[8,208,384]{2,1,0:T(8,128)(2,1)}), bf16[8,208,384]{2,1,0:T(8,128)(2,1)S(1)}, u32[]{:S(2)}, u32[]{:S(2)}) async-start(bf16[8,208,384]{2,1,0:T(8,128)(2,1)} %attention.1), calls=%async_computation | async-start | bytes 2555904 | tf_op jit(solution)/shard_map/all_to_all | solution.py:625
  92.1 14.5 %collective-permute-start.12 = (bf16[208,384]{1,0:T(8,128)(2,1)S(1)}, bf16[208,384]{1,0:T(8,128)(2,1)S(1)}, u32[]{:S(2)}, u32[]{:S(2)}) collective-permute-start(bf16[208,384]{1,0:T(8,128)(2,1)S(1)} %copy-done.2), channel_id=1, source_target_pairs={{0,16},{16,0},{1,17},{17,1},{2,18},{18,2},{3,19},{19,3},{4,20},{20... | collective-permute-start | bytes 479240 | tf_op jit(solution)/shard_map/ppermute | solution.py:623
Sparse Core Ops, SparseCore 0:
  9.7 53.5 all-gather.2

commit v7 on v6

--- a/solution.py
+++ b/solution.py
@@ -194,14 +194,14 @@
             up_ref[4 + 2 * f + h] = top[h * 24 : (h + 1) * 24]
 
 
-def prior_kernel(
-    place_ref, row_ref, prior_ref, fine_ref, from_up_ref, from_down_ref, from_up_far_ref, from_down_far_ref, one_ref, two_ref,
-    sum_one_ref, sum_two_ref, phase_ref, coarse_ref, wide_ref, part_ref, weight_one_ref, weight_two_ref, sem_ref,
+def prior_coarse_kernel(
+    place_ref, row_ref, prior_ref, from_up_ref, from_down_ref, from_up_far_ref, from_down_far_ref, one_ref, two_ref,
+    sum_one_ref, phase_ref, coarse_ref, part_ref, weight_one_ref, weight_two_ref, sem_ref,
 ):
     fetch_one = pltpu.make_async_copy(one_ref.at[pl.ds(0, 2)], weight_one_ref, sem_ref.at[0])
-    fetch_two = pltpu.make_async_copy(two_ref, weight_two_ref, sem_ref.at[1])
+    fetch_two = pltpu.make_async_copy(two_ref.at[pl.ds(2, 1)], weight_two_ref, sem_ref.at[1])
+    fetch_two.start()
     fetch_one.start()
-    fetch_two.start()
     tall = row_ref[place_ref[0]]
     up_tall = size_at(row_ref, place_ref[0] - 1)
     down_tall = size_at(row_ref, place_ref[0] + 1)
@@ -214,6 +214,23 @@
             coarse_ref[f, i] = jnp.zeros((EXT_COLS, 384), jnp.bfloat16)
         coarse_ref[f, tall + 2] = from_down_ref[f]
         coarse_ref[f, tall + 3] = jnp.where(down_tall == 1, from_down_far_ref[f], from_down_ref[2 + f])
+    fetch_two.wait()
+    taps = ((0,), (1, 2), (0, 1), (2,))
+    for u in range(4):
+        rows = [sum(weight_two_ref[0, a, b].astype(jnp.float32) for a in taps[u]) for b in range(3)]
+        for v in range(4):
+            phase_ref[u, v] = sum(rows[b] for b in taps[v]).astype(jnp.bfloat16)
+    fetch_one.wait()
+    sum_one_ref[...] = coarse_conv(lambda f, a, n: coarse_ref[f, a : a + n], weight_one_ref, part_ref, 2)
+
+
+def prior_fine_kernel(
+    place_ref, row_ref, fine_ref, from_up_ref, from_down_ref, two_ref, sum_two_ref, wide_ref, part_ref, weight_two_ref, sem_ref
+):
+    fetch_two = pltpu.make_async_copy(two_ref.at[pl.ds(0, 2)], weight_two_ref, sem_ref.at[0])
+    fetch_two.start()
+    tall = row_ref[place_ref[0]]
+    for f in range(2):
         wide_ref[f, 0] = jnp.concatenate([from_up_ref[4 + 2 * f], from_up_ref[5 + 2 * f]], axis=0)
 
         def copy_fine(i, carry):
@@ -223,21 +240,11 @@
         lax.fori_loop(0, FINE_ROWS, copy_fine, 0)
         wide_ref[f, FINE_ROWS + 1] = jnp.zeros((FINE_PITCH, 384), jnp.bfloat16)
         wide_ref[f, 2 * tall + 1] = jnp.concatenate([from_down_ref[4 + 2 * f], from_down_ref[5 + 2 * f]], axis=0)
-    fetch_one.wait()
-    sum_one_ref[...] = coarse_conv(lambda f, a, n: coarse_ref[f, a : a + n], weight_one_ref, part_ref, 2)
     fetch_two.wait()
     for r in range(0, FINE_ROWS, FINE_STEP):
         sum_two_ref[r * FINE_PITCH : (r + FINE_STEP) * FINE_PITCH, :] = fine_conv(
             lambda f, a, n: wide_ref[f, r + a : r + a + n], weight_two_ref, part_ref, 2
         )
-    taps = ((0,), (1, 2), (0, 1), (2,))
-    for u in range(4):
-        rows = []
-        for b in range(3):
-            tap = sum(weight_two_ref[2, a, b].astype(jnp.float32) for a in taps[u])
-            rows.append(tap)
-        for v in range(4):
-            phase_ref[u, v] = sum(rows[b] for b in taps[v]).astype(jnp.bfloat16)
 
 
 def coarse_conv(rows_of, weight_ref, part_ref, depth):
@@ -621,22 +628,31 @@
         2, "queries", 4 * LAT_ROWS * HALF * channels * channels, (), (2, 3, 4, 5),
     )
     frame_other = lax.ppermute(frame_other, "core", swap)
+    conv_two = jnp.swapaxes(conv_two, 3, 4)
+    channels_out = conv_two.shape[3]
+    from_up, from_down, from_up_far, from_down_far = around
+    sum_one, phases = call(
+        prior_coarse_kernel,
+        [place, row_sizes, prior, from_up, from_down, from_up_far, from_down_far, conv_one, conv_two],
+        [wide_shape((TILE_ROWS + 2) * EXT_COLS, channels), shape(4, 4, channels_out, channels)],
+        [
+            narrow(2, EXT_ROWS, EXT_COLS, channels), scratch(3, 640, 128), narrow(2, 3, 3, channels, channels),
+            narrow(1, 3, 3, channels_out, channels), pltpu.SemaphoreType.DMA((2,)),
+        ],
+        2, "prior_coarse", 2 * 18 * channels * 360 * 384, (7, 8), (3, 4),
+    )
+    queries, sum_one, phases = lax.optimization_barrier((queries, sum_one, phases))
     parts = attend(place, row_sizes, col_sizes, queries, tiles.reshape(2 * n_col, KEY_TILE, channels))
     parts = lax.all_to_all(parts, ROWS, 0, 0)
-    conv_two = jnp.swapaxes(conv_two, 3, 4)
-    channels_out = conv_two.shape[3]
-    sum_one, sum_two, phases = call(
-        prior_kernel,
-        [place, row_sizes, prior, fine, *around, conv_one, conv_two],
+    (sum_two,) = call(
+        prior_fine_kernel,
+        [place, row_sizes, fine, from_up, from_down, conv_two],
+        [wide_shape(FINE_ROWS * FINE_PITCH, channels_out)],
         [
-            wide_shape((TILE_ROWS + 2) * EXT_COLS, channels), wide_shape(FINE_ROWS * FINE_PITCH, channels_out),
-            shape(4, 4, channels_out, channels),
+            narrow(2, FINE_ROWS + 2, FINE_PITCH, channels), scratch(3, 640, 128), narrow(2, 3, 3, channels_out, channels),
+            pltpu.SemaphoreType.DMA((1,)),
         ],
-        [
-            narrow(2, EXT_ROWS, EXT_COLS, channels), narrow(2, FINE_ROWS + 2, FINE_PITCH, channels), scratch(3, 640, 128),
-            narrow(2, 3, 3, channels, channels), narrow(3, 3, 3, channels_out, channels), pltpu.SemaphoreType.DMA((2,)),
-        ],
-        2, "prior", 2 * 18 * channels * (360 * 384 + 1248 * 192), (8, 9), (4, 5),
+        2, "prior_fine", 2 * 18 * channels * 1248 * 192, (5,), (3, 4),
     )
     (decoded,) = call(
         finish_kernel,

time: 125 us -> 126 us (level); the launches traced: 125 us -> 125 us
  waiting for transfers between devices: 21.9 us -> 19.4 us
  Pallas kernels: 61 us -> 63.1 us
    all_gather x1, waiting for transfers between devices: 8.58 us -> 1.11 us  [local(): tiles = lax.all_gather(own_keys, ('core', 'x', 'z'), axis=0, tiled=False)]
    all_to_all x1, waiting for transfers between devices: 3.07 us -> 8.22 us  [local(): parts = lax.all_to_all(parts, ROWS, 0, 0)]
    pallas_call x7 -> x8, Pallas kernels: 61 us -> 63.1 us  [call(): pl.pallas_call(body, in_specs=[smem if i < smem_count else pl.BlockSpec(m...]
  transfers between devices with their start and end apart: 11 -> 11, of which waited for: 7 -> 7; matrix products, arithmetic and copies ran while one was open for 4% -> 4% of each run, Pallas kernels for 21% -> 23%
where the time goes in v7:
time: 126 us; the launch traced here: 125 us
  Pallas kernels  63.1 us (50%)
  starting transfers between devices  22.3 us (18%)
  waiting for transfers between devices  19.4 us (15%)
  between operations  14.9 us (12%)
  other arithmetic  3.01 us (2%)
  local copies, waits for them, and re-layouts  1.85 us (1%)
    pallas_call x8, Pallas kernels, call(): pl.pallas_call(body, in_specs=[smem if i < smem_count else pl.BlockSpec(m...  63.1 us
    ppermute x4, starting transfers between devices, hop(): return lax.ppermute(value, axes, pairs)  12.6 us
    ppermute x4, waiting for transfers between devices, hop(): return lax.ppermute(value, axes, pairs)  8.75 us
    all_to_all x1, waiting for transfers between devices, local(): parts = lax.all_to_all(parts, ROWS, 0, 0)  8.22 us
    ppermute x3, starting transfers between devices, local(): lax.ppermute(pair, 'y', [(i, (i + k) % n_y) for i in range(n_y)])  3.97 us
    all_to_all x1, starting transfers between devices, local(): parts = lax.all_to_all(parts, ROWS, 0, 0)  3.87 us
  transfers between devices with their start and end apart: 11, of which 7 were waited for; matrix products, arithmetic and copies ran while one was open for 4% of the time, Pallas kernels for 23%

profile of v7, /device:TPU:1, one launch (start us, length us, event | category | flops | bytes accessed | tf_op | source)
XLA Modules:
  0.0 124.6 jit_solution(2576616690328279007)
XLA Ops:
  6.5 1.8 %keys.1 = bf16[272,384]{1,0:T(8,128)(2,1)} custom-call(s32[16]{0:T(128)} %col_ref.9, bf16[13,20,384]{2,1,0:T(8,128)(2,1)} %token_ref.5, f32[384]{0:T(512)} %gain_ref.1), custom_call_target="tpu_custom_call" | custom-call | bytes 410176 | tf_op jit(solution)/shard_map/keys/pallas_call | solution.py:535
  8.4 1.8 %copy.16.one_ref = bf16[2,13,20,384]{3,2,1,0:T(8,128)(2,1)} copy(bf16[2,13,20,384]{3,0,2,1:T(2,128)(2,1)} %param.26) | data formatting | bytes 798720 | tf_op args[8]
  10.9 3.0 %edges.1 = (bf16[160,384]{1,0:T(8,128)(2,1)}, bf16[160,384]{1,0:T(8,128)(2,1)}, bf16[48,384]{1,0:T(8,128)(2,1)S(1)}, bf16[48,384]{1,0:T(8,128)(2,1)S(1)}) custom-call(s32[3]{0:T(128)} %pad_add_fusion.place_ref.refs_0_, s32[8]{0:T(128)} %row_ref.11, s32[16]{0:T(128)} %col_ref.9, bf16[13,20,384]{2,1,0:T(8,128)(2,1)} %token_ref.5, ...), custom_call_target="tpu_custom_call" | custom-call | bytes 2516076 | tf_op jit(solution)/shard_map/edges/pallas_call | solution.py:535
  13.9 4.5 %collective-permute-start.4 = (bf16[160,384]{1,0:T(8,128)(2,1)}, bf16[160,384]{1,0:T(8,128)(2,1)S(1)}, u32[]{:S(2)}, u32[]{:S(2)}) collective-permute-start(bf16[160,384]{1,0:T(8,128)(2,1)} %get-tuple-element.57), channel_id=1, source_target_pairs={{0,1},{1,2},{2,3},{3,4},{4,5},{5,6},{6,7},{7,8},{8,9},{9,10},{10,1... | collective-permute-start | bytes 368648 | tf_op jit(solution)/shard_map/ppermute | solution.py:54
  18.4 1.3 %collective-permute-start.5 = (bf16[160,384]{1,0:T(8,128)(2,1)}, bf16[160,384]{1,0:T(8,128)(2,1)S(1)}, u32[]{:S(2)}, u32[]{:S(2)}) collective-permute-start(bf16[160,384]{1,0:T(8,128)(2,1)} %get-tuple-element.58), channel_id=1, source_target_pairs={{1,0},{2,1},{3,2},{4,3},{5,4},{6,5},{7,6},{8,7},{9,8},{10,9},{11,1... | collective-permute-start | bytes 368648 | tf_op jit(solution)/shard_map/ppermute | solution.py:54
  21.1 3.6 %collective-permute-done.5.from_right_ref = bf16[160,384]{1,0:T(8,128)(2,1)S(1)} collective-permute-done((bf16[160,384]{1,0:T(8,128)(2,1)}, bf16[160,384]{1,0:T(8,128)(2,1)S(1)}, u32[]{:S(2)}, u32[]{:S(2)}) %collective-permute-start.5) | collective-permute-done | bytes 122912 | tf_op jit(solution)/shard_map/ppermute | solution.py:54
  24.7 4.9 %columns.1 = (bf16[160,384]{1,0:T(8,128)(2,1)}, bf16[160,384]{1,0:T(8,128)(2,1)}, bf16[26,24,384]{2,1,0:T(8,128)(2,1)}, bf16[52,48,384]{2,1,0:T(8,128)(2,1)}, bf...) custom-call(s32[3]{0:T(128)} %pad_add_fusion.place_ref.refs_0_, ...), custom_call_target="tpu_custom_call" | custom-call | bytes 5526636 | tf_op jit(solution)/shard_map/columns/pallas_call | solution.py:535
  29.6 1.7 %collective-permute-start.6 = (bf16[160,384]{1,0:T(8,128)(2,1)}, bf16[160,384]{1,0:T(8,128)(2,1)S(1)}, u32[]{:S(2)}, u32[]{:S(2)}) collective-permute-start(bf16[160,384]{1,0:T(8,128)(2,1)} %get-tuple-element.64), channel_id=1, source_target_pairs={{0,16},{16,0},{1,17},{17,1},{2,18},{18,2},{3,19},{19,3},{4,20},{20... | collective-permute-start | bytes 368648 | tf_op jit(solution)/shard_map/ppermute | solution.py:612
  31.2 1.2 collective-permute-done.6
  32.4 1.0 maximum_select_fusion.refs_2_
  33.5 3.2 %collective-permute-start.9 = (bf16[2,160,384]{2,1,0:T(8,128)(2,1)S(1)}, bf16[2,160,384]{2,1,0:T(8,128)(2,1)S(1)}, u32[]{:S(2)}, u32[]{:S(2)}) collective-permute-start(bf16[2,160,384]{2,1,0:T(8,128)(2,1)S(1)} %maximum_select_fusion.refs_2_), channel_id=1, source_target_pairs={{0,96},{32,0},{64,32},{96,64},{1,97},{33,1},{65,33},{97,65},{2,98}... | collective-permute-start | bytes 737288 | tf_op jit(solution)/shard_map/ppermute | solution.py:614
  36.7 0.7 collective-permute-start.7
  38.7 4.9 %collective-permute-start.10 = (bf16[8,24,384]{2,1,0:T(8,128)(2,1)}, bf16[8,24,384]{2,1,0:T(8,128)(2,1)S(1)}, u32[]{:S(2)}, u32[]{:S(2)}) collective-permute-start(bf16[8,24,384]{2,1,0:T(8,128)(2,1)} %get-tuple-element.65), channel_id=1, source_target_pairs={{0,16},{16,32},{32,48},{48,64},{64,80},{80,96},{96,112},{1,17},{17... | collective-permute-start | bytes 442376 | tf_op jit(solution)/shard_map/ppermute | solution.py:54
  43.6 1.9 %collective-permute-start.11 = (bf16[8,24,384]{2,1,0:T(8,128)(2,1)}, bf16[8,24,384]{2,1,0:T(8,128)(2,1)S(1)}, u32[]{:S(2)}, u32[]{:S(2)}) collective-permute-start(bf16[8,24,384]{2,1,0:T(8,128)(2,1)} %get-tuple-element.66), channel_id=1, source_target_pairs={{16,0},{32,16},{48,32},{64,48},{80,64},{96,80},{112,96},{17,1},{33... | collective-permute-start | bytes 442376 | tf_op jit(solution)/shard_map/ppermute | solution.py:54
  45.6 3.9 %collective-permute-done.10.from_up_ref = bf16[8,24,384]{2,1,0:T(8,128)(2,1)S(1)} collective-permute-done((bf16[8,24,384]{2,1,0:T(8,128)(2,1)}, bf16[8,24,384]{2,1,0:T(8,128)(2,1)S(1)}, u32[]{:S(2)}, u32[]{:S(2)}) %collective-permute-start.10) | collective-permute-done | bytes 147488 | tf_op jit(solution)/shard_map/ppermute | solution.py:54
  49.5 1.3 %collective-permute-done.11.from_down_ref = bf16[8,24,384]{2,1,0:T(8,128)(2,1)S(1)} collective-permute-done((bf16[8,24,384]{2,1,0:T(8,128)(2,1)}, bf16[8,24,384]{2,1,0:T(8,128)(2,1)S(1)}, u32[]{:S(2)}, u32[]{:S(2)}) %collective-permute-start.11) | collective-permute-done | bytes 147488 | tf_op jit(solution)/shard_map/ppermute | solution.py:54
  50.8 3.9 %queries.1 = (bf16[1056,384]{1,0:T(8,128)(2,1)}, bf16[208,384]{1,0:T(8,128)(2,1)}, bf16[208,384]{1,0:T(8,128)(2,1)}) custom-call(s32[3]{0:T(128)} %pad_add_fusion.place_ref.refs_0_, s32[8]{0:T(128)} %row_ref.11, bf16[2,160,384]{2,1,0:T(8,128)(2,1)S(1)} %maximum_select_fusion.refs_2_, bf16[2,160,384]{2,1,0:T(8,128)(2,1)S(1)} %collective-permute-done.7.refs_3_, ...), custom_call_target="tpu_custom_call" | custom-call | flops 622854144 | bytes 2704940 | tf_op jit(solution)/shard_map/queries/pallas_call | solution.py:535
  54.7 7.5 %prior_coarse.1 = (f32[360,384]{1,0:T(8,128)}, bf16[4,4,192,384]{3,2,1,0:T(8,128)(2,1)}) custom-call(s32[3]{0:T(128)} %pad_add_fusion.place_ref.refs_0_, s32[8]{0:T(128)} %row_ref.11, bf16[26,24,384]{2,1,0:T(8,128)(2,1)} %get-tuple-element.76.prior_ref, bf16[8,24,384]{2,1,0:T(8,128)(2,1)S(1)} %collective-permute-done.10.from_up_ref, ...), custom_call_target="tpu_custom_call" | custom-call | flops 1911029760 | bytes 15704108 | tf_op jit(solution)/shard_map/prior_coarse/pallas_call | solution.py:535
  62.2 1.1 all-gather.3.cloned.1.call-done
  63.3 24.3 %attention.1 = bf16[8,208,384]{2,1,0:T(8,128)(2,1)} custom-call(s32[3]{0:T(128)} %pad_add_fusion.place_ref.refs_0_, s32[8]{0:T(128)} %row_ref.11, s32[16]{0:T(128)} %col_ref.9, bf16[1056,384]{1,0:T(8,128)(2,1)} %get-tuple-element.83.query_ref, bf16[32,272,384]{2,1,0:T(8,128)(2,1)} %bitcast.11), custom_call_target="tpu_custom_call" | custom-call | flops 13287555072 | bytes 8773740 | tf_op jit(solution)/shard_map/attention/pallas_call | solution.py:535
  87.6 3.9 %all-to-all-start = ((bf16[8,208,384]{2,1,0:T(8,128)(2,1)}), bf16[8,208,384]{2,1,0:T(8,128)(2,1)S(1)}, u32[]{:S(2)}, u32[]{:S(2)}) async-start(bf16[8,208,384]{2,1,0:T(8,128)(2,1)} %attention.1), calls=%async_computation | async-start | bytes 2555904 | tf_op jit(solution)/shard_map/all_to_all | solution.py:646
  91.7 9.1 %prior_fine.1.far_two_ref = f32[1248,192]{1,0:T(8,128)} custom-call(s32[3]{0:T(128)} %pad_add_fusion.place_ref.refs_0_, s32[8]{0:T(128)} %row_ref.11, bf16[52,48,384]{2,1,0:T(8,128)(2,1)} %get-tuple-element.87.fine_ref, bf16[8,24,384]{2,1,0:T(8,128)(2,1)S(1)} %collective-permute-done.10.from_up_ref, ...), custom_call_target="tpu_custom_call" | custom-call | flops 3312451584 | bytes 7151660 | tf_op jit(solution)/shard_map/prior_fine/pallas_call | solution.py:535
  100.8 8.2 %all-to-all-done.part_ref = bf16[8,208,384]{2,1,0:T(8,128)(2,1)S(1)} async-done(((bf16[8,208,384]{2,1,0:T(8,128)(2,1)}), bf16[8,208,384]{2,1,0:T(8,128)(2,1)S(1)}, u32[]{:S(2)}, u32[]{:S(2)}) %all-to-all-start) | async-done | bytes 1277984 | tf_op jit(solution)/shard_map/all_to_all | solution.py:646
  109.0 8.7 %finish.1 = bf16[26,40,192]{2,1,0:T(8,128)(2,1)} custom-call(s32[3]{0:T(128)} %pad_add_fusion.place_ref.refs_0_, s32[8]{0:T(128)} %row_ref.11, s32[16]{0:T(128)} %col_ref.9, bf16[8,208,384]{2,1,0:T(8,128)(2,1)S(1)} %all-to-all-done.part_ref, bf16[208,384]{1,0:T(8,128)(2,1)} %get-tuple-element.84.mine_ref, ...), custom_call_target="tpu_custom_call" | custom-call | bytes 14423148 | tf_op jit(solution)/shard_map/finish/pallas_call | solution.py:535
  (20 shorter events, 2.3 us)
Async XLA Ops:
  6.5 13.1 %copy-start.1 = (s32[16]{0:T(128)S(1)}, s32[16]{0:T(128)}, u32[]{:S(2)}) copy-start(s32[16]{0:T(128)} %col_ref.9) | copy-start | bytes 196
  6.5 56.7 %all-gather.3.cloned.1.call-start = ((), (), s32[]{:S(2)}) async-start(), calls=%async_computation.1 | async-start | bytes 6893568 | tf_op jit(solution)/shard_map/all_gather | solution.py:589
  13.9 23.6 %copy-start = (s32[8]{0:T(128)S(1)}, s32[8]{0:T(128)}, u32[]{:S(2)}) copy-start(s32[8]{0:T(128)} %row_ref.11) | copy-start | bytes 100
  13.9 7.2 %collective-permute-start.4 = (bf16[160,384]{1,0:T(8,128)(2,1)}, bf16[160,384]{1,0:T(8,128)(2,1)S(1)}, u32[]{:S(2)}, u32[]{:S(2)}) collective-permute-start(bf16[160,384]{1,0:T(8,128)(2,1)} %get-tuple-element.57), channel_id=1, source_target_pairs={{0,1},{1,2},{2,3},{3,4},{4,5},{5,6},{6,7},{7,8},{8,9},{9,10},{10,1... | collective-permute-start | bytes 368648 | tf_op jit(solution)/shard_map/ppermute | solution.py:54
  18.4 6.4 %collective-permute-start.5 = (bf16[160,384]{1,0:T(8,128)(2,1)}, bf16[160,384]{1,0:T(8,128)(2,1)S(1)}, u32[]{:S(2)}, u32[]{:S(2)}) collective-permute-start(bf16[160,384]{1,0:T(8,128)(2,1)} %get-tuple-element.58), channel_id=1, source_target_pairs={{1,0},{2,1},{3,2},{4,3},{5,4},{6,5},{7,6},{8,7},{9,8},{10,9},{11,1... | collective-permute-start | bytes 368648 | tf_op jit(solution)/shard_map/ppermute | solution.py:54
  29.6 2.9 %collective-permute-start.6 = (bf16[160,384]{1,0:T(8,128)(2,1)}, bf16[160,384]{1,0:T(8,128)(2,1)S(1)}, u32[]{:S(2)}, u32[]{:S(2)}) collective-permute-start(bf16[160,384]{1,0:T(8,128)(2,1)} %get-tuple-element.64), channel_id=1, source_target_pairs={{0,16},{16,0},{1,17},{17,1},{2,18},{18,2},{3,19},{19,3},{4,20},{20... | collective-permute-start | bytes 368648 | tf_op jit(solution)/shard_map/ppermute | solution.py:612
  33.5 17.3 %collective-permute-start.9 = (bf16[2,160,384]{2,1,0:T(8,128)(2,1)S(1)}, bf16[2,160,384]{2,1,0:T(8,128)(2,1)S(1)}, u32[]{:S(2)}, u32[]{:S(2)}) collective-permute-start(bf16[2,160,384]{2,1,0:T(8,128)(2,1)S(1)} %maximum_select_fusion.refs_2_), channel_id=1, source_target_pairs={{0,96},{32,0},{64,32},{96,64},{1,97},{33,1},{65,33},{97,65},{2,98}... | collective-permute-start | bytes 737288 | tf_op jit(solution)/shard_map/ppermute | solution.py:614
  36.7 14.0 %collective-permute-start.8 = (bf16[2,160,384]{2,1,0:T(8,128)(2,1)S(1)}, bf16[2,160,384]{2,1,0:T(8,128)(2,1)S(1)}, u32[]{:S(2)}, u32[]{:S(2)}) collective-permute-start(bf16[2,160,384]{2,1,0:T(8,128)(2,1)S(1)} %maximum_select_fusion.refs_2_), channel_id=1, source_target_pairs={{0,64},{32,96},{64,0},{96,32},{1,65},{33,97},{65,1},{97,33},{2,66}... | collective-permute-start | bytes 737288 | tf_op jit(solution)/shard_map/ppermute | solution.py:614
  36.7 14.1 %collective-permute-start.7 = (bf16[2,160,384]{2,1,0:T(8,128)(2,1)S(1)}, bf16[2,160,384]{2,1,0:T(8,128)(2,1)S(1)}, u32[]{:S(2)}, u32[]{:S(2)}) collective-permute-start(bf16[2,160,384]{2,1,0:T(8,128)(2,1)S(1)} %maximum_select_fusion.refs_2_), channel_id=1, source_target_pairs={{0,32},{32,64},{64,96},{96,0},{1,33},{33,65},{65,97},{97,1},{2,34}... | collective-permute-start | bytes 737288 | tf_op jit(solution)/shard_map/ppermute | solution.py:614
  38.7 10.7 %collective-permute-start.10 = (bf16[8,24,384]{2,1,0:T(8,128)(2,1)}, bf16[8,24,384]{2,1,0:T(8,128)(2,1)S(1)}, u32[]{:S(2)}, u32[]{:S(2)}) collective-permute-start(bf16[8,24,384]{2,1,0:T(8,128)(2,1)} %get-tuple-element.65), channel_id=1, source_target_pairs={{0,16},{16,32},{32,48},{48,64},{64,80},{80,96},{96,112},{1,17},{17... | collective-permute-start | bytes 442376 | tf_op jit(solution)/shard_map/ppermute | solution.py:54
  43.6 7.1 %collective-permute-start.11 = (bf16[8,24,384]{2,1,0:T(8,128)(2,1)}, bf16[8,24,384]{2,1,0:T(8,128)(2,1)S(1)}, u32[]{:S(2)}, u32[]{:S(2)}) collective-permute-start(bf16[8,24,384]{2,1,0:T(8,128)(2,1)} %get-tuple-element.66), channel_id=1, source_target_pairs={{16,0},{32,16},{48,32},{64,48},{80,64},{96,80},{112,96},{17,1},{33... | collective-permute-start | bytes 442376 | tf_op jit(solution)/shard_map/ppermute | solution.py:54
  87.6 3.9 %copy-start.2 = (bf16[208,384]{1,0:T(8,128)(2,1)S(1)}, bf16[208,384]{1,0:T(8,128)(2,1)}, u32[]{:S(2)}) copy-start(bf16[208,384]{1,0:T(8,128)(2,1)} %get-tuple-element.85) | copy-start | bytes 479236
  87.6 21.4 %all-to-all-start = ((bf16[8,208,384]{2,1,0:T(8,128)(2,1)}), bf16[8,208,384]{2,1,0:T(8,128)(2,1)S(1)}, u32[]{:S(2)}, u32[]{:S(2)}) async-start(bf16[8,208,384]{2,1,0:T(8,128)(2,1)} %attention.1), calls=%async_computation | async-start | bytes 2555904 | tf_op jit(solution)/shard_map/all_to_all | solution.py:646
  91.5 9.3 %collective-permute-start.12 = (bf16[208,384]{1,0:T(8,128)(2,1)S(1)}, bf16[208,384]{1,0:T(8,128)(2,1)S(1)}, u32[]{:S(2)}, u32[]{:S(2)}) collective-permute-start(bf16[208,384]{1,0:T(8,128)(2,1)S(1)} %copy-done.2), channel_id=1, source_target_pairs={{0,16},{16,0},{1,17},{17,1},{2,18},{18,2},{3,19},{19,3},{4,20},{20... | collective-permute-start | bytes 479240 | tf_op jit(solution)/shard_map/ppermute | solution.py:630
Sparse Core Ops, SparseCore 0:
  9.7 53.5 all-gather.2

commit v8 on v7

--- a/solution.py
+++ b/solution.py
@@ -591,7 +591,7 @@
         edges_kernel,
         [*place_args, tokens, cache_one, cache_two],
         [shape(message, channels), shape(message, channels), shape(NEAR, channels), shape(NEAR, channels)],
-        [scratch(3, 3 * TILE_ROWS * 24, 128), scratch(3, 2 * FINE_ROWS * FINE_COLS, 128)],
+        [scratch(3, (3 * TILE_ROWS + 1) * 24, 128), scratch(3, (2 * FINE_ROWS + 1) * FINE_COLS, 128)],
         3, "edges",
     )
     from_left = hop(to_right, COLS, n_col, 1)
@@ -605,7 +605,10 @@
             shape(2 * FINE_ROWS, FINE_PITCH, channels), shape(8, EXT_COLS, channels), shape(8, EXT_COLS, channels),
             shape(2, EXT_COLS, channels), shape(2, EXT_COLS, channels),
         ],
-        [scratch(3, 3 * TILE_ROWS * EXT_COLS, 128), scratch(3, 2 * FINE_ROWS * FINE_PITCH, 128), scratch(3, TALL_TILE, 128)],
+        [
+            scratch(3, (3 * TILE_ROWS + 1) * EXT_COLS, 128), scratch(3, (2 * FINE_ROWS + 1) * FINE_PITCH, 128),
+            scratch(3, TALL_TILE, 128),
+        ],
         3, "columns", 0, (), (6, 7),
     )
     swap = [(0, 1), (1, 0)]
@@ -663,7 +666,7 @@
         [
             scratch(3, EXT_ROWS * EXT_COLS, 128), narrow(EXT_ROWS, EXT_COLS, channels),
             scratch(3, 640, 128),
-            scratch(4, 2, TILE_ROWS * EXT_COLS + 8, 128), scratch(2, FINE_ROWS * FINE_PITCH, 128),
+            scratch(4, 2, TILE_ROWS * EXT_COLS + 8, 128), scratch(2, (FINE_ROWS + 1) * FINE_PITCH, 128),
             narrow(1, 3, 3, channels, channels), narrow(4, 4, channels_out, channels),
             scratch((TILE_ROWS + 2) * EXT_COLS, channels), scratch(FINE_ROWS * FINE_PITCH, channels_out), pltpu.SemaphoreType.DMA((4,)),
         ],

time: 126 us -> 126 us (level)
  starting transfers between devices: 22.3 us -> 28.3 us
  Pallas kernels: 63.1 us -> 57.8 us
    all_to_all x1, starting transfers between devices: 3.87 us -> 9.98 us  [local(): parts = lax.all_to_all(parts, ROWS, 0, 0)]
    pallas_call x8, Pallas kernels: 63.1 us -> 57.8 us  [call(): pl.pallas_call(body, in_specs=[smem if i < smem_count else pl.BlockSpec(m...]
where the time goes in v8:
time: 126 us; the launch traced here: 125 us
  Pallas kernels  57.8 us (46%)
  starting transfers between devices  28.3 us (22%)
  waiting for transfers between devices  19.5 us (15%)
  between operations  14.9 us (12%)
  other arithmetic  3.01 us (2%)
  local copies, waits for them, and re-layouts  1.85 us (1%)
    pallas_call x8, Pallas kernels, call(): pl.pallas_call(body, in_specs=[smem if i < smem_count else pl.BlockSpec(m...  57.8 us
    ppermute x4, starting transfers between devices, hop(): return lax.ppermute(value, axes, pairs)  12.6 us
    all_to_all x1, starting transfers between devices, local(): parts = lax.all_to_all(parts, ROWS, 0, 0)  9.98 us
    ppermute x4, waiting for transfers between devices, hop(): return lax.ppermute(value, axes, pairs)  8.77 us
    all_to_all x1, waiting for transfers between devices, local(): parts = lax.all_to_all(parts, ROWS, 0, 0)  8.31 us
    ppermute x3, starting transfers between devices, local(): lax.ppermute(pair, 'y', [(i, (i + k) % n_y) for i in range(n_y)])  3.96 us
  transfers between devices with their start and end apart: 11, of which 7 were waited for; matrix products, arithmetic and copies ran while one was open for 4% of the time, Pallas kernels for 23%

profile of v8, /device:TPU:1, one launch (start us, length us, event | category | flops | bytes accessed | tf_op | source)
XLA Modules:
  0.0 125.4 jit_solution(14468116607019348670)
XLA Ops:
  6.5 1.8 %keys.1 = bf16[272,384]{1,0:T(8,128)(2,1)} custom-call(s32[16]{0:T(128)} %col_ref.9, bf16[13,20,384]{2,1,0:T(8,128)(2,1)} %token_ref.5, f32[384]{0:T(512)} %gain_ref.1), custom_call_target="tpu_custom_call" | custom-call | bytes 410176 | tf_op jit(solution)/shard_map/keys/pallas_call | solution.py:535
  8.4 1.8 %copy.16.one_ref = bf16[2,13,20,384]{3,2,1,0:T(8,128)(2,1)} copy(bf16[2,13,20,384]{3,0,2,1:T(2,128)(2,1)} %param.26) | data formatting | bytes 798720 | tf_op args[8]
  10.9 3.0 %edges.1 = (bf16[160,384]{1,0:T(8,128)(2,1)}, bf16[160,384]{1,0:T(8,128)(2,1)}, bf16[48,384]{1,0:T(8,128)(2,1)S(1)}, bf16[48,384]{1,0:T(8,128)(2,1)S(1)}) custom-call(s32[3]{0:T(128)} %pad_add_fusion.place_ref.refs_0_, s32[8]{0:T(128)} %row_ref.11, s32[16]{0:T(128)} %col_ref.9, bf16[13,20,384]{2,1,0:T(8,128)(2,1)} %token_ref.5, ...), custom_call_target="tpu_custom_call" | custom-call | bytes 2516076 | tf_op jit(solution)/shard_map/edges/pallas_call | solution.py:535
  13.9 4.5 %collective-permute-start.4 = (bf16[160,384]{1,0:T(8,128)(2,1)}, bf16[160,384]{1,0:T(8,128)(2,1)S(1)}, u32[]{:S(2)}, u32[]{:S(2)}) collective-permute-start(bf16[160,384]{1,0:T(8,128)(2,1)} %get-tuple-element.57), channel_id=1, source_target_pairs={{0,1},{1,2},{2,3},{3,4},{4,5},{5,6},{6,7},{7,8},{8,9},{9,10},{10,1... | collective-permute-start | bytes 368648 | tf_op jit(solution)/shard_map/ppermute | solution.py:54
  18.4 1.3 %collective-permute-start.5 = (bf16[160,384]{1,0:T(8,128)(2,1)}, bf16[160,384]{1,0:T(8,128)(2,1)S(1)}, u32[]{:S(2)}, u32[]{:S(2)}) collective-permute-start(bf16[160,384]{1,0:T(8,128)(2,1)} %get-tuple-element.58), channel_id=1, source_target_pairs={{1,0},{2,1},{3,2},{4,3},{5,4},{6,5},{7,6},{8,7},{9,8},{10,9},{11,1... | collective-permute-start | bytes 368648 | tf_op jit(solution)/shard_map/ppermute | solution.py:54
  21.1 3.6 %collective-permute-done.5.from_right_ref = bf16[160,384]{1,0:T(8,128)(2,1)S(1)} collective-permute-done((bf16[160,384]{1,0:T(8,128)(2,1)}, bf16[160,384]{1,0:T(8,128)(2,1)S(1)}, u32[]{:S(2)}, u32[]{:S(2)}) %collective-permute-start.5) | collective-permute-done | bytes 122912 | tf_op jit(solution)/shard_map/ppermute | solution.py:54
  24.7 4.8 %columns.1 = (bf16[160,384]{1,0:T(8,128)(2,1)}, bf16[160,384]{1,0:T(8,128)(2,1)}, bf16[26,24,384]{2,1,0:T(8,128)(2,1)}, bf16[52,48,384]{2,1,0:T(8,128)(2,1)}, bf...) custom-call(s32[3]{0:T(128)} %pad_add_fusion.place_ref.refs_0_, ...), custom_call_target="tpu_custom_call" | custom-call | bytes 5526636 | tf_op jit(solution)/shard_map/columns/pallas_call | solution.py:535
  29.6 1.7 %collective-permute-start.6 = (bf16[160,384]{1,0:T(8,128)(2,1)}, bf16[160,384]{1,0:T(8,128)(2,1)S(1)}, u32[]{:S(2)}, u32[]{:S(2)}) collective-permute-start(bf16[160,384]{1,0:T(8,128)(2,1)} %get-tuple-element.64), channel_id=1, source_target_pairs={{0,16},{16,0},{1,17},{17,1},{2,18},{18,2},{3,19},{19,3},{4,20},{20... | collective-permute-start | bytes 368648 | tf_op jit(solution)/shard_map/ppermute | solution.py:615
  31.2 1.2 collective-permute-done.6
  32.4 1.0 maximum_select_fusion.refs_2_
  33.4 3.2 %collective-permute-start.9 = (bf16[2,160,384]{2,1,0:T(8,128)(2,1)S(1)}, bf16[2,160,384]{2,1,0:T(8,128)(2,1)S(1)}, u32[]{:S(2)}, u32[]{:S(2)}) collective-permute-start(bf16[2,160,384]{2,1,0:T(8,128)(2,1)S(1)} %maximum_select_fusion.refs_2_), channel_id=1, source_target_pairs={{0,96},{32,0},{64,32},{96,64},{1,97},{33,1},{65,33},{97,65},{2,98}... | collective-permute-start | bytes 737288 | tf_op jit(solution)/shard_map/ppermute | solution.py:617
  36.6 0.7 collective-permute-start.7
  38.7 4.9 %collective-permute-start.10 = (bf16[8,24,384]{2,1,0:T(8,128)(2,1)}, bf16[8,24,384]{2,1,0:T(8,128)(2,1)S(1)}, u32[]{:S(2)}, u32[]{:S(2)}) collective-permute-start(bf16[8,24,384]{2,1,0:T(8,128)(2,1)} %get-tuple-element.65), channel_id=1, source_target_pairs={{0,16},{16,32},{32,48},{48,64},{64,80},{80,96},{96,112},{1,17},{17... | collective-permute-start | bytes 442376 | tf_op jit(solution)/shard_map/ppermute | solution.py:54
  43.6 1.9 %collective-permute-start.11 = (bf16[8,24,384]{2,1,0:T(8,128)(2,1)}, bf16[8,24,384]{2,1,0:T(8,128)(2,1)S(1)}, u32[]{:S(2)}, u32[]{:S(2)}) collective-permute-start(bf16[8,24,384]{2,1,0:T(8,128)(2,1)} %get-tuple-element.66), channel_id=1, source_target_pairs={{16,0},{32,16},{48,32},{64,48},{80,64},{96,80},{112,96},{17,1},{33... | collective-permute-start | bytes 442376 | tf_op jit(solution)/shard_map/ppermute | solution.py:54
  45.5 3.9 %collective-permute-done.10.from_up_ref = bf16[8,24,384]{2,1,0:T(8,128)(2,1)S(1)} collective-permute-done((bf16[8,24,384]{2,1,0:T(8,128)(2,1)}, bf16[8,24,384]{2,1,0:T(8,128)(2,1)S(1)}, u32[]{:S(2)}, u32[]{:S(2)}) %collective-permute-start.10) | collective-permute-done | bytes 147488 | tf_op jit(solution)/shard_map/ppermute | solution.py:54
  49.4 1.3 collective-permute-done.11.from_down_ref
  50.8 3.9 %queries.1 = (bf16[1056,384]{1,0:T(8,128)(2,1)}, bf16[208,384]{1,0:T(8,128)(2,1)}, bf16[208,384]{1,0:T(8,128)(2,1)}) custom-call(s32[3]{0:T(128)} %pad_add_fusion.place_ref.refs_0_, s32[8]{0:T(128)} %row_ref.11, bf16[2,160,384]{2,1,0:T(8,128)(2,1)S(1)} %maximum_select_fusion.refs_2_, bf16[2,160,384]{2,1,0:T(8,128)(2,1)S(1)} %collective-permute-done.7.refs_3_, ...), custom_call_target="tpu_custom_call" | custom-call | flops 622854144 | bytes 2704940 | tf_op jit(solution)/shard_map/queries/pallas_call | solution.py:535
  54.7 7.5 %prior_coarse.1 = (f32[360,384]{1,0:T(8,128)}, bf16[4,4,192,384]{3,2,1,0:T(8,128)(2,1)}) custom-call(s32[3]{0:T(128)} %pad_add_fusion.place_ref.refs_0_, s32[8]{0:T(128)} %row_ref.11, bf16[26,24,384]{2,1,0:T(8,128)(2,1)} %get-tuple-element.76.prior_ref, bf16[8,24,384]{2,1,0:T(8,128)(2,1)S(1)} %collective-permute-done.10.from_up_ref, ...), custom_call_target="tpu_custom_call" | custom-call | flops 1911029760 | bytes 15704108 | tf_op jit(solution)/shard_map/prior_coarse/pallas_call | solution.py:535
  62.1 1.1 all-gather.3.cloned.1.call-done
  63.3 19.0 %attention.1 = bf16[8,208,384]{2,1,0:T(8,128)(2,1)} custom-call(s32[3]{0:T(128)} %pad_add_fusion.place_ref.refs_0_, s32[8]{0:T(128)} %row_ref.11, s32[16]{0:T(128)} %col_ref.9, bf16[1056,384]{1,0:T(8,128)(2,1)} %get-tuple-element.83.query_ref, bf16[32,272,384]{2,1,0:T(8,128)(2,1)} %bitcast.11), custom_call_target="tpu_custom_call" | custom-call | flops 13287555072 | bytes 8773740 | tf_op jit(solution)/shard_map/attention/pallas_call | solution.py:535
  82.3 10.0 %all-to-all-start = ((bf16[8,208,384]{2,1,0:T(8,128)(2,1)}), bf16[8,208,384]{2,1,0:T(8,128)(2,1)S(1)}, u32[]{:S(2)}, u32[]{:S(2)}) async-start(bf16[8,208,384]{2,1,0:T(8,128)(2,1)} %attention.1), calls=%async_computation | async-start | bytes 2555904 | tf_op jit(solution)/shard_map/all_to_all | solution.py:649
  92.4 9.1 %prior_fine.1.far_two_ref = f32[1248,192]{1,0:T(8,128)} custom-call(s32[3]{0:T(128)} %pad_add_fusion.place_ref.refs_0_, s32[8]{0:T(128)} %row_ref.11, bf16[52,48,384]{2,1,0:T(8,128)(2,1)} %get-tuple-element.87.fine_ref, bf16[8,24,384]{2,1,0:T(8,128)(2,1)S(1)} %collective-permute-done.10.from_up_ref, ...), custom_call_target="tpu_custom_call" | custom-call | flops 3312451584 | bytes 7151660 | tf_op jit(solution)/shard_map/prior_fine/pallas_call | solution.py:535
  101.5 8.3 %all-to-all-done.part_ref = bf16[8,208,384]{2,1,0:T(8,128)(2,1)S(1)} async-done(((bf16[8,208,384]{2,1,0:T(8,128)(2,1)}), bf16[8,208,384]{2,1,0:T(8,128)(2,1)S(1)}, u32[]{:S(2)}, u32[]{:S(2)}) %all-to-all-start) | async-done | bytes 1277984 | tf_op jit(solution)/shard_map/all_to_all | solution.py:649
  109.8 8.7 %finish.1 = bf16[26,40,192]{2,1,0:T(8,128)(2,1)} custom-call(s32[3]{0:T(128)} %pad_add_fusion.place_ref.refs_0_, s32[8]{0:T(128)} %row_ref.11, s32[16]{0:T(128)} %col_ref.9, bf16[8,208,384]{2,1,0:T(8,128)(2,1)S(1)} %all-to-all-done.part_ref, bf16[208,384]{1,0:T(8,128)(2,1)} %get-tuple-element.84.mine_ref, ...), custom_call_target="tpu_custom_call" | custom-call | bytes 14423148 | tf_op jit(solution)/shard_map/finish/pallas_call | solution.py:535
  (20 shorter events, 2.2 us)
Async XLA Ops:
  6.5 13.1 %copy-start.1 = (s32[16]{0:T(128)S(1)}, s32[16]{0:T(128)}, u32[]{:S(2)}) copy-start(s32[16]{0:T(128)} %col_ref.9) | copy-start | bytes 196
  6.5 56.7 %all-gather.3.cloned.1.call-start = ((), (), s32[]{:S(2)}) async-start(), calls=%async_computation.1 | async-start | bytes 6893568 | tf_op jit(solution)/shard_map/all_gather | solution.py:589
  13.9 23.5 %copy-start = (s32[8]{0:T(128)S(1)}, s32[8]{0:T(128)}, u32[]{:S(2)}) copy-start(s32[8]{0:T(128)} %row_ref.11) | copy-start | bytes 100
  13.9 7.2 %collective-permute-start.4 = (bf16[160,384]{1,0:T(8,128)(2,1)}, bf16[160,384]{1,0:T(8,128)(2,1)S(1)}, u32[]{:S(2)}, u32[]{:S(2)}) collective-permute-start(bf16[160,384]{1,0:T(8,128)(2,1)} %get-tuple-element.57), channel_id=1, source_target_pairs={{0,1},{1,2},{2,3},{3,4},{4,5},{5,6},{6,7},{7,8},{8,9},{9,10},{10,1... | collective-permute-start | bytes 368648 | tf_op jit(solution)/shard_map/ppermute | solution.py:54
  18.4 6.4 %collective-permute-start.5 = (bf16[160,384]{1,0:T(8,128)(2,1)}, bf16[160,384]{1,0:T(8,128)(2,1)S(1)}, u32[]{:S(2)}, u32[]{:S(2)}) collective-permute-start(bf16[160,384]{1,0:T(8,128)(2,1)} %get-tuple-element.58), channel_id=1, source_target_pairs={{1,0},{2,1},{3,2},{4,3},{5,4},{6,5},{7,6},{8,7},{9,8},{10,9},{11,1... | collective-permute-start | bytes 368648 | tf_op jit(solution)/shard_map/ppermute | solution.py:54
  29.6 2.8 %collective-permute-start.6 = (bf16[160,384]{1,0:T(8,128)(2,1)}, bf16[160,384]{1,0:T(8,128)(2,1)S(1)}, u32[]{:S(2)}, u32[]{:S(2)}) collective-permute-start(bf16[160,384]{1,0:T(8,128)(2,1)} %get-tuple-element.64), channel_id=1, source_target_pairs={{0,16},{16,0},{1,17},{17,1},{2,18},{18,2},{3,19},{19,3},{4,20},{20... | collective-permute-start | bytes 368648 | tf_op jit(solution)/shard_map/ppermute | solution.py:615
  33.4 17.3 %collective-permute-start.9 = (bf16[2,160,384]{2,1,0:T(8,128)(2,1)S(1)}, bf16[2,160,384]{2,1,0:T(8,128)(2,1)S(1)}, u32[]{:S(2)}, u32[]{:S(2)}) collective-permute-start(bf16[2,160,384]{2,1,0:T(8,128)(2,1)S(1)} %maximum_select_fusion.refs_2_), channel_id=1, source_target_pairs={{0,96},{32,0},{64,32},{96,64},{1,97},{33,1},{65,33},{97,65},{2,98}... | collective-permute-start | bytes 737288 | tf_op jit(solution)/shard_map/ppermute | solution.py:617
  36.6 14.0 %collective-permute-start.8 = (bf16[2,160,384]{2,1,0:T(8,128)(2,1)S(1)}, bf16[2,160,384]{2,1,0:T(8,128)(2,1)S(1)}, u32[]{:S(2)}, u32[]{:S(2)}) collective-permute-start(bf16[2,160,384]{2,1,0:T(8,128)(2,1)S(1)} %maximum_select_fusion.refs_2_), channel_id=1, source_target_pairs={{0,64},{32,96},{64,0},{96,32},{1,65},{33,97},{65,1},{97,33},{2,66}... | collective-permute-start | bytes 737288 | tf_op jit(solution)/shard_map/ppermute | solution.py:617
  36.6 14.1 %collective-permute-start.7 = (bf16[2,160,384]{2,1,0:T(8,128)(2,1)S(1)}, bf16[2,160,384]{2,1,0:T(8,128)(2,1)S(1)}, u32[]{:S(2)}, u32[]{:S(2)}) collective-permute-start(bf16[2,160,384]{2,1,0:T(8,128)(2,1)S(1)} %maximum_select_fusion.refs_2_), channel_id=1, source_target_pairs={{0,32},{32,64},{64,96},{96,0},{1,33},{33,65},{65,97},{97,1},{2,34}... | collective-permute-start | bytes 737288 | tf_op jit(solution)/shard_map/ppermute | solution.py:617
  38.7 10.7 %collective-permute-start.10 = (bf16[8,24,384]{2,1,0:T(8,128)(2,1)}, bf16[8,24,384]{2,1,0:T(8,128)(2,1)S(1)}, u32[]{:S(2)}, u32[]{:S(2)}) collective-permute-start(bf16[8,24,384]{2,1,0:T(8,128)(2,1)} %get-tuple-element.65), channel_id=1, source_target_pairs={{0,16},{16,32},{32,48},{48,64},{64,80},{80,96},{96,112},{1,17},{17... | collective-permute-start | bytes 442376 | tf_op jit(solution)/shard_map/ppermute | solution.py:54
  43.6 7.1 %collective-permute-start.11 = (bf16[8,24,384]{2,1,0:T(8,128)(2,1)}, bf16[8,24,384]{2,1,0:T(8,128)(2,1)S(1)}, u32[]{:S(2)}, u32[]{:S(2)}) collective-permute-start(bf16[8,24,384]{2,1,0:T(8,128)(2,1)} %get-tuple-element.66), channel_id=1, source_target_pairs={{16,0},{32,16},{48,32},{64,48},{80,64},{96,80},{112,96},{17,1},{33... | collective-permute-start | bytes 442376 | tf_op jit(solution)/shard_map/ppermute | solution.py:54
  82.3 10.0 %copy-start.2 = (bf16[208,384]{1,0:T(8,128)(2,1)S(1)}, bf16[208,384]{1,0:T(8,128)(2,1)}, u32[]{:S(2)}) copy-start(bf16[208,384]{1,0:T(8,128)(2,1)} %get-tuple-element.85) | copy-start | bytes 479236
  82.3 27.5 %all-to-all-start = ((bf16[8,208,384]{2,1,0:T(8,128)(2,1)}), bf16[8,208,384]{2,1,0:T(8,128)(2,1)S(1)}, u32[]{:S(2)}, u32[]{:S(2)}) async-start(bf16[8,208,384]{2,1,0:T(8,128)(2,1)} %attention.1), calls=%async_computation | async-start | bytes 2555904 | tf_op jit(solution)/shard_map/all_to_all | solution.py:649
  92.3 9.2 %collective-permute-start.12 = (bf16[208,384]{1,0:T(8,128)(2,1)S(1)}, bf16[208,384]{1,0:T(8,128)(2,1)S(1)}, u32[]{:S(2)}, u32[]{:S(2)}) collective-permute-start(bf16[208,384]{1,0:T(8,128)(2,1)S(1)} %copy-done.2), channel_id=1, source_target_pairs={{0,16},{16,0},{1,17},{17,1},{2,18},{18,2},{3,19},{19,3},{4,20},{20... | collective-permute-start | bytes 479240 | tf_op jit(solution)/shard_map/ppermute | solution.py:633
Sparse Core Ops, SparseCore 0:
  9.7 53.5 all-gather.2

commit v9 on v8

--- a/solution.py
+++ b/solution.py
@@ -437,17 +437,15 @@
 
 
 def finish_kernel(
-    place_ref, row_ref, col_ref, part_ref, mine_ref, other_ref, vw_ref, ow_ref, gain_one_ref, far_one_ref, far_two_ref, one_ref, two_ref,
-    gain_two_ref, out_ref, act_ref, first_ref, shift_ref, product_ref, fine_ref, weight_one_ref, phase_ref, sum_one_ref, sum_two_ref, sem_ref,
+    place_ref, row_ref, col_ref, part_ref, mine_ref, other_ref, vw_ref, ow_ref, gain_one_ref, far_one_ref, sum_two_ref, one_ref, two_ref,
+    gain_two_ref, out_ref, act_ref, first_ref, shift_ref, product_ref, fine_ref, weight_one_ref, phase_ref, sum_one_ref, sem_ref,
 ):
     fetch_one = pltpu.make_async_copy(one_ref.at[pl.ds(2, 1)], weight_one_ref, sem_ref.at[0])
     fetch_two = pltpu.make_async_copy(two_ref, phase_ref, sem_ref.at[1])
     fetch_sum_one = pltpu.make_async_copy(far_one_ref, sum_one_ref, sem_ref.at[2])
-    fetch_sum_two = pltpu.make_async_copy(far_two_ref, sum_two_ref, sem_ref.at[3])
     fetch_one.start()
     fetch_sum_one.start()
     fetch_two.start()
-    fetch_sum_two.start()
     core = place_ref[2]
     tall = row_ref[place_ref[0]]
     wide = col_ref[place_ref[1]]
@@ -521,7 +519,6 @@
                     next_ = product_ref[2 * q + 1, g, pl.ds(i * EXT_COLS + q + 1, EXT_COLS), :]
                     fine_ref[g, pl.ds((2 * i + p) * FINE_PITCH + q, EXT_COLS, 2), :] = near + next_
     col = lax.broadcasted_iota(jnp.int32, (FINE_COLS, 192), 0)
-    fetch_sum_two.wait()
     for r in range(FINE_ROWS):
         line = get_rows(fine_ref, r * FINE_PITCH, FINE_COLS)[:, 0:192] + sum_two_ref[r * FINE_PITCH : r * FINE_PITCH + FINE_COLS, :]
         usable = (col < 2 * wide) & (r < 2 * tall)
@@ -668,9 +665,9 @@
             scratch(3, 640, 128),
             scratch(4, 2, TILE_ROWS * EXT_COLS + 8, 128), scratch(2, (FINE_ROWS + 1) * FINE_PITCH, 128),
             narrow(1, 3, 3, channels, channels), narrow(4, 4, channels_out, channels),
-            scratch((TILE_ROWS + 2) * EXT_COLS, channels), scratch(FINE_ROWS * FINE_PITCH, channels_out), pltpu.SemaphoreType.DMA((4,)),
-        ],
-        3, "finish", 0, (9, 10, 11, 12), (3, 5),
+            scratch((TILE_ROWS + 2) * EXT_COLS, channels), pltpu.SemaphoreType.DMA((3,)),
+        ],
+        3, "finish", 0, (9, 11, 12), (3, 5, 10),
     )
     return decoded
 

time: 126 us -> 127 us (level)
  starting transfers between devices: 28.3 us -> 22.5 us
  Pallas kernels: 57.8 us -> 63 us
  local copies, waits for them, and re-layouts: 1.85 us -> 3.16 us
    all_to_all x1, starting transfers between devices: 9.98 us -> 4.41 us  [local(): parts = lax.all_to_all(parts, ROWS, 0, 0)]
    pallas_call x8, Pallas kernels: 57.8 us -> 63 us  [call(): pl.pallas_call(body, in_specs=[smem if i < smem_count else pl.BlockSpec(m...]
    unnamed x7 -> x9, local copies, waits for them, and re-layouts: 1.85 us -> 3.16 us
  transfers between devices with their start and end apart: 11 -> 11, of which waited for: 7 -> 7; matrix products, arithmetic and copies ran while one was open for 4% -> 4% of each run, Pallas kernels for 23% -> 22%
where the time goes in v9:
time: 127 us; the launch traced here: 126 us
  Pallas kernels  63 us (50%)
  starting transfers between devices  22.5 us (18%)
  waiting for transfers between devices  20.1 us (16%)
  between operations  14.8 us (12%)
  local copies, waits for them, and re-layouts  3.16 us (2%)
  other arithmetic  2.88 us (2%)
    pallas_call x8, Pallas kernels, call(): pl.pallas_call(body, in_specs=[smem if i < smem_count else pl.BlockSpec(m...  63 us
    ppermute x4, starting transfers between devices, hop(): return lax.ppermute(value, axes, pairs)  12.4 us
    ppermute x4, waiting for transfers between devices, hop(): return lax.ppermute(value, axes, pairs)  8.95 us
    all_to_all x1, waiting for transfers between devices, local(): parts = lax.all_to_all(parts, ROWS, 0, 0)  8.31 us
    all_to_all x1, starting transfers between devices, local(): parts = lax.all_to_all(parts, ROWS, 0, 0)  4.41 us
    ppermute x3, starting transfers between devices, local(): lax.ppermute(pair, 'y', [(i, (i + k) % n_y) for i in range(n_y)])  3.88 us
    unnamed x9, local copies, waits for them, and re-layouts  3.16 us
  transfers between devices with their start and end apart: 11, of which 7 were waited for; matrix products, arithmetic and copies ran while one was open for 4% of the time, Pallas kernels for 22%

profile of v9, /device:TPU:1, one launch (start us, length us, event | category | flops | bytes accessed | tf_op | source)
XLA Modules:
  0.0 126.4 jit_solution(2133104363280497059)
XLA Ops:
  6.5 1.8 %keys.1 = bf16[272,384]{1,0:T(8,128)(2,1)} custom-call(s32[16]{0:T(128)} %col_ref.9, bf16[13,20,384]{2,1,0:T(8,128)(2,1)} %token_ref.5, f32[384]{0:T(512)} %gain_ref.1), custom_call_target="tpu_custom_call" | custom-call | bytes 410176 | tf_op jit(solution)/shard_map/keys/pallas_call | solution.py:532
  8.4 1.8 %copy.16.one_ref = bf16[2,13,20,384]{3,2,1,0:T(8,128)(2,1)} copy(bf16[2,13,20,384]{3,0,2,1:T(2,128)(2,1)} %param.26) | data formatting | bytes 798720 | tf_op args[8]
  10.8 3.0 %edges.1 = (bf16[160,384]{1,0:T(8,128)(2,1)}, bf16[160,384]{1,0:T(8,128)(2,1)}, bf16[48,384]{1,0:T(8,128)(2,1)S(1)}, bf16[48,384]{1,0:T(8,128)(2,1)S(1)}) custom-call(s32[3]{0:T(128)} %pad_add_fusion.place_ref.refs_0_, s32[8]{0:T(128)} %row_ref.11, s32[16]{0:T(128)} %col_ref.9, bf16[13,20,384]{2,1,0:T(8,128)(2,1)} %token_ref.5, ...), custom_call_target="tpu_custom_call" | custom-call | bytes 2516076 | tf_op jit(solution)/shard_map/edges/pallas_call | solution.py:532
  13.8 4.5 %collective-permute-start.4 = (bf16[160,384]{1,0:T(8,128)(2,1)}, bf16[160,384]{1,0:T(8,128)(2,1)S(1)}, u32[]{:S(2)}, u32[]{:S(2)}) collective-permute-start(bf16[160,384]{1,0:T(8,128)(2,1)} %get-tuple-element.57), channel_id=1, source_target_pairs={{0,1},{1,2},{2,3},{3,4},{4,5},{5,6},{6,7},{7,8},{8,9},{9,10},{10,1... | collective-permute-start | bytes 368648 | tf_op jit(solution)/shard_map/ppermute | solution.py:54
  18.3 1.3 %collective-permute-start.5 = (bf16[160,384]{1,0:T(8,128)(2,1)}, bf16[160,384]{1,0:T(8,128)(2,1)S(1)}, u32[]{:S(2)}, u32[]{:S(2)}) collective-permute-start(bf16[160,384]{1,0:T(8,128)(2,1)} %get-tuple-element.58), channel_id=1, source_target_pairs={{1,0},{2,1},{3,2},{4,3},{5,4},{6,5},{7,6},{8,7},{9,8},{10,9},{11,1... | collective-permute-start | bytes 368648 | tf_op jit(solution)/shard_map/ppermute | solution.py:54
  20.9 3.8 %collective-permute-done.5.from_right_ref = bf16[160,384]{1,0:T(8,128)(2,1)S(1)} collective-permute-done((bf16[160,384]{1,0:T(8,128)(2,1)}, bf16[160,384]{1,0:T(8,128)(2,1)S(1)}, u32[]{:S(2)}, u32[]{:S(2)}) %collective-permute-start.5) | collective-permute-done | bytes 122912 | tf_op jit(solution)/shard_map/ppermute | solution.py:54
  24.7 4.8 %columns.1 = (bf16[160,384]{1,0:T(8,128)(2,1)}, bf16[160,384]{1,0:T(8,128)(2,1)}, bf16[26,24,384]{2,1,0:T(8,128)(2,1)}, bf16[52,48,384]{2,1,0:T(8,128)(2,1)}, bf...) custom-call(s32[3]{0:T(128)} %pad_add_fusion.place_ref.refs_0_, ...), custom_call_target="tpu_custom_call" | custom-call | bytes 5526636 | tf_op jit(solution)/shard_map/columns/pallas_call | solution.py:532
  29.5 1.7 %collective-permute-start.6 = (bf16[160,384]{1,0:T(8,128)(2,1)}, bf16[160,384]{1,0:T(8,128)(2,1)S(1)}, u32[]{:S(2)}, u32[]{:S(2)}) collective-permute-start(bf16[160,384]{1,0:T(8,128)(2,1)} %get-tuple-element.64), channel_id=1, source_target_pairs={{0,16},{16,0},{1,17},{17,1},{2,18},{18,2},{3,19},{19,3},{4,20},{20... | collective-permute-start | bytes 368648 | tf_op jit(solution)/shard_map/ppermute | solution.py:612
  31.2 1.2 collective-permute-done.6
  32.3 1.0 maximum_select_fusion.refs_2_
  33.4 3.0 %collective-permute-start.9 = (bf16[2,160,384]{2,1,0:T(8,128)(2,1)S(1)}, bf16[2,160,384]{2,1,0:T(8,128)(2,1)S(1)}, u32[]{:S(2)}, u32[]{:S(2)}) collective-permute-start(bf16[2,160,384]{2,1,0:T(8,128)(2,1)S(1)} %maximum_select_fusion.refs_2_), channel_id=1, source_target_pairs={{0,96},{32,0},{64,32},{96,64},{1,97},{33,1},{65,33},{97,65},{2,98}... | collective-permute-start | bytes 737288 | tf_op jit(solution)/shard_map/ppermute | solution.py:614
  38.6 4.7 %collective-permute-start.10 = (bf16[8,24,384]{2,1,0:T(8,128)(2,1)}, bf16[8,24,384]{2,1,0:T(8,128)(2,1)S(1)}, u32[]{:S(2)}, u32[]{:S(2)}) collective-permute-start(bf16[8,24,384]{2,1,0:T(8,128)(2,1)} %get-tuple-element.65), channel_id=1, source_target_pairs={{0,16},{16,32},{32,48},{48,64},{64,80},{80,96},{96,112},{1,17},{17... | collective-permute-start | bytes 442376 | tf_op jit(solution)/shard_map/ppermute | solution.py:54
  43.3 1.9 %collective-permute-start.11 = (bf16[8,24,384]{2,1,0:T(8,128)(2,1)}, bf16[8,24,384]{2,1,0:T(8,128)(2,1)S(1)}, u32[]{:S(2)}, u32[]{:S(2)}) collective-permute-start(bf16[8,24,384]{2,1,0:T(8,128)(2,1)} %get-tuple-element.66), channel_id=1, source_target_pairs={{16,0},{32,16},{48,32},{64,48},{80,64},{96,80},{112,96},{17,1},{33... | collective-permute-start | bytes 442376 | tf_op jit(solution)/shard_map/ppermute | solution.py:54
  45.2 4.1 %collective-permute-done.10.from_up_ref = bf16[8,24,384]{2,1,0:T(8,128)(2,1)S(1)} collective-permute-done((bf16[8,24,384]{2,1,0:T(8,128)(2,1)}, bf16[8,24,384]{2,1,0:T(8,128)(2,1)S(1)}, u32[]{:S(2)}, u32[]{:S(2)}) %collective-permute-start.10) | collective-permute-done | bytes 147488 | tf_op jit(solution)/shard_map/ppermute | solution.py:54
  49.3 1.1 collective-permute-done.11.from_down_ref
  50.9 3.9 %queries.1 = (bf16[1056,384]{1,0:T(8,128)(2,1)}, bf16[208,384]{1,0:T(8,128)(2,1)}, bf16[208,384]{1,0:T(8,128)(2,1)}) custom-call(s32[3]{0:T(128)} %pad_add_fusion.place_ref.refs_0_, s32[8]{0:T(128)} %row_ref.11, bf16[2,160,384]{2,1,0:T(8,128)(2,1)S(1)} %maximum_select_fusion.refs_2_, bf16[2,160,384]{2,1,0:T(8,128)(2,1)S(1)} %collective-permute-done.7.refs_3_, ...), custom_call_target="tpu_custom_call" | custom-call | flops 622854144 | bytes 2704940 | tf_op jit(solution)/shard_map/queries/pallas_call | solution.py:532
  54.8 7.4 %prior_coarse.1 = (f32[360,384]{1,0:T(8,128)}, bf16[4,4,192,384]{3,2,1,0:T(8,128)(2,1)}) custom-call(s32[3]{0:T(128)} %pad_add_fusion.place_ref.refs_0_, s32[8]{0:T(128)} %row_ref.11, bf16[26,24,384]{2,1,0:T(8,128)(2,1)} %get-tuple-element.76.prior_ref, bf16[8,24,384]{2,1,0:T(8,128)(2,1)S(1)} %collective-permute-done.10.from_up_ref, ...), custom_call_target="tpu_custom_call" | custom-call | flops 1911029760 | bytes 15704108 | tf_op jit(solution)/shard_map/prior_coarse/pallas_call | solution.py:532
  62.2 1.1 all-gather.3.cloned.1.call-done
  63.3 24.3 %attention.1 = bf16[8,208,384]{2,1,0:T(8,128)(2,1)} custom-call(s32[3]{0:T(128)} %pad_add_fusion.place_ref.refs_0_, s32[8]{0:T(128)} %row_ref.11, s32[16]{0:T(128)} %col_ref.9, bf16[1056,384]{1,0:T(8,128)(2,1)} %get-tuple-element.83.query_ref, bf16[32,272,384]{2,1,0:T(8,128)(2,1)} %bitcast.11), custom_call_target="tpu_custom_call" | custom-call | flops 13287555072 | bytes 8773740 | tf_op jit(solution)/shard_map/attention/pallas_call | solution.py:532
  87.6 4.4 %all-to-all-start = ((bf16[8,208,384]{2,1,0:T(8,128)(2,1)}), bf16[8,208,384]{2,1,0:T(8,128)(2,1)S(1)}, u32[]{:S(2)}, u32[]{:S(2)}) async-start(bf16[8,208,384]{2,1,0:T(8,128)(2,1)} %attention.1), calls=%async_computation | async-start | bytes 2555904 | tf_op jit(solution)/shard_map/all_to_all | solution.py:646
  92.1 9.1 %prior_fine.1.sum_two_ref = f32[1248,192]{1,0:T(8,128)} custom-call(s32[3]{0:T(128)} %pad_add_fusion.place_ref.refs_0_, s32[8]{0:T(128)} %row_ref.11, bf16[52,48,384]{2,1,0:T(8,128)(2,1)} %get-tuple-element.87.fine_ref, bf16[8,24,384]{2,1,0:T(8,128)(2,1)S(1)} %collective-permute-done.10.from_up_ref, ...), custom_call_target="tpu_custom_call" | custom-call | flops 3312451584 | bytes 7151660 | tf_op jit(solution)/shard_map/prior_fine/pallas_call | solution.py:532
  101.3 8.3 %all-to-all-done.part_ref = bf16[8,208,384]{2,1,0:T(8,128)(2,1)S(1)} async-done(((bf16[8,208,384]{2,1,0:T(8,128)(2,1)}), bf16[8,208,384]{2,1,0:T(8,128)(2,1)S(1)}, u32[]{:S(2)}, u32[]{:S(2)}) %all-to-all-start) | async-done | bytes 1277984 | tf_op jit(solution)/shard_map/all_to_all | solution.py:646
  109.6 1.3 %copy-done = f32[1248,192]{1,0:T(8,128)S(1)} copy-done((f32[1248,192]{1,0:T(8,128)S(1)}, f32[1248,192]{1,0:T(8,128)}, u32[]{:S(2)}) %copy-start) | copy-done | bytes 958488
  110.9 8.6 %finish.1 = bf16[26,40,192]{2,1,0:T(8,128)(2,1)} custom-call(s32[3]{0:T(128)} %pad_add_fusion.place_ref.refs_0_, s32[8]{0:T(128)} %row_ref.11, s32[16]{0:T(128)} %col_ref.9, bf16[8,208,384]{2,1,0:T(8,128)(2,1)S(1)} %all-to-all-done.part_ref, bf16[208,384]{1,0:T(8,128)(2,1)} %get-tuple-element.84.mine_ref, ...), custom_call_target="tpu_custom_call" | custom-call | bytes 14423148 | tf_op jit(solution)/shard_map/finish/pallas_call | solution.py:532
  (22 shorter events, 3.5 us)
Async XLA Ops:
  6.5 13.1 %copy-start.2 = (s32[16]{0:T(128)S(1)}, s32[16]{0:T(128)}, u32[]{:S(2)}) copy-start(s32[16]{0:T(128)} %col_ref.9) | copy-start | bytes 196
  6.5 56.7 %all-gather.3.cloned.1.call-start = ((), (), s32[]{:S(2)}) async-start(), calls=%async_computation.1 | async-start | bytes 6893568 | tf_op jit(solution)/shard_map/all_gather | solution.py:586
  13.8 23.5 %copy-start.1 = (s32[8]{0:T(128)S(1)}, s32[8]{0:T(128)}, u32[]{:S(2)}) copy-start(s32[8]{0:T(128)} %row_ref.11) | copy-start | bytes 100
  13.8 7.1 %collective-permute-start.4 = (bf16[160,384]{1,0:T(8,128)(2,1)}, bf16[160,384]{1,0:T(8,128)(2,1)S(1)}, u32[]{:S(2)}, u32[]{:S(2)}) collective-permute-start(bf16[160,384]{1,0:T(8,128)(2,1)} %get-tuple-element.57), channel_id=1, source_target_pairs={{0,1},{1,2},{2,3},{3,4},{4,5},{5,6},{6,7},{7,8},{8,9},{9,10},{10,1... | collective-permute-start | bytes 368648 | tf_op jit(solution)/shard_map/ppermute | solution.py:54
  18.3 6.4 %collective-permute-start.5 = (bf16[160,384]{1,0:T(8,128)(2,1)}, bf16[160,384]{1,0:T(8,128)(2,1)S(1)}, u32[]{:S(2)}, u32[]{:S(2)}) collective-permute-start(bf16[160,384]{1,0:T(8,128)(2,1)} %get-tuple-element.58), channel_id=1, source_target_pairs={{1,0},{2,1},{3,2},{4,3},{5,4},{6,5},{7,6},{8,7},{9,8},{10,9},{11,1... | collective-permute-start | bytes 368648 | tf_op jit(solution)/shard_map/ppermute | solution.py:54
  29.5 2.8 %collective-permute-start.6 = (bf16[160,384]{1,0:T(8,128)(2,1)}, bf16[160,384]{1,0:T(8,128)(2,1)S(1)}, u32[]{:S(2)}, u32[]{:S(2)}) collective-permute-start(bf16[160,384]{1,0:T(8,128)(2,1)} %get-tuple-element.64), channel_id=1, source_target_pairs={{0,16},{16,0},{1,17},{17,1},{2,18},{18,2},{3,19},{19,3},{4,20},{20... | collective-permute-start | bytes 368648 | tf_op jit(solution)/shard_map/ppermute | solution.py:612
  33.4 17.0 %collective-permute-start.9 = (bf16[2,160,384]{2,1,0:T(8,128)(2,1)S(1)}, bf16[2,160,384]{2,1,0:T(8,128)(2,1)S(1)}, u32[]{:S(2)}, u32[]{:S(2)}) collective-permute-start(bf16[2,160,384]{2,1,0:T(8,128)(2,1)S(1)} %maximum_select_fusion.refs_2_), channel_id=1, source_target_pairs={{0,96},{32,0},{64,32},{96,64},{1,97},{33,1},{65,33},{97,65},{2,98}... | collective-permute-start | bytes 737288 | tf_op jit(solution)/shard_map/ppermute | solution.py:614
  36.3 14.0 %collective-permute-start.8 = (bf16[2,160,384]{2,1,0:T(8,128)(2,1)S(1)}, bf16[2,160,384]{2,1,0:T(8,128)(2,1)S(1)}, u32[]{:S(2)}, u32[]{:S(2)}) collective-permute-start(bf16[2,160,384]{2,1,0:T(8,128)(2,1)S(1)} %maximum_select_fusion.refs_2_), channel_id=1, source_target_pairs={{0,64},{32,96},{64,0},{96,32},{1,65},{33,97},{65,1},{97,33},{2,66}... | collective-permute-start | bytes 737288 | tf_op jit(solution)/shard_map/ppermute | solution.py:614
  36.5 14.4 %collective-permute-start.7 = (bf16[2,160,384]{2,1,0:T(8,128)(2,1)S(1)}, bf16[2,160,384]{2,1,0:T(8,128)(2,1)S(1)}, u32[]{:S(2)}, u32[]{:S(2)}) collective-permute-start(bf16[2,160,384]{2,1,0:T(8,128)(2,1)S(1)} %maximum_select_fusion.refs_2_), channel_id=1, source_target_pairs={{0,32},{32,64},{64,96},{96,0},{1,33},{33,65},{65,97},{97,1},{2,34}... | collective-permute-start | bytes 737288 | tf_op jit(solution)/shard_map/ppermute | solution.py:614
  38.6 10.7 %collective-permute-start.10 = (bf16[8,24,384]{2,1,0:T(8,128)(2,1)}, bf16[8,24,384]{2,1,0:T(8,128)(2,1)S(1)}, u32[]{:S(2)}, u32[]{:S(2)}) collective-permute-start(bf16[8,24,384]{2,1,0:T(8,128)(2,1)} %get-tuple-element.65), channel_id=1, source_target_pairs={{0,16},{16,32},{32,48},{48,64},{64,80},{80,96},{96,112},{1,17},{17... | collective-permute-start | bytes 442376 | tf_op jit(solution)/shard_map/ppermute | solution.py:54
  43.3 7.1 %collective-permute-start.11 = (bf16[8,24,384]{2,1,0:T(8,128)(2,1)}, bf16[8,24,384]{2,1,0:T(8,128)(2,1)S(1)}, u32[]{:S(2)}, u32[]{:S(2)}) collective-permute-start(bf16[8,24,384]{2,1,0:T(8,128)(2,1)} %get-tuple-element.66), channel_id=1, source_target_pairs={{16,0},{32,16},{48,32},{64,48},{80,64},{96,80},{112,96},{17,1},{33... | collective-permute-start | bytes 442376 | tf_op jit(solution)/shard_map/ppermute | solution.py:54
  87.6 4.4 %copy-start.3 = (bf16[208,384]{1,0:T(8,128)(2,1)S(1)}, bf16[208,384]{1,0:T(8,128)(2,1)}, u32[]{:S(2)}) copy-start(bf16[208,384]{1,0:T(8,128)(2,1)} %get-tuple-element.85) | copy-start | bytes 479236
  87.6 22.0 %all-to-all-start = ((bf16[8,208,384]{2,1,0:T(8,128)(2,1)}), bf16[8,208,384]{2,1,0:T(8,128)(2,1)S(1)}, u32[]{:S(2)}, u32[]{:S(2)}) async-start(bf16[8,208,384]{2,1,0:T(8,128)(2,1)} %attention.1), calls=%async_computation | async-start | bytes 2555904 | tf_op jit(solution)/shard_map/all_to_all | solution.py:646
  92.0 9.2 %collective-permute-start.12 = (bf16[208,384]{1,0:T(8,128)(2,1)S(1)}, bf16[208,384]{1,0:T(8,128)(2,1)S(1)}, u32[]{:S(2)}, u32[]{:S(2)}) collective-permute-start(bf16[208,384]{1,0:T(8,128)(2,1)S(1)} %copy-done.3), channel_id=1, source_target_pairs={{0,16},{16,0},{1,17},{17,1},{2,18},{18,2},{3,19},{19,3},{4,20},{20... | collective-permute-start | bytes 479240 | tf_op jit(solution)/shard_map/ppermute | solution.py:630
  109.6 1.3 %copy-start = (f32[1248,192]{1,0:T(8,128)S(1)}, f32[1248,192]{1,0:T(8,128)}, u32[]{:S(2)}) copy-start(f32[1248,192]{1,0:T(8,128)} %prior_fine.1.sum_two_ref) | copy-start | bytes 2875396
Sparse Core Ops, SparseCore 0:
  9.7 53.5 all-gather.2
